TPU v7x, 768 devices: a whole 4x8x12 slice. The times are simulated.
768 devices in a mesh: ctx: 48 (over x, z_lo, core), tp: 16 (over z_hi, y).
Axes of the slice: x: 4, y: 8, z: 12 (z_hi: 2, z_lo: 6; z = z_hi * 6 + z_lo), core: 2. Of those that a mesh axis runs over, the one named last changes fastest.
Arguments:
- queries: bfloat16 [6144, 6144], P('ctx', 'tp'), may hold values from -80 to 80
- key_rows: bfloat16 [6144, 1024], P('ctx'), may hold values from -4 to 4
- value_rows: bfloat16 [6144, 1024], P('ctx'), may hold values from -6 to 6
- out_grad: bfloat16 [6144, 6144], P('ctx', 'tp'), may hold values from -6 to 6
- attn_out: bfloat16 [6144, 6144], P('ctx', 'tp'), may hold values from -6 to 6
- doc_ids: int32 [6144], replicated, may hold values from 0 to 7, never falling along the last dimension, each value on 1 to 3200 neighbouring positions
- row_grad: bfloat16 [6144, 6144], P('ctx', 'tp'), may hold values from -6 to 6
- gate_weights: float32 [6144, 2], P('ctx'), may hold values from 0.1 to 0.9
- expert_ids: int32 [6144, 2], P('ctx'), may hold values from 0 to 7, all different within a row; in each aligned block of 128 rows (0 to 127, 128 to 255, ...) at most 64 rows name the same one
- expert_out: bfloat16 [48, 512, 6144], P('ctx', 'tp'), may hold values from -0.079589844 to 0.079589844
Outputs:
- query_grad: bfloat16 [6144, 6144], P('ctx', 'tp')
- key_grad: bfloat16 [6144, 1024], P('ctx', 'tp')
- value_grad: bfloat16 [6144, 1024], P('ctx', 'tp')
- gate_grad: float32 [48, 512], P('ctx', 'tp')
- expert_grad: bfloat16 [48, 512, 6144], P('ctx', 'tp')
Inputs may be any that keep to these rules, and one draw needn't show every extreme that they name: `doc_ids`: never falling along the tokens; each document holds 1 to 3200 tokens and one holds exactly 3200. `expert_ids`: A token's 2 experts differ; within each aligned block of 128 tokens no expert is named by more than 64 entries, and in some block an expert is named by exactly 64.
All inputs are finite; a program needn't handle non-finite values.
Results may differ from a plain program's by a relative error of at most 0.006.
Values may be sent and summed in bfloat16 or wider, within the bound.
No kernel may reach another device: no remote copies, remote signals or barrier semaphores. Data moves between devices by JAX's collectives and lax.ppermute only.
A program may use at most 32 MiB of HBM per device.

v0:
```python
import math

import jax
import jax.numpy as jnp
from jax import lax
from jax.sharding import PartitionSpec as P

HD = 128
QH_DEV = 3
TOP = 2


def shifted(x, axis, by):
    size = lax.axis_size(axis)
    pairs = [(i, i + by) for i in range(size) if 0 <= i + by < size]
    return lax.ppermute(x, axis, pairs)


def from_partner(value, axis, distance):
    mask = 2**distance
    pairs = [(source, source ^ mask) for source in range(lax.axis_size(axis))]
    return lax.ppermute(value, axis, pairs)


def slot_table(routes_block, experts_total, capacity):
    flat_ids = routes_block.reshape(-1)
    onehot = (flat_ids[:, None] == jnp.arange(experts_total, dtype=jnp.int32)[None, :]).astype(
        jnp.int32
    )
    earlier = jnp.cumsum(onehot, axis=0) - onehot
    ranking = jnp.sum(earlier * onehot, axis=1)
    return (2 * flat_ids + ranking // capacity) * capacity + ranking % capacity


def split_halves(terms, half_index):
    quarter = HD // 2
    other_index = 1 - half_index
    keep_part = jnp.concatenate(
        [
            lax.dynamic_slice_in_dim(terms, half_index * quarter, quarter, 1),
            lax.dynamic_slice_in_dim(terms, HD + half_index * quarter, quarter, 1),
        ],
        axis=1,
    )
    send_part = jnp.concatenate(
        [
            lax.dynamic_slice_in_dim(terms, other_index * quarter, quarter, 1),
            lax.dynamic_slice_in_dim(terms, HD + other_index * quarter, quarter, 1),
        ],
        axis=1,
    )
    return (keep_part, send_part)


def local(
    queries,
    key_rows,
    value_rows,
    out_grad,
    attn_out,
    doc_ids,
    row_grad,
    gate_weights,
    expert_ids,
    expert_out,
):
    tensor_index = lax.axis_index("tp")
    context_index = lax.axis_index("ctx")
    local_rows = queries.shape[0]
    scaling = 1.0 / math.sqrt(HD)
    group_index = tensor_index // 2
    own_keys = lax.dynamic_slice_in_dim(key_rows, group_index * HD, HD, 1)
    own_values = lax.dynamic_slice_in_dim(value_rows, group_index * HD, HD, 1)
    all_keys, all_values = (
        lax.all_gather(own_keys, "ctx", axis=0, tiled=True),
        lax.all_gather(own_values, "ctx", axis=0, tiled=True),
    )
    total_rows = all_keys.shape[0]
    longest = total_rows // 2 + local_rows
    window = longest + local_rows
    window_start = jnp.maximum((context_index + 1) * local_rows - window, 0)
    window_keys = lax.dynamic_slice_in_dim(all_keys, window_start, window, 0)
    window_values = lax.dynamic_slice_in_dim(all_values, window_start, window, 0)
    window_docs = lax.dynamic_slice_in_dim(doc_ids, window_start, window, 0)
    query_pos = context_index * local_rows + jnp.arange(local_rows, dtype=jnp.int32)
    key_pos = window_start + jnp.arange(window, dtype=jnp.int32)
    query_docs = lax.dynamic_slice_in_dim(doc_ids, context_index * local_rows, local_rows, 0)
    allowed = (query_docs[:, None] == window_docs[None, :]) & (
        key_pos[None, :] <= query_pos[:, None]
    )
    query_parts = []
    score_list = []
    prob_list = []
    query_list = []
    grad_list = []
    for head_slot in range(QH_DEV):
        query_head = queries[:, head_slot * HD : (head_slot + 1) * HD]
        grad_head = out_grad[:, head_slot * HD : (head_slot + 1) * HD]
        output_head = attn_out[:, head_slot * HD : (head_slot + 1) * HD]
        scores = jnp.dot(query_head, window_keys.T, preferred_element_type=jnp.float32) * scaling
        scores = jnp.where(allowed, scores, -1e30)
        row_max = jnp.max(scores, axis=1, keepdims=True)
        totals = jnp.sum(jnp.where(allowed, jnp.exp(scores - row_max), 0.0), axis=1, keepdims=True)
        log_total = row_max + jnp.log(totals)
        probs = jnp.where(allowed, jnp.exp(scores - log_total), 0.0)
        row_delta = jnp.sum(
            grad_head.astype(jnp.float32) * output_head.astype(jnp.float32), axis=1, keepdims=True
        )
        prob_grad = jnp.dot(grad_head, window_values.T, preferred_element_type=jnp.float32)
        score_grad = (probs * (prob_grad - row_delta)).astype(jnp.bfloat16)
        query_parts.append(
            (jnp.dot(score_grad, window_keys, preferred_element_type=jnp.float32) * scaling).astype(
                jnp.bfloat16
            )
        )
        score_list.append(score_grad)
        prob_list.append(probs.astype(jnp.bfloat16))
        query_list.append(query_head)
        grad_list.append(grad_head)
    query_grad = jnp.concatenate(query_parts, axis=1)
    stacked_scores = jnp.stack(score_list)
    stacked_probs = jnp.stack(prob_list)
    stacked_queries = jnp.stack(query_list)
    stacked_grads = jnp.stack(grad_list)

    def window_terms(start, count):
        score_block = lax.dynamic_slice_in_dim(stacked_scores, start, count, 2)
        prob_block = lax.dynamic_slice_in_dim(stacked_probs, start, count, 2)
        key_part = (
            jnp.einsum(
                "hqk,hqd->kd", score_block, stacked_queries, preferred_element_type=jnp.float32
            )
            * scaling
        )
        value_part = jnp.einsum(
            "hqk,hqd->kd", prob_block, stacked_grads, preferred_element_type=jnp.float32
        )
        return jnp.concatenate([key_part, value_part], axis=1)

    half_index = tensor_index % 2
    reach = longest // local_rows

    def window_term(offset):
        target = context_index - offset
        local_start = jnp.clip(target * local_rows - window_start, 0, window - local_rows)
        valid = (target >= 0).astype(jnp.float32)
        return window_terms(local_start, local_rows) * valid

    def window_step(step_index, running):
        running = shifted(running, "ctx", -1)
        return running + window_term(reach - step_index)

    summed = lax.fori_loop(1, reach + 1, window_step, window_term(reach))
    keep_part, send_part = split_halves(summed, half_index)
    partner = from_partner(send_part, "tp", 0)
    combined = keep_part + partner
    key_grad = combined[:, : HD // 2].astype(jnp.bfloat16)
    value_grad = combined[:, HD // 2 :].astype(jnp.bfloat16)
    group_slots = expert_out.shape[1]
    tensor_count = lax.axis_size("tp")
    slot_count = tensor_count * group_slots
    positions = slot_table(expert_ids, tensor_count // 2, group_slots)
    chosen = (jnp.arange(slot_count, dtype=jnp.int32)[:, None] == positions[None, :]).astype(
        jnp.int32
    )
    by_token = jnp.sum(chosen.reshape(slot_count, local_rows, TOP), axis=2)
    buffer = jnp.dot(
        by_token.astype(jnp.bfloat16), row_grad, preferred_element_type=jnp.float32
    ).astype(jnp.bfloat16)
    buffer = buffer.reshape(tensor_count, group_slots, row_grad.shape[1])
    arrived = lax.all_to_all(buffer, "tp", split_axis=0, concat_axis=2, tiled=True)[0]
    my_entries = lax.dynamic_slice_in_dim(chosen, tensor_index * group_slots, group_slots, 0)
    slot_gates = jnp.sum(jnp.where(my_entries > 0, gate_weights.reshape(-1)[None, :], 0.0), axis=1)
    arrived_wide = arrived.astype(jnp.float32)
    gate_grad = jnp.sum(arrived_wide * expert_out[0].astype(jnp.float32), axis=1)[None, :]
    expert_grad = (slot_gates[:, None] * arrived_wide).astype(jnp.bfloat16)[None]
    return (query_grad, key_grad, value_grad, gate_grad, expert_grad)


def solution(mesh):
    in_specs = (
        P("ctx", "tp"),
        P("ctx", None),
        P("ctx", None),
        P("ctx", "tp"),
        P("ctx", "tp"),
        P(),
        P("ctx", "tp"),
        P("ctx", None),
        P("ctx", None),
        P("ctx", "tp", None),
    )
    out_specs = (
        P("ctx", "tp"),
        P("ctx", "tp"),
        P("ctx", "tp"),
        P("ctx", "tp"),
        P("ctx", "tp", None),
    )
    return jax.shard_map(local, mesh=mesh, in_specs=in_specs, out_specs=out_specs, check_vma=False)
```

profile of v0, /device:TPU:4, one launch (start us, length us, event | category | flops | bytes accessed | tf_op | source)
XLA Modules:
  0.0 540.6 jit_solution(12359434354432267020)
XLA Ops:
  13.7 20.0 %all-to-all-start = ((bf16[16,32,384]{2,1,0:T(8,128)(2,1)}), bf16[16,32,384]{2,1,0:T(8,128)(2,1)S(1)}, u32[]{:S(2)}, u32[]{:S(2)}) async-start(bf16[16,32,384]{2,1,0:T(8,128)(2,1)} %bitcast.24), calls=%async_computation | async-start | bytes 786432 | tf_op jit(solution)/shard_map/all_to_all | solution.py:171
  39.6 10.8 %all-to-all-done = bf16[16,32,384]{2,1,0:T(8,128)(2,1)S(1)} async-done(((bf16[16,32,384]{2,1,0:T(8,128)(2,1)}), bf16[16,32,384]{2,1,0:T(8,128)(2,1)S(1)}, u32[]{:S(2)}, u32[]{:S(2)}) %all-to-all-start) | async-done | bytes 393248 | tf_op jit(solution)/shard_map/all_to_all | solution.py:171
  52.2 65.9 %all-gather.3.cloned.1.call-done = bf16[6144,128]{1,0:T(8,128)(2,1)} async-done(((bf16[128,128]{1,0:T(8,128)(2,1)}), bf16[6144,128]{1,0:T(8,128)(2,1)}) %all-gather.3.cloned.1.call-update) | async-done | bytes 1572880 | tf_op jit(solution)/shard_map/all_gather | solution.py:75
  131.2 86.5 %all-gather.5.cloned.1.call-done = bf16[6144,128]{1,0:T(8,128)(2,1)} async-done(((bf16[128,128]{1,0:T(8,128)(2,1)}), bf16[6144,128]{1,0:T(8,128)(2,1)}) %all-gather.5.cloned.1.call-update) | async-done | bytes 1572880 | tf_op jit(solution)/shard_map/all_gather | solution.py:76
  217.7 4.1 fusion.18
  228.8 297.9 %while.13 = (s32[]{:T(128)}, f32[128,256]{0,1:T(8,128)S(1)}, s32[]{:T(128)}, s32[]{:T(128)}, bf16[3,128,3328]{1,2,0:T(8,128)(2,1)}, /*index=5*/bf16[3,128,128]{1...) while((s32[]{:T(128)}, f32[128,256]{0,1:T(8,128)S(1)}, ...), condition=%wide.region_10.11_spmd, body=%wide.region_9.10_spmd.sunk | while | flops 25280520 | bytes 1442055 | solution.py:153
  228.8 6.9 %collective-permute-start = (f32[128,256]{0,1:T(8,128)S(1)}, f32[128,256]{0,1:T(8,128)S(1)}, u32[]{:S(2)}, u32[]{:S(2)}) collective-permute-start(f32[128,256]{0,1:T(8,128)S(1)} %get-tuple-element.307), channel_id=1, source_target_pairs={{16,0},{32,16},{48,32},{64,48},{80,64},{96,80},{112,96},{128,112},... | collective-permute-start | bytes 393224 | tf_op jit(solution)/shard_map/while/body/eval_jaxpr/ppermute | solution.py:16
  238.2 9.5 %collective-permute-start = (f32[128,256]{0,1:T(8,128)S(1)}, f32[128,256]{0,1:T(8,128)S(1)}, u32[]{:S(2)}, u32[]{:S(2)}) collective-permute-start(f32[128,256]{0,1:T(8,128)S(1)} %get-tuple-element.307), channel_id=1, source_target_pairs={{16,0},{32,16},{48,32},{64,48},{80,64},{96,80},{112,96},{128,112},... | collective-permute-start | bytes 393224 | tf_op jit(solution)/shard_map/while/body/eval_jaxpr/ppermute | solution.py:16
  250.2 9.5 %collective-permute-start = (f32[128,256]{0,1:T(8,128)S(1)}, f32[128,256]{0,1:T(8,128)S(1)}, u32[]{:S(2)}, u32[]{:S(2)}) collective-permute-start(f32[128,256]{0,1:T(8,128)S(1)} %get-tuple-element.307), channel_id=1, source_target_pairs={{16,0},{32,16},{48,32},{64,48},{80,64},{96,80},{112,96},{128,112},... | collective-permute-start | bytes 393224 | tf_op jit(solution)/shard_map/while/body/eval_jaxpr/ppermute | solution.py:16
  262.3 9.5 %collective-permute-start = (f32[128,256]{0,1:T(8,128)S(1)}, f32[128,256]{0,1:T(8,128)S(1)}, u32[]{:S(2)}, u32[]{:S(2)}) collective-permute-start(f32[128,256]{0,1:T(8,128)S(1)} %get-tuple-element.307), channel_id=1, source_target_pairs={{16,0},{32,16},{48,32},{64,48},{80,64},{96,80},{112,96},{128,112},... | collective-permute-start | bytes 393224 | tf_op jit(solution)/shard_map/while/body/eval_jaxpr/ppermute | solution.py:16
  274.3 9.5 %collective-permute-start = (f32[128,256]{0,1:T(8,128)S(1)}, f32[128,256]{0,1:T(8,128)S(1)}, u32[]{:S(2)}, u32[]{:S(2)}) collective-permute-start(f32[128,256]{0,1:T(8,128)S(1)} %get-tuple-element.307), channel_id=1, source_target_pairs={{16,0},{32,16},{48,32},{64,48},{80,64},{96,80},{112,96},{128,112},... | collective-permute-start | bytes 393224 | tf_op jit(solution)/shard_map/while/body/eval_jaxpr/ppermute | solution.py:16
  286.3 9.5 %collective-permute-start = (f32[128,256]{0,1:T(8,128)S(1)}, f32[128,256]{0,1:T(8,128)S(1)}, u32[]{:S(2)}, u32[]{:S(2)}) collective-permute-start(f32[128,256]{0,1:T(8,128)S(1)} %get-tuple-element.307), channel_id=1, source_target_pairs={{16,0},{32,16},{48,32},{64,48},{80,64},{96,80},{112,96},{128,112},... | collective-permute-start | bytes 393224 | tf_op jit(solution)/shard_map/while/body/eval_jaxpr/ppermute | solution.py:16
  298.3 9.5 %collective-permute-start = (f32[128,256]{0,1:T(8,128)S(1)}, f32[128,256]{0,1:T(8,128)S(1)}, u32[]{:S(2)}, u32[]{:S(2)}) collective-permute-start(f32[128,256]{0,1:T(8,128)S(1)} %get-tuple-element.307), channel_id=1, source_target_pairs={{16,0},{32,16},{48,32},{64,48},{80,64},{96,80},{112,96},{128,112},... | collective-permute-start | bytes 393224 | tf_op jit(solution)/shard_map/while/body/eval_jaxpr/ppermute | solution.py:16
  310.4 9.5 %collective-permute-start = (f32[128,256]{0,1:T(8,128)S(1)}, f32[128,256]{0,1:T(8,128)S(1)}, u32[]{:S(2)}, u32[]{:S(2)}) collective-permute-start(f32[128,256]{0,1:T(8,128)S(1)} %get-tuple-element.307), channel_id=1, source_target_pairs={{16,0},{32,16},{48,32},{64,48},{80,64},{96,80},{112,96},{128,112},... | collective-permute-start | bytes 393224 | tf_op jit(solution)/shard_map/while/body/eval_jaxpr/ppermute | solution.py:16
  322.4 9.5 %collective-permute-start = (f32[128,256]{0,1:T(8,128)S(1)}, f32[128,256]{0,1:T(8,128)S(1)}, u32[]{:S(2)}, u32[]{:S(2)}) collective-permute-start(f32[128,256]{0,1:T(8,128)S(1)} %get-tuple-element.307), channel_id=1, source_target_pairs={{16,0},{32,16},{48,32},{64,48},{80,64},{96,80},{112,96},{128,112},... | collective-permute-start | bytes 393224 | tf_op jit(solution)/shard_map/while/body/eval_jaxpr/ppermute | solution.py:16
  334.4 9.5 %collective-permute-start = (f32[128,256]{0,1:T(8,128)S(1)}, f32[128,256]{0,1:T(8,128)S(1)}, u32[]{:S(2)}, u32[]{:S(2)}) collective-permute-start(f32[128,256]{0,1:T(8,128)S(1)} %get-tuple-element.307), channel_id=1, source_target_pairs={{16,0},{32,16},{48,32},{64,48},{80,64},{96,80},{112,96},{128,112},... | collective-permute-start | bytes 393224 | tf_op jit(solution)/shard_map/while/body/eval_jaxpr/ppermute | solution.py:16
  346.4 9.5 %collective-permute-start = (f32[128,256]{0,1:T(8,128)S(1)}, f32[128,256]{0,1:T(8,128)S(1)}, u32[]{:S(2)}, u32[]{:S(2)}) collective-permute-start(f32[128,256]{0,1:T(8,128)S(1)} %get-tuple-element.307), channel_id=1, source_target_pairs={{16,0},{32,16},{48,32},{64,48},{80,64},{96,80},{112,96},{128,112},... | collective-permute-start | bytes 393224 | tf_op jit(solution)/shard_map/while/body/eval_jaxpr/ppermute | solution.py:16
  358.4 9.5 %collective-permute-start = (f32[128,256]{0,1:T(8,128)S(1)}, f32[128,256]{0,1:T(8,128)S(1)}, u32[]{:S(2)}, u32[]{:S(2)}) collective-permute-start(f32[128,256]{0,1:T(8,128)S(1)} %get-tuple-element.307), channel_id=1, source_target_pairs={{16,0},{32,16},{48,32},{64,48},{80,64},{96,80},{112,96},{128,112},... | collective-permute-start | bytes 393224 | tf_op jit(solution)/shard_map/while/body/eval_jaxpr/ppermute | solution.py:16
  370.5 9.5 %collective-permute-start = (f32[128,256]{0,1:T(8,128)S(1)}, f32[128,256]{0,1:T(8,128)S(1)}, u32[]{:S(2)}, u32[]{:S(2)}) collective-permute-start(f32[128,256]{0,1:T(8,128)S(1)} %get-tuple-element.307), channel_id=1, source_target_pairs={{16,0},{32,16},{48,32},{64,48},{80,64},{96,80},{112,96},{128,112},... | collective-permute-start | bytes 393224 | tf_op jit(solution)/shard_map/while/body/eval_jaxpr/ppermute | solution.py:16
  382.5 9.5 %collective-permute-start = (f32[128,256]{0,1:T(8,128)S(1)}, f32[128,256]{0,1:T(8,128)S(1)}, u32[]{:S(2)}, u32[]{:S(2)}) collective-permute-start(f32[128,256]{0,1:T(8,128)S(1)} %get-tuple-element.307), channel_id=1, source_target_pairs={{16,0},{32,16},{48,32},{64,48},{80,64},{96,80},{112,96},{128,112},... | collective-permute-start | bytes 393224 | tf_op jit(solution)/shard_map/while/body/eval_jaxpr/ppermute | solution.py:16
  394.5 9.5 %collective-permute-start = (f32[128,256]{0,1:T(8,128)S(1)}, f32[128,256]{0,1:T(8,128)S(1)}, u32[]{:S(2)}, u32[]{:S(2)}) collective-permute-start(f32[128,256]{0,1:T(8,128)S(1)} %get-tuple-element.307), channel_id=1, source_target_pairs={{16,0},{32,16},{48,32},{64,48},{80,64},{96,80},{112,96},{128,112},... | collective-permute-start | bytes 393224 | tf_op jit(solution)/shard_map/while/body/eval_jaxpr/ppermute | solution.py:16
  406.5 9.5 %collective-permute-start = (f32[128,256]{0,1:T(8,128)S(1)}, f32[128,256]{0,1:T(8,128)S(1)}, u32[]{:S(2)}, u32[]{:S(2)}) collective-permute-start(f32[128,256]{0,1:T(8,128)S(1)} %get-tuple-element.307), channel_id=1, source_target_pairs={{16,0},{32,16},{48,32},{64,48},{80,64},{96,80},{112,96},{128,112},... | collective-permute-start | bytes 393224 | tf_op jit(solution)/shard_map/while/body/eval_jaxpr/ppermute | solution.py:16
  418.6 9.5 %collective-permute-start = (f32[128,256]{0,1:T(8,128)S(1)}, f32[128,256]{0,1:T(8,128)S(1)}, u32[]{:S(2)}, u32[]{:S(2)}) collective-permute-start(f32[128,256]{0,1:T(8,128)S(1)} %get-tuple-element.307), channel_id=1, source_target_pairs={{16,0},{32,16},{48,32},{64,48},{80,64},{96,80},{112,96},{128,112},... | collective-permute-start | bytes 393224 | tf_op jit(solution)/shard_map/while/body/eval_jaxpr/ppermute | solution.py:16
  430.6 9.5 %collective-permute-start = (f32[128,256]{0,1:T(8,128)S(1)}, f32[128,256]{0,1:T(8,128)S(1)}, u32[]{:S(2)}, u32[]{:S(2)}) collective-permute-start(f32[128,256]{0,1:T(8,128)S(1)} %get-tuple-element.307), channel_id=1, source_target_pairs={{16,0},{32,16},{48,32},{64,48},{80,64},{96,80},{112,96},{128,112},... | collective-permute-start | bytes 393224 | tf_op jit(solution)/shard_map/while/body/eval_jaxpr/ppermute | solution.py:16
  442.6 9.5 %collective-permute-start = (f32[128,256]{0,1:T(8,128)S(1)}, f32[128,256]{0,1:T(8,128)S(1)}, u32[]{:S(2)}, u32[]{:S(2)}) collective-permute-start(f32[128,256]{0,1:T(8,128)S(1)} %get-tuple-element.307), channel_id=1, source_target_pairs={{16,0},{32,16},{48,32},{64,48},{80,64},{96,80},{112,96},{128,112},... | collective-permute-start | bytes 393224 | tf_op jit(solution)/shard_map/while/body/eval_jaxpr/ppermute | solution.py:16
  454.6 9.5 %collective-permute-start = (f32[128,256]{0,1:T(8,128)S(1)}, f32[128,256]{0,1:T(8,128)S(1)}, u32[]{:S(2)}, u32[]{:S(2)}) collective-permute-start(f32[128,256]{0,1:T(8,128)S(1)} %get-tuple-element.307), channel_id=1, source_target_pairs={{16,0},{32,16},{48,32},{64,48},{80,64},{96,80},{112,96},{128,112},... | collective-permute-start | bytes 393224 | tf_op jit(solution)/shard_map/while/body/eval_jaxpr/ppermute | solution.py:16
  466.6 9.5 %collective-permute-start = (f32[128,256]{0,1:T(8,128)S(1)}, f32[128,256]{0,1:T(8,128)S(1)}, u32[]{:S(2)}, u32[]{:S(2)}) collective-permute-start(f32[128,256]{0,1:T(8,128)S(1)} %get-tuple-element.307), channel_id=1, source_target_pairs={{16,0},{32,16},{48,32},{64,48},{80,64},{96,80},{112,96},{128,112},... | collective-permute-start | bytes 393224 | tf_op jit(solution)/shard_map/while/body/eval_jaxpr/ppermute | solution.py:16
  478.7 9.5 %collective-permute-start = (f32[128,256]{0,1:T(8,128)S(1)}, f32[128,256]{0,1:T(8,128)S(1)}, u32[]{:S(2)}, u32[]{:S(2)}) collective-permute-start(f32[128,256]{0,1:T(8,128)S(1)} %get-tuple-element.307), channel_id=1, source_target_pairs={{16,0},{32,16},{48,32},{64,48},{80,64},{96,80},{112,96},{128,112},... | collective-permute-start | bytes 393224 | tf_op jit(solution)/shard_map/while/body/eval_jaxpr/ppermute | solution.py:16
  490.7 9.5 %collective-permute-start = (f32[128,256]{0,1:T(8,128)S(1)}, f32[128,256]{0,1:T(8,128)S(1)}, u32[]{:S(2)}, u32[]{:S(2)}) collective-permute-start(f32[128,256]{0,1:T(8,128)S(1)} %get-tuple-element.307), channel_id=1, source_target_pairs={{16,0},{32,16},{48,32},{64,48},{80,64},{96,80},{112,96},{128,112},... | collective-permute-start | bytes 393224 | tf_op jit(solution)/shard_map/while/body/eval_jaxpr/ppermute | solution.py:16
  502.7 9.5 %collective-permute-start = (f32[128,256]{0,1:T(8,128)S(1)}, f32[128,256]{0,1:T(8,128)S(1)}, u32[]{:S(2)}, u32[]{:S(2)}) collective-permute-start(f32[128,256]{0,1:T(8,128)S(1)} %get-tuple-element.307), channel_id=1, source_target_pairs={{16,0},{32,16},{48,32},{64,48},{80,64},{96,80},{112,96},{128,112},... | collective-permute-start | bytes 393224 | tf_op jit(solution)/shard_map/while/body/eval_jaxpr/ppermute | solution.py:16
  514.7 9.5 %collective-permute-start = (f32[128,256]{0,1:T(8,128)S(1)}, f32[128,256]{0,1:T(8,128)S(1)}, u32[]{:S(2)}, u32[]{:S(2)}) collective-permute-start(f32[128,256]{0,1:T(8,128)S(1)} %get-tuple-element.307), channel_id=1, source_target_pairs={{16,0},{32,16},{48,32},{64,48},{80,64},{96,80},{112,96},{128,112},... | collective-permute-start | bytes 393224 | tf_op jit(solution)/shard_map/while/body/eval_jaxpr/ppermute | solution.py:16
  526.8 3.5 collective-permute-start.1
  (279 shorter events, 98.6 us)
Async XLA Ops:
  7.2 110.9 %all-gather.3.cloned.1.call-start = ((), (), s32[]{:S(2)}) async-start(), calls=%async_computation.1 | async-start | bytes 1605632 | tf_op jit(solution)/shard_map/all_gather | solution.py:75
  13.7 36.7 %all-to-all-start = ((bf16[16,32,384]{2,1,0:T(8,128)(2,1)}), bf16[16,32,384]{2,1,0:T(8,128)(2,1)S(1)}, u32[]{:S(2)}, u32[]{:S(2)}) async-start(bf16[16,32,384]{2,1,0:T(8,128)(2,1)} %bitcast.24), calls=%async_computation | async-start | bytes 786432 | tf_op jit(solution)/shard_map/all_to_all | solution.py:171
  33.7 184.0 %all-gather.5.cloned.1.call-start = ((), (), s32[]{:S(2)}) async-start(), calls=%async_computation.2 | async-start | bytes 1605632 | tf_op jit(solution)/shard_map/all_gather | solution.py:76
  35.5 82.6 %copy-start.38 = (s32[128]{0:T(128)}, s32[128]{0:T(128)S(1)}, u32[]{:S(2)}) copy-start(s32[128]{0:T(128)S(1)} %dynamic_slice.53) | copy-start | bytes 1540
  37.0 81.1 %copy-start.41 = (s32[128]{0:T(128)}, s32[128]{0:T(128)S(1)}, u32[]{:S(2)}) copy-start(s32[128]{0:T(128)S(1)} %iota_add_fusion.1) | copy-start | bytes 1540
  228.8 301.5 %copy-start.10 = (bf16[128,3328]{0,1:T(8,128)(2,1)S(1)}, bf16[128,3328]{0,1:T(8,128)(2,1)}, u32[]{:S(2)}) copy-start(bf16[128,3328]{0,1:T(8,128)(2,1)} %copy-done.9) | copy-start | bytes 2555908
  228.8 9.4 %collective-permute-start = (f32[128,256]{0,1:T(8,128)S(1)}, f32[128,256]{0,1:T(8,128)S(1)}, u32[]{:S(2)}, u32[]{:S(2)}) collective-permute-start(f32[128,256]{0,1:T(8,128)S(1)} %get-tuple-element.307), channel_id=1, source_target_pairs={{16,0},{32,16},{48,32},{64,48},{80,64},{96,80},{112,96},{128,112},... | collective-permute-start | bytes 393224 | tf_op jit(solution)/shard_map/while/body/eval_jaxpr/ppermute | solution.py:16
  238.2 12.0 %collective-permute-start = (f32[128,256]{0,1:T(8,128)S(1)}, f32[128,256]{0,1:T(8,128)S(1)}, u32[]{:S(2)}, u32[]{:S(2)}) collective-permute-start(f32[128,256]{0,1:T(8,128)S(1)} %get-tuple-element.307), channel_id=1, source_target_pairs={{16,0},{32,16},{48,32},{64,48},{80,64},{96,80},{112,96},{128,112},... | collective-permute-start | bytes 393224 | tf_op jit(solution)/shard_map/while/body/eval_jaxpr/ppermute | solution.py:16
  250.2 12.0 %collective-permute-start = (f32[128,256]{0,1:T(8,128)S(1)}, f32[128,256]{0,1:T(8,128)S(1)}, u32[]{:S(2)}, u32[]{:S(2)}) collective-permute-start(f32[128,256]{0,1:T(8,128)S(1)} %get-tuple-element.307), channel_id=1, source_target_pairs={{16,0},{32,16},{48,32},{64,48},{80,64},{96,80},{112,96},{128,112},... | collective-permute-start | bytes 393224 | tf_op jit(solution)/shard_map/while/body/eval_jaxpr/ppermute | solution.py:16
  262.3 12.0 %collective-permute-start = (f32[128,256]{0,1:T(8,128)S(1)}, f32[128,256]{0,1:T(8,128)S(1)}, u32[]{:S(2)}, u32[]{:S(2)}) collective-permute-start(f32[128,256]{0,1:T(8,128)S(1)} %get-tuple-element.307), channel_id=1, source_target_pairs={{16,0},{32,16},{48,32},{64,48},{80,64},{96,80},{112,96},{128,112},... | collective-permute-start | bytes 393224 | tf_op jit(solution)/shard_map/while/body/eval_jaxpr/ppermute | solution.py:16
  274.3 12.0 %collective-permute-start = (f32[128,256]{0,1:T(8,128)S(1)}, f32[128,256]{0,1:T(8,128)S(1)}, u32[]{:S(2)}, u32[]{:S(2)}) collective-permute-start(f32[128,256]{0,1:T(8,128)S(1)} %get-tuple-element.307), channel_id=1, source_target_pairs={{16,0},{32,16},{48,32},{64,48},{80,64},{96,80},{112,96},{128,112},... | collective-permute-start | bytes 393224 | tf_op jit(solution)/shard_map/while/body/eval_jaxpr/ppermute | solution.py:16
  286.3 12.0 %collective-permute-start = (f32[128,256]{0,1:T(8,128)S(1)}, f32[128,256]{0,1:T(8,128)S(1)}, u32[]{:S(2)}, u32[]{:S(2)}) collective-permute-start(f32[128,256]{0,1:T(8,128)S(1)} %get-tuple-element.307), channel_id=1, source_target_pairs={{16,0},{32,16},{48,32},{64,48},{80,64},{96,80},{112,96},{128,112},... | collective-permute-start | bytes 393224 | tf_op jit(solution)/shard_map/while/body/eval_jaxpr/ppermute | solution.py:16
  298.3 12.0 %collective-permute-start = (f32[128,256]{0,1:T(8,128)S(1)}, f32[128,256]{0,1:T(8,128)S(1)}, u32[]{:S(2)}, u32[]{:S(2)}) collective-permute-start(f32[128,256]{0,1:T(8,128)S(1)} %get-tuple-element.307), channel_id=1, source_target_pairs={{16,0},{32,16},{48,32},{64,48},{80,64},{96,80},{112,96},{128,112},... | collective-permute-start | bytes 393224 | tf_op jit(solution)/shard_map/while/body/eval_jaxpr/ppermute | solution.py:16
  310.4 12.0 %collective-permute-start = (f32[128,256]{0,1:T(8,128)S(1)}, f32[128,256]{0,1:T(8,128)S(1)}, u32[]{:S(2)}, u32[]{:S(2)}) collective-permute-start(f32[128,256]{0,1:T(8,128)S(1)} %get-tuple-element.307), channel_id=1, source_target_pairs={{16,0},{32,16},{48,32},{64,48},{80,64},{96,80},{112,96},{128,112},... | collective-permute-start | bytes 393224 | tf_op jit(solution)/shard_map/while/body/eval_jaxpr/ppermute | solution.py:16
  322.4 12.0 %collective-permute-start = (f32[128,256]{0,1:T(8,128)S(1)}, f32[128,256]{0,1:T(8,128)S(1)}, u32[]{:S(2)}, u32[]{:S(2)}) collective-permute-start(f32[128,256]{0,1:T(8,128)S(1)} %get-tuple-element.307), channel_id=1, source_target_pairs={{16,0},{32,16},{48,32},{64,48},{80,64},{96,80},{112,96},{128,112},... | collective-permute-start | bytes 393224 | tf_op jit(solution)/shard_map/while/body/eval_jaxpr/ppermute | solution.py:16
  334.4 12.0 %collective-permute-start = (f32[128,256]{0,1:T(8,128)S(1)}, f32[128,256]{0,1:T(8,128)S(1)}, u32[]{:S(2)}, u32[]{:S(2)}) collective-permute-start(f32[128,256]{0,1:T(8,128)S(1)} %get-tuple-element.307), channel_id=1, source_target_pairs={{16,0},{32,16},{48,32},{64,48},{80,64},{96,80},{112,96},{128,112},... | collective-permute-start | bytes 393224 | tf_op jit(solution)/shard_map/while/body/eval_jaxpr/ppermute | solution.py:16
  346.4 12.0 %collective-permute-start = (f32[128,256]{0,1:T(8,128)S(1)}, f32[128,256]{0,1:T(8,128)S(1)}, u32[]{:S(2)}, u32[]{:S(2)}) collective-permute-start(f32[128,256]{0,1:T(8,128)S(1)} %get-tuple-element.307), channel_id=1, source_target_pairs={{16,0},{32,16},{48,32},{64,48},{80,64},{96,80},{112,96},{128,112},... | collective-permute-start | bytes 393224 | tf_op jit(solution)/shard_map/while/body/eval_jaxpr/ppermute | solution.py:16
  358.4 12.0 %collective-permute-start = (f32[128,256]{0,1:T(8,128)S(1)}, f32[128,256]{0,1:T(8,128)S(1)}, u32[]{:S(2)}, u32[]{:S(2)}) collective-permute-start(f32[128,256]{0,1:T(8,128)S(1)} %get-tuple-element.307), channel_id=1, source_target_pairs={{16,0},{32,16},{48,32},{64,48},{80,64},{96,80},{112,96},{128,112},... | collective-permute-start | bytes 393224 | tf_op jit(solution)/shard_map/while/body/eval_jaxpr/ppermute | solution.py:16
  370.5 12.0 %collective-permute-start = (f32[128,256]{0,1:T(8,128)S(1)}, f32[128,256]{0,1:T(8,128)S(1)}, u32[]{:S(2)}, u32[]{:S(2)}) collective-permute-start(f32[128,256]{0,1:T(8,128)S(1)} %get-tuple-element.307), channel_id=1, source_target_pairs={{16,0},{32,16},{48,32},{64,48},{80,64},{96,80},{112,96},{128,112},... | collective-permute-start | bytes 393224 | tf_op jit(solution)/shard_map/while/body/eval_jaxpr/ppermute | solution.py:16
  382.5 12.0 %collective-permute-start = (f32[128,256]{0,1:T(8,128)S(1)}, f32[128,256]{0,1:T(8,128)S(1)}, u32[]{:S(2)}, u32[]{:S(2)}) collective-permute-start(f32[128,256]{0,1:T(8,128)S(1)} %get-tuple-element.307), channel_id=1, source_target_pairs={{16,0},{32,16},{48,32},{64,48},{80,64},{96,80},{112,96},{128,112},... | collective-permute-start | bytes 393224 | tf_op jit(solution)/shard_map/while/body/eval_jaxpr/ppermute | solution.py:16
  394.5 12.0 %collective-permute-start = (f32[128,256]{0,1:T(8,128)S(1)}, f32[128,256]{0,1:T(8,128)S(1)}, u32[]{:S(2)}, u32[]{:S(2)}) collective-permute-start(f32[128,256]{0,1:T(8,128)S(1)} %get-tuple-element.307), channel_id=1, source_target_pairs={{16,0},{32,16},{48,32},{64,48},{80,64},{96,80},{112,96},{128,112},... | collective-permute-start | bytes 393224 | tf_op jit(solution)/shard_map/while/body/eval_jaxpr/ppermute | solution.py:16
  406.5 12.0 %collective-permute-start = (f32[128,256]{0,1:T(8,128)S(1)}, f32[128,256]{0,1:T(8,128)S(1)}, u32[]{:S(2)}, u32[]{:S(2)}) collective-permute-start(f32[128,256]{0,1:T(8,128)S(1)} %get-tuple-element.307), channel_id=1, source_target_pairs={{16,0},{32,16},{48,32},{64,48},{80,64},{96,80},{112,96},{128,112},... | collective-permute-start | bytes 393224 | tf_op jit(solution)/shard_map/while/body/eval_jaxpr/ppermute | solution.py:16
  418.6 12.0 %collective-permute-start = (f32[128,256]{0,1:T(8,128)S(1)}, f32[128,256]{0,1:T(8,128)S(1)}, u32[]{:S(2)}, u32[]{:S(2)}) collective-permute-start(f32[128,256]{0,1:T(8,128)S(1)} %get-tuple-element.307), channel_id=1, source_target_pairs={{16,0},{32,16},{48,32},{64,48},{80,64},{96,80},{112,96},{128,112},... | collective-permute-start | bytes 393224 | tf_op jit(solution)/shard_map/while/body/eval_jaxpr/ppermute | solution.py:16
  430.6 12.0 %collective-permute-start = (f32[128,256]{0,1:T(8,128)S(1)}, f32[128,256]{0,1:T(8,128)S(1)}, u32[]{:S(2)}, u32[]{:S(2)}) collective-permute-start(f32[128,256]{0,1:T(8,128)S(1)} %get-tuple-element.307), channel_id=1, source_target_pairs={{16,0},{32,16},{48,32},{64,48},{80,64},{96,80},{112,96},{128,112},... | collective-permute-start | bytes 393224 | tf_op jit(solution)/shard_map/while/body/eval_jaxpr/ppermute | solution.py:16
  442.6 12.0 %collective-permute-start = (f32[128,256]{0,1:T(8,128)S(1)}, f32[128,256]{0,1:T(8,128)S(1)}, u32[]{:S(2)}, u32[]{:S(2)}) collective-permute-start(f32[128,256]{0,1:T(8,128)S(1)} %get-tuple-element.307), channel_id=1, source_target_pairs={{16,0},{32,16},{48,32},{64,48},{80,64},{96,80},{112,96},{128,112},... | collective-permute-start | bytes 393224 | tf_op jit(solution)/shard_map/while/body/eval_jaxpr/ppermute | solution.py:16
  454.6 12.0 %collective-permute-start = (f32[128,256]{0,1:T(8,128)S(1)}, f32[128,256]{0,1:T(8,128)S(1)}, u32[]{:S(2)}, u32[]{:S(2)}) collective-permute-start(f32[128,256]{0,1:T(8,128)S(1)} %get-tuple-element.307), channel_id=1, source_target_pairs={{16,0},{32,16},{48,32},{64,48},{80,64},{96,80},{112,96},{128,112},... | collective-permute-start | bytes 393224 | tf_op jit(solution)/shard_map/while/body/eval_jaxpr/ppermute | solution.py:16
  466.6 12.0 %collective-permute-start = (f32[128,256]{0,1:T(8,128)S(1)}, f32[128,256]{0,1:T(8,128)S(1)}, u32[]{:S(2)}, u32[]{:S(2)}) collective-permute-start(f32[128,256]{0,1:T(8,128)S(1)} %get-tuple-element.307), channel_id=1, source_target_pairs={{16,0},{32,16},{48,32},{64,48},{80,64},{96,80},{112,96},{128,112},... | collective-permute-start | bytes 393224 | tf_op jit(solution)/shard_map/while/body/eval_jaxpr/ppermute | solution.py:16
  478.7 12.0 %collective-permute-start = (f32[128,256]{0,1:T(8,128)S(1)}, f32[128,256]{0,1:T(8,128)S(1)}, u32[]{:S(2)}, u32[]{:S(2)}) collective-permute-start(f32[128,256]{0,1:T(8,128)S(1)} %get-tuple-element.307), channel_id=1, source_target_pairs={{16,0},{32,16},{48,32},{64,48},{80,64},{96,80},{112,96},{128,112},... | collective-permute-start | bytes 393224 | tf_op jit(solution)/shard_map/while/body/eval_jaxpr/ppermute | solution.py:16
  490.7 12.0 %collective-permute-start = (f32[128,256]{0,1:T(8,128)S(1)}, f32[128,256]{0,1:T(8,128)S(1)}, u32[]{:S(2)}, u32[]{:S(2)}) collective-permute-start(f32[128,256]{0,1:T(8,128)S(1)} %get-tuple-element.307), channel_id=1, source_target_pairs={{16,0},{32,16},{48,32},{64,48},{80,64},{96,80},{112,96},{128,112},... | collective-permute-start | bytes 393224 | tf_op jit(solution)/shard_map/while/body/eval_jaxpr/ppermute | solution.py:16
  502.7 12.0 %collective-permute-start = (f32[128,256]{0,1:T(8,128)S(1)}, f32[128,256]{0,1:T(8,128)S(1)}, u32[]{:S(2)}, u32[]{:S(2)}) collective-permute-start(f32[128,256]{0,1:T(8,128)S(1)} %get-tuple-element.307), channel_id=1, source_target_pairs={{16,0},{32,16},{48,32},{64,48},{80,64},{96,80},{112,96},{128,112},... | collective-permute-start | bytes 393224 | tf_op jit(solution)/shard_map/while/body/eval_jaxpr/ppermute | solution.py:16
  514.7 12.0 %collective-permute-start = (f32[128,256]{0,1:T(8,128)S(1)}, f32[128,256]{0,1:T(8,128)S(1)}, u32[]{:S(2)}, u32[]{:S(2)}) collective-permute-start(f32[128,256]{0,1:T(8,128)S(1)} %get-tuple-element.307), channel_id=1, source_target_pairs={{16,0},{32,16},{48,32},{64,48},{80,64},{96,80},{112,96},{128,112},... | collective-permute-start | bytes 393224 | tf_op jit(solution)/shard_map/while/body/eval_jaxpr/ppermute | solution.py:16
  526.8 6.3 %collective-permute-start.1 = (f32[128,128]{0,1:T(8,128)S(1)}, f32[128,128]{0,1:T(8,128)S(1)}, u32[]{:S(2)}, u32[]{:S(2)}) collective-permute-start(f32[128,128]{0,1:T(8,128)S(1)} %pad_maximum_fusion.5), channel_id=1, source_target_pairs={{0,1},{1,0},{2,3},{3,2},{4,5},{5,4},{6,7},{7,6},{8,9},{9,8},{10,11... | collective-permute-start | bytes 196616 | tf_op jit(solution)/shard_map/ppermute | solution.py:22
  (50 other events, 426.5 us)
Sparse Core Ops, SparseCore 0:
  10.6 107.4 all-gather.2
  120.6 97.0 all-gather.4
where the time goes:
time: 544 us; the launch traced here: 541 us
  starting transfers between devices  258 us (47%)
  waiting for transfers between devices  171 us (31%)
  matrix products  73.9 us (14%)
  between operations  15.1 us (3%)
  local copies, waits for them, and re-layouts  10.8 us (2%)
  other arithmetic  10.7 us (2%)
    ppermute x25, starting transfers between devices, shifted(): return lax.ppermute(x, axis, pairs)  235 us
    all_gather x1, waiting for transfers between devices, local(): lax.all_gather(own_values, 'ctx', axis=0, tiled=True)  86.5 us
    all_gather x1, waiting for transfers between devices, local(): lax.all_gather(own_keys, 'ctx', axis=0, tiled=True)  65.9 us
    dot_general x26, matrix products, window_terms(): jnp.einsum('hqk,hqd->kd', prob_block, stacked_grads, preferred_element_ty...  28.2 us
    dot_general x26, matrix products, window_terms(): jnp.einsum('hqk,hqd->kd', score_block, stacked_queries, preferred_element...  27.6 us
    all_to_all x1, starting transfers between devices, local(): lax.all_to_all(buffer, 'tp', split_axis=0, concat_axis=2, tiled=True)[0]  20 us
  transfers between devices with their start and end apart: 29, of which 29 were waited for; matrix products, arithmetic and copies ran while one was open for 15% of the time, Pallas kernels for 0%

commit v1 on v0

v1 whole, which is shorter than its diff:
```python
import functools
import math

import jax
import jax.numpy as jnp
from jax import lax
from jax.experimental import pallas as pl
from jax.experimental.pallas import tpu as pltpu
from jax.sharding import Mesh
from jax.sharding import PartitionSpec as P

HD = 128
X, Z = 4, 6
ROWS = 128
KB = 64
PLANE = Z * KB
HEADS = 6
OWN = 3
WINDOW = 14
CHUNK = 2 * KB
STEPS = WINDOW // 2
PLACES = KB + 3 * PLANE
SCALE = 1.0 / math.sqrt(HD)
LOG2E = 1.4426950408889634
NEG = -1e30
SLOTS = 32

F32 = jnp.float32
BF16 = jnp.bfloat16
VMEM_LIMIT = 48 * 1024 * 1024


def dot_nt(a, b):
    return lax.dot_general(a, b, (((1,), (1,)), ((), ())), preferred_element_type=F32)


def dot_nn(a, b):
    return lax.dot_general(a, b, (((1,), (0,)), ((), ())), preferred_element_type=F32)


def call(kernel, out_shape, scratch_shapes, flops=0, nbytes=1 << 20, name=None):
    return pl.pallas_call(
        kernel,
        out_shape=out_shape,
        scratch_shapes=scratch_shapes,
        compiler_params=pltpu.CompilerParams(vmem_limit_bytes=VMEM_LIMIT),
        cost_estimate=pl.CostEstimate(flops=flops, bytes_accessed=nbytes, transcendentals=0),
        name=name,
    )


def place(z, c, p, parts, q_s, do_s, kv_s):
    qd, qd_y, qd_c, kvx, kv2, kv1, kv0 = parts
    for owner, ref, base in ((p, qd, 0), (1 - p, qd_y, 0)):
        for h in range(OWN):
            q_s[owner * OWN + h, pl.ds(c * ROWS, ROWS), :] = ref[:, h * HD : (h + 1) * HD]
            do_s[owner * OWN + h, pl.ds(c * ROWS, ROWS), :] = ref[:, (OWN + h) * HD : (OWN + h + 1) * HD]
    for owner, base in ((p, 0), (1 - p, ROWS)):
        for h in range(OWN):
            q_s[owner * OWN + h, pl.ds((1 - c) * ROWS, ROWS), :] = qd_c[base : base + ROWS, h * HD : (h + 1) * HD]
            do_s[owner * OWN + h, pl.ds((1 - c) * ROWS, ROWS), :] = qd_c[
                base : base + ROWS, (OWN + h) * HD : (OWN + h + 1) * HD
            ]
    kv_s[0:KB, :] = kvx[...]
    kv_s[KB : KB + PLANE, :] = kv2[...]
    kv_s[KB + PLANE : KB + 2 * PLANE, :] = kv1[...]
    kv_s[KB + 2 * PLANE : KB + 3 * PLANE, :] = kv0[...]


def query_spans(doc, chip):
    docs = doc[...]
    mine = jnp.concatenate([doc[pl.ds(2 * chip, 1), :], doc[pl.ds(2 * chip + 1, 1), :]], axis=1)
    first = jnp.zeros((1, 2 * ROWS), jnp.int32)
    for d in range(1, 8):
        before = jnp.sum((docs < d).astype(F32)).astype(jnp.int32)
        first = jnp.where(mine == d, before, first)
    last = chip * 2 * ROWS + lax.broadcasted_iota(jnp.int32, (1, 2 * ROWS), 1)
    return first, last


def bias_of(t, chip, c, p, first, last):
    i = lax.broadcasted_iota(jnp.int32, (CHUNK, 2 * ROWS), 0)
    base = (2 * (chip - (WINDOW - 1) + 2 * t) + c) * ROWS + p * KB
    pos = base + (i // KB) * (2 * ROWS) + i % KB
    return jnp.where((pos >= first) & (pos <= last), 0.0, NEG)


def stats_kernel(qd, qd_y, qd_c, kvx, kv2, kv1, kv0, o_own, doc, stats, q_s, do_s, kv_s, m_s, l_s):
    x, z, c, p = (lax.axis_index(a) for a in ("x", "z", "c", "yl"))
    chip = x * Z + z
    place(z, c, p, (qd, qd_y, qd_c, kvx, kv2, kv1, kv0), q_s, do_s, kv_s)
    first, last = query_spans(doc, chip)
    m_s[...] = jnp.full(m_s.shape, NEG, F32)
    l_s[...] = jnp.zeros(l_s.shape, F32)

    def step(t, _):
        keys = kv_s[pl.ds(pl.multiple_of(z * KB + t * CHUNK, KB), CHUNK), 0:HD]
        bias = bias_of(t, chip, c, p, first, last)
        for h in range(HEADS):
            s = dot_nt(keys, q_s[h]) * (SCALE * LOG2E) + bias
            s = s.reshape(CHUNK // 8, 8, 2 * ROWS)
            old = m_s[h]
            new = jnp.maximum(old, jnp.max(s, axis=0))
            l_s[h] = l_s[h] * jnp.exp2(old - new) + jnp.sum(jnp.exp2(s - new[None]), axis=0)
            m_s[h] = new
        return 0

    lax.fori_loop(0, STEPS, step, 0)
    for h in range(HEADS):
        top = jnp.max(m_s[h], axis=0, keepdims=True)
        total = jnp.sum(l_s[h] * jnp.exp2(m_s[h] - top), axis=0, keepdims=True)
        for r in range(2):
            stats[2 * h + r : 2 * h + r + 1, :] = top[:, r * ROWS : (r + 1) * ROWS]
            stats[12 + 2 * h + r : 13 + 2 * h + r, :] = total[:, r * ROWS : (r + 1) * ROWS]
    for h in range(OWN):
        prod = qd[:, (OWN + h) * HD : (OWN + h + 1) * HD].astype(F32) * o_own[:, h * HD : (h + 1) * HD].astype(F32)
        stats[24 + h : 25 + h, :] = jnp.sum(prod.T, axis=0, keepdims=True)
    stats[27:32, :] = jnp.zeros((5, ROWS), F32)


def grads_kernel(
    qd, qd_y, qd_c, kvx, kv2, kv1, kv0, doc, stats, d2, d1, d0, dx, dq, q_s, do_s, kv_s, acc_s, dq_s
):
    x, z, c, p = (lax.axis_index(a) for a in ("x", "z", "c", "yl"))
    chip = x * Z + z
    place(z, c, p, (qd, qd_y, qd_c, kvx, kv2, kv1, kv0), q_s, do_s, kv_s)
    first, last = query_spans(doc, chip)
    acc_s[...] = jnp.zeros(acc_s.shape, F32)
    dq_s[...] = jnp.zeros(dq_s.shape, F32)
    tops = [stats[i, 0:12, :] for i in range(4)]
    top = jnp.maximum(jnp.maximum(tops[0], tops[1]), jnp.maximum(tops[2], tops[3]))
    total = sum(stats[i, 12:24, :] * jnp.exp2(tops[i] - top) for i in range(4))
    lse = top + jnp.log(total) * LOG2E
    lses, deltas = [], []
    for h in range(HEADS):
        lses.append(jnp.concatenate([lse[2 * h : 2 * h + 1, :], lse[2 * h + 1 : 2 * h + 2, :]], axis=1))
        owner, k = h // OWN, 24 + h % OWN
        deltas.append(jnp.concatenate([stats[owner, k : k + 1, :], stats[2 + owner, k : k + 1, :]], axis=1))

    def step(t, _):
        at = pl.multiple_of(z * KB + t * CHUNK, KB)
        keys = kv_s[pl.ds(at, CHUNK), 0:HD]
        values = kv_s[pl.ds(at, CHUNK), HD : 2 * HD]
        keys_t = keys.astype(F32).T.astype(BF16)
        bias = bias_of(t, chip, c, p, first, last)
        dk = jnp.zeros((CHUNK, HD), F32)
        dv = jnp.zeros((CHUNK, HD), F32)
        for h in range(HEADS):
            q, do = q_s[h], do_s[h]
            probs = jnp.exp2(dot_nt(keys, q) * (SCALE * LOG2E) + bias - lses[h])
            score = (probs * (dot_nt(values, do) - deltas[h])).astype(BF16)
            dv = dv + dot_nn(probs.astype(BF16), do)
            dk = dk + dot_nn(score, q)
            dq_s[h] += dot_nn(keys_t, score)
        acc_s[pl.ds(at, CHUNK), 0:HD] = dk * SCALE
        acc_s[pl.ds(at, CHUNK), HD : 2 * HD] = dv
        return 0

    lax.fori_loop(0, STEPS, step, 0)
    for ref, start, size in (
        (dx, 0, KB),
        (d2, KB, PLANE),
        (d1, KB + PLANE, PLANE),
        (d0, KB + 2 * PLANE, PLANE),
    ):
        dk, dv = acc_s[start : start + size, 0:HD], acc_s[start : start + size, HD : 2 * HD]
        low = lax.broadcasted_iota(jnp.int32, (size, HD), 1) < HD // 2
        ref[:, 0:HD] = jnp.where(low, dk, pltpu.roll(dv, HD // 2, 1)).astype(ref.dtype)
        ref[:, HD : 2 * HD] = jnp.where(low, pltpu.roll(dk, HD // 2, 1), dv).astype(ref.dtype)
    for core in range(2):
        for owner in range(2):
            for h in range(OWN):
                part = dq_s[owner * OWN + h, :, core * ROWS : (core + 1) * ROWS] * SCALE
                dq[2 * core + owner, h * HD : (h + 1) * HD, :] = part.astype(dq.dtype)


def plane_kernel(d0, r1, r2, rx, out):
    for block in range(Z):
        rows = slice(block * KB, (block + 1) * KB)
        total = d0[rows, :] + r1[rows, :].astype(F32) + r2[rows, :].astype(F32)
        if block == Z - 1:
            total = total + rx[...].astype(F32)
        for half in range(2):
            out[2 * block + half] = total[:, half * HD : (half + 1) * HD].astype(BF16)


def block_kernel(parts, key_grad, value_grad):
    for half in range(2):
        total = parts[half].astype(F32)
        for block in range(1, Z):
            total = total + parts[2 * block + half].astype(F32)
        rows = slice(half * KB, (half + 1) * KB)
        key_grad[rows, :] = total[:, 0 : HD // 2].astype(BF16)
        value_grad[rows, :] = total[:, HD // 2 :].astype(BF16)


def query_kernel(parts, query_grad):
    for h in range(OWN):
        rows = slice(h * HD, (h + 1) * HD)
        total = sum(parts[i, rows, :].astype(F32) for i in range(4))
        query_grad[:, rows] = total.T.astype(BF16)


def attention(queries, key_rows, value_rows, out_grad, attn_out, doc_ids):
    group = lax.axis_index("zh") * lax.axis_size("yh") + lax.axis_index("yh")
    half = lax.axis_index("yl")
    keys = lax.dynamic_slice(key_rows, (half * KB, group * HD), (KB, HD))
    values = lax.dynamic_slice(value_rows, (half * KB, group * HD), (KB, HD))
    own = jnp.concatenate([keys, values], axis=1)
    plane = lax.all_to_all(
        jnp.broadcast_to(own[None], (Z, KB, 2 * HD)), "z", split_axis=0, concat_axis=0, tiled=True
    ).reshape(PLANE, 2 * HD)
    lone = [((0 * Z + 5) * 2 + 1, (3 * Z + 0) * 2 + 1)]
    ahead1 = lax.ppermute(plane, "x", [(i, i + 1) for i in range(X - 1)])
    ahead2 = lax.ppermute(plane, "x", [(i, i + 2) for i in range(X - 2)])
    aheadx = lax.ppermute(own, ("x", "z", "c"), lone)

    pool = jnp.concatenate([queries, out_grad], axis=1)
    pool_y = lax.ppermute(pool, "yl", [(0, 1), (1, 0)])
    pool_c = lax.ppermute(jnp.concatenate([pool, pool_y], axis=0), "c", [(0, 1), (1, 0)])

    doc = doc_ids.reshape(-1, ROWS)
    shared = (pool, pool_y, pool_c, aheadx, ahead2, ahead1, plane)
    pool_scratch = [
        pltpu.VMEM((HEADS, 2 * ROWS, HD), BF16),
        pltpu.VMEM((HEADS, 2 * ROWS, HD), BF16),
        pltpu.VMEM((PLACES, 2 * HD), BF16),
    ]
    pairs = WINDOW * KB * HEADS * 2 * ROWS
    stats = call(
        stats_kernel,
        jax.ShapeDtypeStruct((32, ROWS), F32),
        pool_scratch + [pltpu.VMEM((HEADS, 8, 2 * ROWS), F32), pltpu.VMEM((HEADS, 8, 2 * ROWS), F32)],
        flops=2 * HD * pairs,
        name="softmax_stats",
    )(*shared, attn_out, doc)
    stats = lax.all_to_all(
        jnp.broadcast_to(stats[None], (4, 32, ROWS)), ("c", "yl"), split_axis=0, concat_axis=0, tiled=True
    )
    d2, d1, d0, dx, dq = call(
        grads_kernel,
        (
            jax.ShapeDtypeStruct((PLANE, 2 * HD), BF16),
            jax.ShapeDtypeStruct((PLANE, 2 * HD), BF16),
            jax.ShapeDtypeStruct((PLANE, 2 * HD), F32),
            jax.ShapeDtypeStruct((KB, 2 * HD), BF16),
            jax.ShapeDtypeStruct((4, OWN * HD, ROWS), BF16),
        ),
        pool_scratch + [pltpu.VMEM((PLACES, 2 * HD), F32), pltpu.VMEM((HEADS, HD, 2 * ROWS), F32)],
        flops=10 * HD * pairs,
        name="score_grads",
    )(*shared, doc, stats)
    back2 = lax.ppermute(d2, "x", [(i + 2, i) for i in range(X - 2)])
    back1 = lax.ppermute(d1, "x", [(i + 1, i) for i in range(X - 1)])
    backx = lax.ppermute(dx, ("x", "z", "c"), [(b, a) for a, b in lone])
    plane_sums = call(plane_kernel, jax.ShapeDtypeStruct((2 * Z, KB, HD), BF16), [], name="plane_sum")(
        d0, back1, back2, backx
    )
    parts = lax.all_to_all(plane_sums, ("z", "yl"), split_axis=0, concat_axis=0, tiled=True)
    key_grad, value_grad = call(
        block_kernel,
        (jax.ShapeDtypeStruct((ROWS, HD // 2), BF16), jax.ShapeDtypeStruct((ROWS, HD // 2), BF16)),
        [],
        name="block_sum",
    )(parts)
    dq_parts = lax.all_to_all(dq, ("c", "yl"), split_axis=0, concat_axis=0, tiled=True)
    query_grad = call(query_kernel, jax.ShapeDtypeStruct((ROWS, OWN * HD), BF16), [], name="query_sum")(dq_parts)
    return query_grad, key_grad, value_grad


def combine_kernel(rows, ids, gates, stored, gate_grad, expert_grad):
    y = lax.axis_index("yh") * 2 + lax.axis_index("yl")
    place_in_tp = lax.axis_index("zh") * 8 + y
    expert, second = place_in_tp // 2, place_in_tp % 2
    first_hit, other_hit = ids[0:1, :] == expert, ids[1:2, :] == expert
    hit = jnp.where(first_hit | other_hit, 1.0, 0.0)
    earlier = lax.broadcasted_iota(jnp.int32, (ROWS, ROWS), 0) < lax.broadcasted_iota(jnp.int32, (ROWS, ROWS), 1)
    rank = dot_nn(
        jnp.broadcast_to(hit, (16, ROWS)).astype(BF16), jnp.where(earlier, 1.0, 0.0).astype(BF16)
    )[0:1, :].astype(jnp.int32)
    slot = second * SLOTS + lax.broadcasted_iota(jnp.int32, (SLOTS, ROWS), 0)
    chosen = jnp.where((slot == rank) & (hit > 0.0), 1.0, 0.0)
    gate = jnp.where(first_hit, gates[0:1, :], 0.0) + jnp.where(other_hit, gates[1:2, :], 0.0)
    slot_gate = jnp.sum(jnp.where(chosen > 0.0, gate, 0.0), axis=1, keepdims=True)
    chosen = chosen.astype(BF16)
    total = jnp.zeros((SLOTS, OWN * HD), F32)
    for hi in range(2):
        for y in range(8):
            routed = dot_nn(chosen, rows[y, hi])
            cols = slice((hi * 8 + y) * OWN * HD, (hi * 8 + y + 1) * OWN * HD)
            total = total + routed * stored[:, cols].astype(F32)
            expert_grad[:, cols] = (slot_gate * routed).astype(BF16)
    gate_grad[...] = jnp.sum(total.T, axis=0, keepdims=True)


def combine(row_grad, gate_weights, expert_ids, expert_out):
    high = lax.axis_index("zh")
    other = lax.ppermute(row_grad, "zh", [(0, 1), (1, 0)])
    both = jnp.where(
        high == 0, jnp.stack([row_grad, other]), jnp.stack([other, row_grad])
    )
    rows = lax.all_gather(both, ("yh", "yl"), axis=0, tiled=False)
    gate_grad, expert_grad = call(
        combine_kernel,
        (
            jax.ShapeDtypeStruct((1, SLOTS), F32),
            jax.ShapeDtypeStruct((SLOTS, expert_out.shape[2]), BF16),
        ),
        [],
        name="combine_grads",
    )(rows, expert_ids.T, gate_weights.T, expert_out[0])
    return gate_grad, expert_grad[None]


def local(
    queries,
    key_rows,
    value_rows,
    out_grad,
    attn_out,
    doc_ids,
    row_grad,
    gate_weights,
    expert_ids,
    expert_out,
):
    gate_grad, expert_grad = combine(row_grad, gate_weights, expert_ids, expert_out)
    query_grad, key_grad, value_grad = attention(queries, key_rows, value_rows, out_grad, attn_out, doc_ids)
    return (query_grad, key_grad, value_grad, gate_grad, expert_grad)


def solution(mesh):
    devices = mesh.devices.reshape(X, Z, 2, 2, 4, 2)
    split = Mesh(devices, ("x", "z", "c", "zh", "yh", "yl"))
    ctx, tp = ("x", "z", "c"), ("zh", "yh", "yl")
    in_specs = (
        P(ctx, tp),
        P(ctx, None),
        P(ctx, None),
        P(ctx, tp),
        P(ctx, tp),
        P(),
        P(ctx, tp),
        P(ctx, None),
        P(ctx, None),
        P(ctx, tp, None),
    )
    out_specs = (P(ctx, tp), P(ctx, tp), P(ctx, tp), P(ctx, tp), P(ctx, tp, None))
    return jax.shard_map(local, mesh=split, in_specs=in_specs, out_specs=out_specs, check_vma=False)
```

time: 544 us -> 137 us (0.25)
  the two profiles are of different devices: /device:TPU:4 before, /device:TPU:1 now
where the time goes in v1:
time: 137 us; the launch traced here: 136 us
  starting transfers between devices  55.6 us (41%)
  waiting for transfers between devices  33.2 us (24%)
  Pallas kernels  16.6 us (12%)
  between operations  14.2 us (10%)
  blocking collectives  8.1 us (6%)
  local copies, waits for them, and re-layouts  6.77 us (5%)
  other arithmetic  1.72 us (1%)
    ppermute x1, starting transfers between devices, combine(): other = lax.ppermute(row_grad, 'zh', [(0, 1), (1, 0)])  15.7 us
    all_to_all x1, starting transfers between devices, attention(): lax.all_to_all(jnp.broadcast_to(own[None], (Z, KB, 2 * HD)), 'z', split_a...  10.7 us
    pallas_call x1, Pallas kernels, attention(): call(grads_kernel, (jax.ShapeDtypeStruct((PLANE, 2 * HD), BF16), jax.Shap...  10.7 us
    all_to_all x1, waiting for transfers between devices, attention(): lax.all_to_all(plane_sums, ('z', 'yl'), split_axis=0, concat_axis=0, tile...  9.97 us
    all_to_all x1, blocking collectives, attention(): lax.all_to_all(jnp.broadcast_to(stats[None], (4, 32, ROWS)), ('c', 'yl'),...  8.1 us
    all_to_all x1, waiting for transfers between devices, attention(): lax.all_to_all(jnp.broadcast_to(own[None], (Z, KB, 2 * HD)), 'z', split_a...  7.89 us
    all_to_all x1, starting transfers between devices, attention(): lax.all_to_all(plane_sums, ('z', 'yl'), split_axis=0, concat_axis=0, tile...  7.23 us
    ppermute x1, waiting for transfers between devices, attention(): back1 = lax.ppermute(d1, 'x', [(i + 1, i) for i in range(X - 1)])  6.05 us
  transfers between devices with their start and end apart: 13, of which 6 were waited for; matrix products, arithmetic and copies ran while one was open for 4% of the time, Pallas kernels for 11%

profile of v1, /device:TPU:1, one launch (start us, length us, event | category | flops | bytes accessed | tf_op | source)
XLA Modules:
  0.0 136.2 jit_solution(3708780277969054619)
XLA Ops:
  7.2 15.7 %collective-permute-start.8 = (bf16[128,384]{1,0:T(8,128)(2,1)}, bf16[128,384]{1,0:T(8,128)(2,1)S(1)}, u32[]{:S(2)}, u32[]{:S(2)}) collective-permute-start(bf16[128,384]{1,0:T(8,128)(2,1)} %param.16), channel_id=1, source_target_pairs={{0,8},{8,0},{1,9},{9,1},{2,10},{10,2},{3,11},{11,3},{4,12},{12,4},... | collective-permute-start | bytes 294920 | tf_op jit(solution)/shard_map/ppermute | solution.py:298
  22.9 2.4 %collective-permute-done.8 = bf16[128,384]{1,0:T(8,128)(2,1)S(1)} collective-permute-done((bf16[128,384]{1,0:T(8,128)(2,1)}, bf16[128,384]{1,0:T(8,128)(2,1)S(1)}, u32[]{:S(2)}, u32[]{:S(2)}) %collective-permute-start.8) | collective-permute-done | bytes 98336 | tf_op jit(solution)/shard_map/ppermute | solution.py:298
  25.3 1.7 %maximum_select_fusion = bf16[1,2,128,384]{3,2,1,0:T(8,128)(2,1)} fusion(bf16[1,1,128,384]{3,2,1,0:T(8,128)(2,1)S(1)} %bitcast.18, bf16[1,1,128,384]{3,2,1,0:T(8,128)(2,1)} %bitcast.17, pred[]{:T(512)S(6)} %eq.3), kind=kLoop, calls=%fused_computation.1 | loop fusion | flops 294912 | bytes 393217 | tf_op jit(solution)/shard_map/jit(_where)/select_n | solution.py:299
  27.0 0.9 constant_dynamic-update-slice_fusion.1
  28.0 0.9 constant_dynamic-update-slice_fusion.qd
  28.9 3.5 %collective-permute-start = (bf16[128,768]{1,0:T(8,128)(2,1)S(1)}, bf16[128,768]{1,0:T(8,128)(2,1)S(1)}, u32[]{:S(2)}, u32[]{:S(2)}) collective-permute-start(bf16[128,768]{1,0:T(8,128)(2,1)S(1)} %constant_dynamic-update-slice_fusion.qd), channel_id=1, source_target_pairs={{0,1},{1,0},{2,3},{3,2},{4,5},{5,4},{6,7},{7,6},{8,9},{9,8},{10,11... | collective-permute-start | bytes 589832 | tf_op jit(solution)/shard_map/ppermute | solution.py:219
  32.4 0.7 dynamic_slice.6
  33.1 0.7 dynamic_slice.7
  33.9 0.7 broadcast_in_dim.6
  34.5 10.7 %all-to-all-start = ((bf16[6,64,256]{2,1,0:T(8,128)(2,1)}), bf16[6,64,256]{2,1,0:T(8,128)(2,1)S(1)}, u32[]{:S(2)}, u32[]{:S(2)}) async-start(bf16[6,64,256]{2,1,0:T(8,128)(2,1)} %broadcast_in_dim.6), calls=%async_computation | async-start | bytes 393216 | tf_op jit(solution)/shard_map/all_to_all | solution.py:210
  45.3 3.1 %collective-permute-start.1 = (bf16[256,768]{1,0:T(8,128)(2,1)S(1)}, bf16[256,768]{1,0:T(8,128)(2,1)S(1)}, u32[]{:S(2)}, u32[]{:S(2)}) collective-permute-start(bf16[256,768]{1,0:T(8,128)(2,1)S(1)} %pad_maximum_fusion), channel_id=1, source_target_pairs={{0,16},{16,0},{1,17},{17,1},{2,18},{18,2},{3,19},{19,3},{4,20},{20... | collective-permute-start | bytes 1179656 | tf_op jit(solution)/shard_map/ppermute | solution.py:220
  48.5 7.9 %all-to-all-done = bf16[6,64,256]{2,1,0:T(8,128)(2,1)S(1)} async-done(((bf16[6,64,256]{2,1,0:T(8,128)(2,1)}), bf16[6,64,256]{2,1,0:T(8,128)(2,1)S(1)}, u32[]{:S(2)}, u32[]{:S(2)}) %all-to-all-start) | async-done | bytes 196640 | tf_op jit(solution)/shard_map/all_to_all | solution.py:210
  56.4 4.6 %collective-permute-start.3 = (bf16[384,256]{1,0:T(8,128)(2,1)S(1)}, bf16[384,256]{1,0:T(8,128)(2,1)S(1)}, u32[]{:S(2)}, u32[]{:S(2)}) collective-permute-start(bf16[384,256]{1,0:T(8,128)(2,1)S(1)} %bitcast.8), channel_id=1, source_target_pairs={{0,384},{192,576},{1,385},{193,577},{2,386},{194,578},{3,387},{195... | collective-permute-start | bytes 589832 | tf_op jit(solution)/shard_map/ppermute | solution.py:215
  61.0 2.2 %collective-permute-start.4 = (bf16[384,256]{1,0:T(8,128)(2,1)S(1)}, bf16[384,256]{1,0:T(8,128)(2,1)S(1)}, u32[]{:S(2)}, u32[]{:S(2)}) collective-permute-start(bf16[384,256]{1,0:T(8,128)(2,1)S(1)} %bitcast.9), channel_id=1, source_target_pairs={{0,192},{192,384},{384,576},{1,193},{193,385},{385,577},{2,194},{1... | collective-permute-start | bytes 589832 | tf_op jit(solution)/shard_map/ppermute | solution.py:214
  63.3 0.7 collective-permute-start.2
  64.0 4.0 %collective-permute-done.4.kv1 = bf16[384,256]{1,0:T(8,128)(2,1)S(1)} collective-permute-done((bf16[384,256]{1,0:T(8,128)(2,1)S(1)}, bf16[384,256]{1,0:T(8,128)(2,1)S(1)}, u32[]{:S(2)}, u32[]{:S(2)}) %collective-permute-start.4) | collective-permute-done | bytes 196640 | tf_op jit(solution)/shard_map/ppermute | solution.py:214
  68.0 2.9 %softmax_stats.1 = f32[32,128]{1,0:T(8,128)S(1)} custom-call(bf16[128,768]{1,0:T(8,128)(2,1)S(1)} %constant_dynamic-update-slice_fusion.qd, bf16[128,768]{1,0:T(8,128)(2,1)S(1)} %collective-permute-done.qd_y, bf16[256,768]{1,0:T(8,128)(2,1)S(1)} %collective-permute-done.1.qd_c, bf16[64,256]{1,0:T(8,128)(2,1)S(1)} %collective-permute-done.2.kvx, ...), custom_call_target="tpu_custom_call" | custom-call | flops 352321536 | bytes 1048576 | tf_op jit(solution)/shard_map/softmax_stats/pallas_call | solution.py:230
  70.9 8.1 %all_to_all.20.stats = f32[4,32,128]{2,1,0:T(8,128)S(1)} all-to-all(f32[4,32,128]{2,1,0:T(8,128)S(1)} %broadcast_in_dim.7), channel_id=1, replica_groups=mesh['x'=4,'z'=6,'c'=2,'zh'=2,'yh'=4,'yl'=2] {'c','yl'}, dimensions={0} | all-to-all | bytes 131072 | tf_op jit(solution)/shard_map/all_to_all | solution.py:237
  79.0 10.7 %score_grads.1 = (bf16[384,256]{1,0:T(8,128)(2,1)S(1)}, bf16[384,256]{1,0:T(8,128)(2,1)S(1)}, f32[384,256]{1,0:T(8,128)S(1)}, bf16[64,256]{1,0:T(8,128)(2,1)S(1)}, bf16[4,384,128]{2,1,0:T(8,128)(2,1)}) custom-call(bf16[128,768]{1,0:T(8,128)(2,1)S(1)} %constant_dynamic-update-slice_fusion.qd, bf16[128,768]{1,0:T(8,128)(2,1)S(1)} %collective-permute-done.qd_y, ...), custom_call_target="tpu_custom_call" | custom-call | flops 1761607680 | bytes 1048576 | tf_op jit(solution)/shard_map/score_grads/pallas_call | solution.py:240
  89.7 4.4 %all-to-all-start.2 = ((bf16[4,384,128]{2,1,0:T(8,128)(2,1)}), bf16[4,384,128]{2,1,0:T(8,128)(2,1)S(1)}, u32[]{:S(2)}, u32[]{:S(2)}) async-start(bf16[4,384,128]{2,1,0:T(8,128)(2,1)} %get-tuple-element.14), calls=%async_computation.2 | async-start | bytes 786432 | tf_op jit(solution)/shard_map/all_to_all | solution.py:266
  94.1 1.3 collective-permute-start.5
  95.4 1.3 collective-permute-start.6
  97.4 6.1 %collective-permute-done.5.r1 = bf16[384,256]{1,0:T(8,128)(2,1)S(1)} collective-permute-done((bf16[384,256]{1,0:T(8,128)(2,1)S(1)}, bf16[384,256]{1,0:T(8,128)(2,1)S(1)}, u32[]{:S(2)}, u32[]{:S(2)}) %collective-permute-start.5) | collective-permute-done | bytes 196640 | tf_op jit(solution)/shard_map/ppermute | solution.py:254
  103.4 2.9 %collective-permute-done.6.r2 = bf16[384,256]{1,0:T(8,128)(2,1)S(1)} collective-permute-done((bf16[384,256]{1,0:T(8,128)(2,1)S(1)}, bf16[384,256]{1,0:T(8,128)(2,1)S(1)}, u32[]{:S(2)}, u32[]{:S(2)}) %collective-permute-start.6) | collective-permute-done | bytes 196640 | tf_op jit(solution)/shard_map/ppermute | solution.py:253
  106.3 0.7 plane_sum.1
  107.0 7.2 %all-to-all-start.3 = ((bf16[12,64,128]{2,1,0:T(8,128)(2,1)}), bf16[12,64,128]{2,1,0:T(8,128)(2,1)S(1)}, u32[]{:S(2)}, u32[]{:S(2)}) async-start(bf16[12,64,128]{2,1,0:T(8,128)(2,1)} %plane_sum.1), calls=%async_computation.3 | async-start | bytes 393216 | tf_op jit(solution)/shard_map/all_to_all | solution.py:259
  114.3 0.8 query_sum.1
  115.0 10.0 %all-to-all-done.3.parts = bf16[12,64,128]{2,1,0:T(8,128)(2,1)S(1)} async-done(((bf16[12,64,128]{2,1,0:T(8,128)(2,1)}), bf16[12,64,128]{2,1,0:T(8,128)(2,1)S(1)}, u32[]{:S(2)}, u32[]{:S(2)}) %all-to-all-start.3) | async-done | bytes 196640 | tf_op jit(solution)/shard_map/all_to_all | solution.py:259
  125.1 0.7 copy.17
  125.8 0.7 copy.18
  126.5 1.4 %copy-done = bf16[8,2,128,384]{3,2,1,0:T(8,128)(2,1)S(1)} copy-done((bf16[8,2,128,384]{3,2,1,0:T(8,128)(2,1)S(1)}, bf16[8,2,128,384]{3,2,1,0:T(8,128)(2,1)}, u32[]{:S(2)}) %copy-start) | copy-done | bytes 1572888
  127.9 1.4 %combine_grads.1 = (f32[1,32]{1,0:T(1,128)}, bf16[32,6144]{1,0:T(8,128)(2,1)}) custom-call(bf16[8,2,128,384]{3,2,1,0:T(8,128)(2,1)S(1)} %copy-done, s32[2,128]{1,0:T(2,128)S(1)} %bitcast.15, f32[2,128]{1,0:T(2,128)S(1)} %bitcast.16, bf16[32,6144]{1,0:T(8,128)(2,1)S(1)} %bitcast.12), custom_call_target="tpu_custom_call" | custom-call | bytes 1048576 | tf_op jit(solution)/shard_map/combine_grads/pallas_call | solution.py:303
  (25 shorter events, 0.9 us)
Async XLA Ops:
  7.2 60.8 %copy-start.3 = (s32[6144]{0:T(1024)S(1)}, s32[6144]{0:T(1024)}, u32[]{:S(2)}) copy-start(s32[6144]{0:T(1024)} %param.15) | copy-start | bytes 73732
  7.2 60.8 %copy-start.2 = (bf16[128,384]{1,0:T(8,128)(2,1)S(1)}, bf16[128,384]{1,0:T(8,128)(2,1)}, u32[]{:S(2)}) copy-start(bf16[128,384]{1,0:T(8,128)(2,1)} %o_own.1) | copy-start | bytes 294916
  7.2 119.3 %all-gather.2.cloned.1.call-start = ((), (), s32[]{:S(2)}) async-start(), calls=%async_computation.4 | async-start | bytes 1769472 | tf_op jit(solution)/shard_map/all_gather | solution.py:302
  7.2 18.1 %collective-permute-start.8 = (bf16[128,384]{1,0:T(8,128)(2,1)}, bf16[128,384]{1,0:T(8,128)(2,1)S(1)}, u32[]{:S(2)}, u32[]{:S(2)}) collective-permute-start(bf16[128,384]{1,0:T(8,128)(2,1)} %param.16), channel_id=1, source_target_pairs={{0,8},{8,0},{1,9},{9,1},{2,10},{10,2},{3,11},{11,3},{4,12},{12,4},... | collective-permute-start | bytes 294920 | tf_op jit(solution)/shard_map/ppermute | solution.py:298
  28.9 16.4 %collective-permute-start = (bf16[128,768]{1,0:T(8,128)(2,1)S(1)}, bf16[128,768]{1,0:T(8,128)(2,1)S(1)}, u32[]{:S(2)}, u32[]{:S(2)}) collective-permute-start(bf16[128,768]{1,0:T(8,128)(2,1)S(1)} %constant_dynamic-update-slice_fusion.qd), channel_id=1, source_target_pairs={{0,1},{1,0},{2,3},{3,2},{4,5},{5,4},{6,7},{7,6},{8,9},{9,8},{10,11... | collective-permute-start | bytes 589832 | tf_op jit(solution)/shard_map/ppermute | solution.py:219
  34.5 21.8 %all-to-all-start = ((bf16[6,64,256]{2,1,0:T(8,128)(2,1)}), bf16[6,64,256]{2,1,0:T(8,128)(2,1)S(1)}, u32[]{:S(2)}, u32[]{:S(2)}) async-start(bf16[6,64,256]{2,1,0:T(8,128)(2,1)} %broadcast_in_dim.6), calls=%async_computation | async-start | bytes 393216 | tf_op jit(solution)/shard_map/all_to_all | solution.py:210
  45.3 18.6 %collective-permute-start.1 = (bf16[256,768]{1,0:T(8,128)(2,1)S(1)}, bf16[256,768]{1,0:T(8,128)(2,1)S(1)}, u32[]{:S(2)}, u32[]{:S(2)}) collective-permute-start(bf16[256,768]{1,0:T(8,128)(2,1)S(1)} %pad_maximum_fusion), channel_id=1, source_target_pairs={{0,16},{16,0},{1,17},{17,1},{2,18},{18,2},{3,19},{19,3},{4,20},{20... | collective-permute-start | bytes 1179656 | tf_op jit(solution)/shard_map/ppermute | solution.py:220
  56.4 7.6 %collective-permute-start.3 = (bf16[384,256]{1,0:T(8,128)(2,1)S(1)}, bf16[384,256]{1,0:T(8,128)(2,1)S(1)}, u32[]{:S(2)}, u32[]{:S(2)}) collective-permute-start(bf16[384,256]{1,0:T(8,128)(2,1)S(1)} %bitcast.8), channel_id=1, source_target_pairs={{0,384},{192,576},{1,385},{193,577},{2,386},{194,578},{3,387},{195... | collective-permute-start | bytes 589832 | tf_op jit(solution)/shard_map/ppermute | solution.py:215
  61.0 6.9 %collective-permute-start.4 = (bf16[384,256]{1,0:T(8,128)(2,1)S(1)}, bf16[384,256]{1,0:T(8,128)(2,1)S(1)}, u32[]{:S(2)}, u32[]{:S(2)}) collective-permute-start(bf16[384,256]{1,0:T(8,128)(2,1)S(1)} %bitcast.9), channel_id=1, source_target_pairs={{0,192},{192,384},{384,576},{1,193},{193,385},{385,577},{2,194},{1... | collective-permute-start | bytes 589832 | tf_op jit(solution)/shard_map/ppermute | solution.py:214
  63.3 0.7 collective-permute-start.2
  89.7 36.8 %copy-start.1 = (bf16[1,32,6144]{2,1,0:T(8,128)(2,1)S(1)}, bf16[1,32,6144]{2,1,0:T(8,128)(2,1)}, u32[]{:S(2)}) copy-start(bf16[1,32,6144]{2,1,0:T(8,128)(2,1)} %param.19) | copy-start | bytes 1179652
  89.7 36.8 %copy-start.4 = (s32[128,2]{0,1:T(2,128)S(1)}, s32[128,2]{0,1:T(2,128)}, u32[]{:S(2)}) copy-start(s32[128,2]{0,1:T(2,128)} %param.18) | copy-start | bytes 3076
  89.7 36.8 %copy-start.5 = (f32[128,2]{0,1:T(2,128)S(1)}, f32[128,2]{0,1:T(2,128)}, u32[]{:S(2)}) copy-start(f32[128,2]{0,1:T(2,128)} %param.17) | copy-start | bytes 3076
  89.7 17.4 %all-to-all-start.2 = ((bf16[4,384,128]{2,1,0:T(8,128)(2,1)}), bf16[4,384,128]{2,1,0:T(8,128)(2,1)S(1)}, u32[]{:S(2)}, u32[]{:S(2)}) async-start(bf16[4,384,128]{2,1,0:T(8,128)(2,1)} %get-tuple-element.14), calls=%async_computation.2 | async-start | bytes 786432 | tf_op jit(solution)/shard_map/all_to_all | solution.py:266
  94.1 9.3 %collective-permute-start.5 = (bf16[384,256]{1,0:T(8,128)(2,1)S(1)}, bf16[384,256]{1,0:T(8,128)(2,1)S(1)}, u32[]{:S(2)}, u32[]{:S(2)}) collective-permute-start(bf16[384,256]{1,0:T(8,128)(2,1)S(1)} %get-tuple-element.16), channel_id=1, source_target_pairs={{192,0},{384,192},{576,384},{193,1},{385,193},{577,385},{194,2},{3... | collective-permute-start | bytes 589832 | tf_op jit(solution)/shard_map/ppermute | solution.py:254
  95.4 10.9 %collective-permute-start.6 = (bf16[384,256]{1,0:T(8,128)(2,1)S(1)}, bf16[384,256]{1,0:T(8,128)(2,1)S(1)}, u32[]{:S(2)}, u32[]{:S(2)}) collective-permute-start(bf16[384,256]{1,0:T(8,128)(2,1)S(1)} %get-tuple-element.17), channel_id=1, source_target_pairs={{384,0},{576,192},{385,1},{577,193},{386,2},{578,194},{387,3},{579... | collective-permute-start | bytes 589832 | tf_op jit(solution)/shard_map/ppermute | solution.py:253
  96.7 0.7 collective-permute-start.7
  107.0 18.0 %all-to-all-start.3 = ((bf16[12,64,128]{2,1,0:T(8,128)(2,1)}), bf16[12,64,128]{2,1,0:T(8,128)(2,1)S(1)}, u32[]{:S(2)}, u32[]{:S(2)}) async-start(bf16[12,64,128]{2,1,0:T(8,128)(2,1)} %plane_sum.1), calls=%async_computation.3 | async-start | bytes 393216 | tf_op jit(solution)/shard_map/all_to_all | solution.py:259
  126.5 1.4 %copy-start = (bf16[8,2,128,384]{3,2,1,0:T(8,128)(2,1)S(1)}, bf16[8,2,128,384]{3,2,1,0:T(8,128)(2,1)}, u32[]{:S(2)}) copy-start(bf16[8,2,128,384]{3,2,1,0:T(8,128)(2,1)} %all-gather.2.cloned.1.call-done.rows) | copy-start | bytes 4718596
Sparse Core Ops, SparseCore 0:
  27.2 47.8 all-gather.1

commit v2 on v1

v2 whole, which is shorter than its diff:
```python
import functools
import math

import jax
import jax.numpy as jnp
from jax import lax
from jax.experimental import pallas as pl
from jax.experimental.pallas import tpu as pltpu
from jax.sharding import Mesh
from jax.sharding import PartitionSpec as P

HD = 128
X, Z = 4, 6
ROWS = 128
KB = 64
PLANE = Z * KB
HEADS = 6
OWN = 3
WINDOW = 14
SPAN = WINDOW * KB
PLACES = KB + 3 * PLANE
SCALE = 1.0 / math.sqrt(HD)
LOG2E = 1.4426950408889634
NEG = -1e30
SLOTS = 32

F32 = jnp.float32
BF16 = jnp.bfloat16
VMEM_LIMIT = 48 * 1024 * 1024


def dot_nt(a, b):
    return lax.dot_general(a, b, (((1,), (1,)), ((), ())), preferred_element_type=F32)


def dot_nn(a, b):
    return lax.dot_general(a, b, (((1,), (0,)), ((), ())), preferred_element_type=F32)


def call(kernel, out_shape, scratch_shapes, flops=0, nbytes=1 << 20, name=None, vmem=VMEM_LIMIT, **specs):
    return pl.pallas_call(
        kernel,
        out_shape=out_shape,
        scratch_shapes=scratch_shapes,
        compiler_params=pltpu.CompilerParams(vmem_limit_bytes=vmem),
        cost_estimate=pl.CostEstimate(flops=flops, bytes_accessed=nbytes, transcendentals=0),
        name=name,
        **specs,
    )


def place(z, c, p, parts, q_s, do_s, kv_s):
    qd, qd_y, qd_c, kvx, kv2, kv1, kv0 = parts
    for owner, ref, base in ((p, qd, 0), (1 - p, qd_y, 0)):
        for h in range(OWN):
            q_s[owner * OWN + h, pl.ds(c * ROWS, ROWS), :] = ref[:, h * HD : (h + 1) * HD]
            do_s[owner * OWN + h, pl.ds(c * ROWS, ROWS), :] = ref[:, (OWN + h) * HD : (OWN + h + 1) * HD]
    for owner, base in ((p, 0), (1 - p, ROWS)):
        for h in range(OWN):
            q_s[owner * OWN + h, pl.ds((1 - c) * ROWS, ROWS), :] = qd_c[base : base + ROWS, h * HD : (h + 1) * HD]
            do_s[owner * OWN + h, pl.ds((1 - c) * ROWS, ROWS), :] = qd_c[
                base : base + ROWS, (OWN + h) * HD : (OWN + h + 1) * HD
            ]
    kv_s[0:KB, :] = kvx[...]
    kv_s[KB : KB + PLANE, :] = kv2[...]
    kv_s[KB + PLANE : KB + 2 * PLANE, :] = kv1[...]
    kv_s[KB + 2 * PLANE : KB + 3 * PLANE, :] = kv0[...]


def query_spans(doc, chip):
    docs = doc[...]
    mine = jnp.concatenate([doc[pl.ds(2 * chip, 1), :], doc[pl.ds(2 * chip + 1, 1), :]], axis=1)
    first = jnp.zeros((1, 2 * ROWS), jnp.int32)
    for d in range(1, 8):
        before = jnp.sum((docs < d).astype(F32)).astype(jnp.int32)
        first = jnp.where(mine == d, before, first)
    last = chip * 2 * ROWS + lax.broadcasted_iota(jnp.int32, (1, 2 * ROWS), 1)
    return first, last


def bias_of(chip, c, p, first, last):
    i = lax.broadcasted_iota(jnp.int32, (SPAN, 2 * ROWS), 0)
    base = (2 * (chip - (WINDOW - 1)) + c) * ROWS + p * KB
    pos = base + (i // KB) * (2 * ROWS) + i % KB
    return jnp.where((pos >= first) & (pos <= last), 0.0, NEG)


def prep_kernel(queries, out_grad, key_rows, value_rows, pool, spread, sems):
    group = lax.axis_index("zh") * 4 + lax.axis_index("yh")
    rows = pl.ds(pl.multiple_of(lax.axis_index("yl") * KB, KB), KB)
    cols = pl.ds(pl.multiple_of(group * HD, HD), HD)
    copies = [
        pltpu.make_async_copy(key_rows.at[rows, cols], spread.at[0, :, 0:HD], sems.at[0]),
        pltpu.make_async_copy(value_rows.at[rows, cols], spread.at[0, :, HD : 2 * HD], sems.at[1]),
        pltpu.make_async_copy(queries, pool.at[:, 0 : OWN * HD], sems.at[2]),
        pltpu.make_async_copy(out_grad, pool.at[:, OWN * HD : 2 * OWN * HD], sems.at[3]),
    ]
    for copy in copies:
        copy.start()
    copies[0].wait()
    copies[1].wait()
    for block in range(1, Z):
        spread[block] = spread[0]
    copies[2].wait()
    copies[3].wait()


def stats_kernel(qd, qd_y, qd_c, kvx, kv2, kv1, kv0, o_own, doc, stats, q_s, do_s, kv_s):
    x, z, c, p = (lax.axis_index(a) for a in ("x", "z", "c", "yl"))
    chip = x * Z + z
    place(z, c, p, (qd, qd_y, qd_c, kvx, kv2, kv1, kv0), q_s, do_s, kv_s)
    first, last = query_spans(doc, chip)
    keys = kv_s[pl.ds(pl.multiple_of(z * KB, KB), SPAN), 0:HD]
    bias = bias_of(chip, c, p, first, last)
    rows = []
    for h in range(HEADS):
        s = dot_nt(keys, q_s[h]) * (SCALE * LOG2E) + bias
        s = s.reshape(SPAN // 8, 8, 2 * ROWS)
        fold = jnp.max(s, axis=0)
        sums = jnp.sum(jnp.exp2(s - fold[None]), axis=0)
        top = jnp.max(fold, axis=0, keepdims=True)
        total = jnp.sum(sums * jnp.exp2(fold - top), axis=0, keepdims=True)
        for r in range(2):
            rows.append((2 * h + r, top[:, r * ROWS : (r + 1) * ROWS]))
            rows.append((12 + 2 * h + r, total[:, r * ROWS : (r + 1) * ROWS]))
    for h in range(OWN):
        prod = qd[:, (OWN + h) * HD : (OWN + h + 1) * HD].astype(F32) * o_own[:, h * HD : (h + 1) * HD].astype(F32)
        rows.append((24 + h, jnp.sum(prod.T, axis=0, keepdims=True)))
    for peer in range(4):
        for at, row in rows:
            stats[peer, at : at + 1, :] = row
        stats[peer, 27:32, :] = jnp.zeros((5, ROWS), F32)


def grads_kernel(
    qd, qd_y, qd_c, kvx, kv2, kv1, kv0, doc, stats, d2, d1, d0, dx, dq_keep, dq_send, q_s, do_s, kv_s, acc_s
):
    x, z, c, p = (lax.axis_index(a) for a in ("x", "z", "c", "yl"))
    chip = x * Z + z
    place(z, c, p, (qd, qd_y, qd_c, kvx, kv2, kv1, kv0), q_s, do_s, kv_s)
    first, last = query_spans(doc, chip)
    acc_s[...] = jnp.zeros(acc_s.shape, F32)
    tops = [stats[i, 0:12, :] for i in range(4)]
    top = jnp.maximum(jnp.maximum(tops[0], tops[1]), jnp.maximum(tops[2], tops[3]))
    total = sum(stats[i, 12:24, :] * jnp.exp2(tops[i] - top) for i in range(4))
    lse = top + jnp.log(total) * LOG2E

    at = pl.multiple_of(z * KB, KB)
    keys = kv_s[pl.ds(at, SPAN), 0:HD]
    values = kv_s[pl.ds(at, SPAN), HD : 2 * HD]
    keys_t = keys.astype(F32).T.astype(BF16)
    bias = bias_of(chip, c, p, first, last)
    dk = jnp.zeros((SPAN, HD), F32)
    dv = jnp.zeros((SPAN, HD), F32)
    for h in range(HEADS):
        owner, k = h // OWN, 24 + h % OWN
        row_lse = jnp.concatenate([lse[2 * h : 2 * h + 1, :], lse[2 * h + 1 : 2 * h + 2, :]], axis=1)
        delta = jnp.concatenate([stats[owner, k : k + 1, :], stats[2 + owner, k : k + 1, :]], axis=1)
        q, do = q_s[h], do_s[h]
        probs = jnp.exp2(dot_nt(keys, q) * (SCALE * LOG2E) + bias - row_lse)
        score = (probs * (dot_nt(values, do) - delta)).astype(BF16)
        dv = dv + dot_nn(probs.astype(BF16), do)
        dk = dk + dot_nn(score, q)
        part = dot_nn(keys_t, score) * SCALE
        lower, upper = part[:, 0:ROWS], part[:, ROWS : 2 * ROWS]
        rows = slice((h % OWN) * HD, (h % OWN + 1) * HD)
        dq_keep[owner, rows, :] = jnp.where(c == 0, lower, upper)
        dq_send[owner, rows, :] = jnp.where(c == 0, upper, lower).astype(BF16)
    acc_s[pl.ds(at, SPAN), 0:HD] = dk * SCALE
    acc_s[pl.ds(at, SPAN), HD : 2 * HD] = dv
    for ref, start, size in (
        (dx, 0, KB),
        (d2, KB, PLANE),
        (d1, KB + PLANE, PLANE),
        (d0, KB + 2 * PLANE, PLANE),
    ):
        dk, dv = acc_s[start : start + size, 0:HD], acc_s[start : start + size, HD : 2 * HD]
        low = lax.broadcasted_iota(jnp.int32, (size, HD), 1) < HD // 2
        ref[:, 0:HD] = jnp.where(low, dk, pltpu.roll(dv, HD // 2, 1)).astype(ref.dtype)
        ref[:, HD : 2 * HD] = jnp.where(low, pltpu.roll(dk, HD // 2, 1), dv).astype(ref.dtype)


def plane_kernel(d0, r1, r2, rx, out):
    for block in range(Z):
        rows = slice(block * KB, (block + 1) * KB)
        total = d0[rows, :] + r1[rows, :].astype(F32) + r2[rows, :].astype(F32)
        if block == Z - 1:
            total = total + rx[...].astype(F32)
        for half in range(2):
            out[2 * block + half] = total[:, half * HD : (half + 1) * HD].astype(BF16)


def block_kernel(parts, key_grad, value_grad):
    halves = []
    for half in range(2):
        total = parts[half].astype(F32)
        for block in range(1, Z):
            total = total + parts[2 * block + half].astype(F32)
        halves.append(total)
    total = jnp.concatenate(halves, axis=0).T
    key_grad[...] = total[0 : HD // 2, :].astype(BF16)
    value_grad[...] = total[HD // 2 :, :].astype(BF16)


def pool_kernel(keep, arrived, mine, other):
    p = lax.axis_index("yl")
    mine[...] = keep[p] + arrived[p].astype(F32)
    other[...] = (keep[1 - p] + arrived[1 - p].astype(F32)).astype(BF16)


def query_kernel(mine, arrived, query_grad):
    for h in range(OWN):
        rows = slice(h * HD, (h + 1) * HD)
        query_grad[:, rows] = (mine[rows, :] + arrived[rows, :].astype(F32)).T.astype(BF16)


def combine_kernel(rows, ids, gates, stored, gate_grad, expert_grad):
    y = lax.axis_index("yh") * 2 + lax.axis_index("yl")
    high = lax.axis_index("zh")
    place_in_tp = high * 8 + y
    expert, second = place_in_tp // 2, place_in_tp % 2
    first_hit, other_hit = ids[0:1, :] == expert, ids[1:2, :] == expert
    hit = jnp.where(first_hit | other_hit, 1.0, 0.0)
    earlier = lax.broadcasted_iota(jnp.int32, (ROWS, ROWS), 0) < lax.broadcasted_iota(jnp.int32, (ROWS, ROWS), 1)
    rank = dot_nn(
        jnp.broadcast_to(hit, (16, ROWS)).astype(BF16), jnp.where(earlier, 1.0, 0.0).astype(BF16)
    )[0:1, :].astype(jnp.int32)
    slot = second * SLOTS + lax.broadcasted_iota(jnp.int32, (SLOTS, ROWS), 0)
    chosen = jnp.where((slot == rank) & (hit > 0.0), 1.0, 0.0)
    gate = jnp.where(first_hit, gates[0:1, :], 0.0) + jnp.where(other_hit, gates[1:2, :], 0.0)
    slot_gate = jnp.sum(jnp.where(chosen > 0.0, gate, 0.0), axis=1, keepdims=True)
    chosen = chosen.astype(BF16)
    total = jnp.zeros((SLOTS, OWN * HD), F32)
    for other in range(2):
        for y in range(8):
            routed = dot_nn(chosen, rows[y, other])
            half = jnp.where(high == other, 0, 1)
            cols = pl.ds(pl.multiple_of((half * 8 + y) * OWN * HD, HD), OWN * HD)
            total = total + routed * stored[:, cols].astype(F32)
            expert_grad[:, cols] = (slot_gate * routed).astype(BF16)
    gate_grad[...] = jnp.sum(total.T, axis=0, keepdims=True)


def local(
    queries,
    key_rows,
    value_rows,
    out_grad,
    attn_out,
    doc_ids,
    row_grad,
    gate_weights,
    expert_ids,
    expert_out,
):
    pool, spread = call(
        prep_kernel,
        (
            jax.ShapeDtypeStruct((ROWS, 2 * OWN * HD), BF16),
            jax.ShapeDtypeStruct((Z, KB, 2 * HD), BF16),
        ),
        [pltpu.SemaphoreType.DMA((4,))],
        name="prep",
        vmem=None,
        in_specs=[pl.BlockSpec(memory_space=pltpu.HBM)] * 4,
    )(queries, out_grad, key_rows, value_rows)
    plane = lax.all_to_all(spread, "z", split_axis=0, concat_axis=0, tiled=True).reshape(PLANE, 2 * HD)
    pool_y = lax.ppermute(pool, "yl", [(0, 1), (1, 0)])
    row_grad, pool_y = lax.optimization_barrier((row_grad, pool_y))
    pool_c = lax.ppermute(jnp.concatenate([pool, pool_y], axis=0), "c", [(0, 1), (1, 0)])
    plane, pool_c = lax.optimization_barrier((plane, pool_c))
    row_other = lax.ppermute(row_grad, "zh", [(0, 1), (1, 0)])
    row_pair, plane = lax.optimization_barrier((jnp.stack([row_grad, row_other]), plane))
    rows = lax.all_gather(row_pair, ("yh", "yl"), axis=0, tiled=False)

    lone = [((0 * Z + 5) * 2 + 1, (3 * Z + 0) * 2 + 1)]
    ahead2 = lax.ppermute(plane, "x", [(i, i + 2) for i in range(X - 2)])
    ahead1 = lax.ppermute(plane, "x", [(i, i + 1) for i in range(X - 1)])
    aheadx = lax.ppermute(spread[0], ("x", "z", "c"), lone)

    doc = doc_ids.reshape(-1, ROWS)
    shared = (pool, pool_y, pool_c, aheadx, ahead2, ahead1, plane)
    pool_scratch = [
        pltpu.VMEM((HEADS, 2 * ROWS, HD), BF16),
        pltpu.VMEM((HEADS, 2 * ROWS, HD), BF16),
        pltpu.VMEM((PLACES, 2 * HD), BF16),
    ]
    pairs = SPAN * HEADS * 2 * ROWS
    stats = call(
        stats_kernel,
        jax.ShapeDtypeStruct((4, 32, ROWS), F32),
        pool_scratch,
        flops=2 * HD * pairs,
        name="softmax_stats",
    )(*shared, attn_out, doc)
    stats = lax.all_to_all(stats, ("c", "yl"), split_axis=0, concat_axis=0, tiled=True)
    d2, d1, d0, dx, dq_keep, dq_send = call(
        grads_kernel,
        (
            jax.ShapeDtypeStruct((PLANE, 2 * HD), BF16),
            jax.ShapeDtypeStruct((PLANE, 2 * HD), BF16),
            jax.ShapeDtypeStruct((PLANE, 2 * HD), F32),
            jax.ShapeDtypeStruct((KB, 2 * HD), BF16),
            jax.ShapeDtypeStruct((2, OWN * HD, ROWS), F32),
            jax.ShapeDtypeStruct((2, OWN * HD, ROWS), BF16),
        ),
        pool_scratch + [pltpu.VMEM((PLACES, 2 * HD), F32)],
        flops=10 * HD * pairs,
        name="score_grads",
    )(*shared, doc, stats)
    back2 = lax.ppermute(d2, "x", [(i + 2, i) for i in range(X - 2)])
    back1 = lax.ppermute(d1, "x", [(i + 1, i) for i in range(X - 1)])
    backx = lax.ppermute(dx, ("x", "z", "c"), [(b, a) for a, b in lone])
    dq_mine, dq_other = call(
        pool_kernel,
        (jax.ShapeDtypeStruct((OWN * HD, ROWS), F32), jax.ShapeDtypeStruct((OWN * HD, ROWS), BF16)),
        [],
        name="query_pool",
    )(dq_keep, lax.ppermute(dq_send, "c", [(0, 1), (1, 0)]))
    dq_other = lax.ppermute(dq_other, "yl", [(0, 1), (1, 0)])
    plane_sums = call(plane_kernel, jax.ShapeDtypeStruct((2 * Z, KB, HD), BF16), [], name="plane_sum")(
        d0, back1, back2, backx
    )
    parts = lax.all_to_all(plane_sums, ("z", "yl"), split_axis=0, concat_axis=0, tiled=True)

    expert_stored, _ = lax.optimization_barrier((expert_out[0], plane_sums))
    gate_grad, expert_grad = call(
        combine_kernel,
        (
            jax.ShapeDtypeStruct((1, SLOTS), F32),
            jax.ShapeDtypeStruct((SLOTS, expert_out.shape[2]), BF16),
        ),
        [],
        name="combine_grads",
    )(rows, expert_ids.T, gate_weights.T, expert_stored)
    query_grad = call(query_kernel, jax.ShapeDtypeStruct((ROWS, OWN * HD), BF16), [], name="query_sum")(
        dq_mine, dq_other
    )
    parts, expert_grad, query_grad = lax.optimization_barrier((parts, expert_grad, query_grad))
    key_grad, value_grad = call(
        block_kernel,
        (jax.ShapeDtypeStruct((HD // 2, ROWS), BF16), jax.ShapeDtypeStruct((HD // 2, ROWS), BF16)),
        [],
        name="block_sum",
    )(parts)
    return (query_grad, key_grad.T, value_grad.T, gate_grad, expert_grad[None])


def solution(mesh):
    devices = mesh.devices.reshape(X, Z, 2, 2, 4, 2)
    split = Mesh(devices, ("x", "z", "c", "zh", "yh", "yl"))
    ctx, tp = ("x", "z", "c"), ("zh", "yh", "yl")
    in_specs = (
        P(ctx, tp),
        P(ctx, None),
        P(ctx, None),
        P(ctx, tp),
        P(ctx, tp),
        P(),
        P(ctx, tp),
        P(ctx, None),
        P(ctx, None),
        P(ctx, tp, None),
    )
    out_specs = (P(ctx, tp), P(ctx, tp), P(ctx, tp), P(ctx, tp), P(ctx, tp, None))
    return jax.shard_map(local, mesh=split, in_specs=in_specs, out_specs=out_specs, check_vma=False)
```

time: 137 us -> 118 us (0.86)
  the two profiles are of different devices: /device:TPU:1 before, /device:TPU:42 now
where the time goes in v2:
time: 118 us; the launch traced here: 117 us
  starting transfers between devices  54 us (46%)
  waiting for transfers between devices  28.2 us (24%)
  between operations  14.2 us (12%)
  Pallas kernels  11.7 us (10%)
  blocking collectives  5.19 us (4%)
  local copies, waits for them, and re-layouts  2.2 us (2%)
  other arithmetic  1.69 us (1%)
    all_to_all x1, starting transfers between devices, local(): lax.all_to_all(spread, 'z', split_axis=0, concat_axis=0, tiled=True)  12.1 us
    all_to_all x1, starting transfers between devices, local(): lax.all_to_all(plane_sums, ('z', 'yl'), split_axis=0, concat_axis=0, tile...  12 us
    ppermute x1, starting transfers between devices, local(): row_other = lax.ppermute(row_grad, 'zh', [(0, 1), (1, 0)])  10 us
    ppermute x1, waiting for transfers between devices, local(): back2 = lax.ppermute(d2, 'x', [(i + 2, i) for i in range(X - 2)])  6.6 us
    ppermute x1, waiting for transfers between devices, local(): ahead1 = lax.ppermute(plane, 'x', [(i, i + 1) for i in range(X - 1)])  6.14 us
    all_to_all x1, blocking collectives, local(): lax.all_to_all(stats, ('c', 'yl'), split_axis=0, concat_axis=0, tiled=True)  5.19 us
    ppermute x1, waiting for transfers between devices, local(): dq_other = lax.ppermute(dq_other, 'yl', [(0, 1), (1, 0)])  4.94 us
    ppermute x1, waiting for transfers between devices, local(): back1 = lax.ppermute(d1, 'x', [(i + 1, i) for i in range(X - 1)])  4.9 us
  transfers between devices with their start and end apart: 14, of which 7 were waited for; matrix products, arithmetic and copies ran while one was open for 2% of the time, Pallas kernels for 8%

profile of v2, /device:TPU:42, one launch (start us, length us, event | category | flops | bytes accessed | tf_op | source)
XLA Modules:
  0.0 117.2 jit_solution(15965007475141407425)
XLA Ops:
  7.2 1.8 %prep.1 = (bf16[128,768]{1,0:T(8,128)(2,1)}, bf16[6,64,256]{2,1,0:T(8,128)(2,1)}) custom-call(bf16[128,384]{1,0:T(8,128)(2,1)} %queries.1, bf16[128,384]{1,0:T(8,128)(2,1)} %out_grad.1, bf16[128,1024]{1,0:T(8,128)(2,1)} %key_rows.1, bf16[128,1024]{1,0:T(8,128)(2,1)} %value_rows.1), custom_call_target="tpu_custom_call" | custom-call | bytes 1048576 | tf_op jit(solution)/shard_map/prep/pallas_call | solution.py:256
  9.0 3.4 %collective-permute-start = (bf16[128,768]{1,0:T(8,128)(2,1)}, bf16[128,768]{1,0:T(8,128)(2,1)S(1)}, u32[]{:S(2)}, u32[]{:S(2)}) collective-permute-start(bf16[128,768]{1,0:T(8,128)(2,1)} %get-tuple-element.29.qd), channel_id=1, source_target_pairs={{0,1},{1,0},{2,3},{3,2},{4,5},{5,4},{6,7},{7,6},{8,9},{9,8},{10,11... | collective-permute-start | bytes 589832 | tf_op jit(solution)/shard_map/ppermute | solution.py:268
  12.4 12.1 %all-to-all-start = ((bf16[6,64,256]{2,1,0:T(8,128)(2,1)}), bf16[6,64,256]{2,1,0:T(8,128)(2,1)S(1)}, u32[]{:S(2)}, u32[]{:S(2)}) async-start(bf16[6,64,256]{2,1,0:T(8,128)(2,1)} %get-tuple-element.31), calls=%async_computation | async-start | bytes 393216 | tf_op jit(solution)/shard_map/all_to_all | solution.py:267
  24.6 1.0 pad_maximum_fusion
  25.5 1.9 %collective-permute-start.1 = (bf16[256,768]{1,0:T(8,128)(2,1)S(1)}, bf16[256,768]{1,0:T(8,128)(2,1)S(1)}, u32[]{:S(2)}, u32[]{:S(2)}) collective-permute-start(bf16[256,768]{1,0:T(8,128)(2,1)S(1)} %pad_maximum_fusion), channel_id=1, source_target_pairs={{0,16},{16,0},{1,17},{17,1},{2,18},{18,2},{3,19},{19,3},{4,20},{20... | collective-permute-start | bytes 1179656 | tf_op jit(solution)/shard_map/ppermute | solution.py:270
  27.4 10.0 %collective-permute-start.3 = (bf16[128,384]{1,0:T(8,128)(2,1)S(1)}, bf16[128,384]{1,0:T(8,128)(2,1)S(1)}, u32[]{:S(2)}, u32[]{:S(2)}) collective-permute-start(bf16[128,384]{1,0:T(8,128)(2,1)S(1)} %copy-done.7), channel_id=1, source_target_pairs={{0,8},{8,0},{1,9},{9,1},{2,10},{10,2},{3,11},{11,3},{4,12},{12,4},... | collective-permute-start | bytes 294920 | tf_op jit(solution)/shard_map/ppermute | solution.py:272
  37.5 3.5 %collective-permute-done.3 = bf16[128,384]{1,0:T(8,128)(2,1)S(1)} collective-permute-done((bf16[128,384]{1,0:T(8,128)(2,1)S(1)}, bf16[128,384]{1,0:T(8,128)(2,1)S(1)}, u32[]{:S(2)}, u32[]{:S(2)}) %collective-permute-start.3) | collective-permute-done | bytes 98336 | tf_op jit(solution)/shard_map/ppermute | solution.py:272
  41.0 0.7 pad_maximum_fusion.1
  41.8 4.0 %collective-permute-start.4 = (bf16[384,256]{1,0:T(8,128)(2,1)S(1)}, bf16[384,256]{1,0:T(8,128)(2,1)S(1)}, u32[]{:S(2)}, u32[]{:S(2)}) collective-permute-start(bf16[384,256]{1,0:T(8,128)(2,1)S(1)} %bitcast.14), channel_id=1, source_target_pairs={{0,384},{192,576},{1,385},{193,577},{2,386},{194,578},{3,387},{195... | collective-permute-start | bytes 589832 | tf_op jit(solution)/shard_map/ppermute | solution.py:277
  45.9 1.9 %collective-permute-start.5 = (bf16[384,256]{1,0:T(8,128)(2,1)S(1)}, bf16[384,256]{1,0:T(8,128)(2,1)S(1)}, u32[]{:S(2)}, u32[]{:S(2)}) collective-permute-start(bf16[384,256]{1,0:T(8,128)(2,1)S(1)} %bitcast.15), channel_id=1, source_target_pairs={{0,192},{192,384},{384,576},{1,193},{193,385},{385,577},{2,194},{1... | collective-permute-start | bytes 589832 | tf_op jit(solution)/shard_map/ppermute | solution.py:278
  47.8 0.8 slice_bitcast_fusion
  48.5 0.7 collective-permute-start.2
  49.2 0.6 collective-permute-done.4.kv2
  49.9 6.1 %collective-permute-done.5.kv1 = bf16[384,256]{1,0:T(8,128)(2,1)S(1)} collective-permute-done((bf16[384,256]{1,0:T(8,128)(2,1)S(1)}, bf16[384,256]{1,0:T(8,128)(2,1)S(1)}, u32[]{:S(2)}, u32[]{:S(2)}) %collective-permute-start.5) | collective-permute-done | bytes 196640 | tf_op jit(solution)/shard_map/ppermute | solution.py:278
  56.0 2.0 %softmax_stats.1 = f32[4,32,128]{2,1,0:T(8,128)S(1)} custom-call(bf16[128,768]{1,0:T(8,128)(2,1)S(1)} %copy-done.1, bf16[128,768]{1,0:T(8,128)(2,1)S(1)} %collective-permute-done.qd_y, bf16[256,768]{1,0:T(8,128)(2,1)S(1)} %collective-permute-done.1.qd_c, bf16[64,256]{1,0:T(8,128)(2,1)S(1)} %collective-permute-done.2.kvx, ...), custom_call_target="tpu_custom_call" | custom-call | flops 352321536 | bytes 1048576 | tf_op jit(solution)/shard_map/softmax_stats/pallas_call | solution.py:289
  58.0 5.2 %all_to_all.15.stats = f32[4,32,128]{2,1,0:T(8,128)S(1)} all-to-all(f32[4,32,128]{2,1,0:T(8,128)S(1)} %softmax_stats.1), channel_id=1, replica_groups=mesh['x'=4,'z'=6,'c'=2,'zh'=2,'yh'=4,'yl'=2] {'c','yl'}, dimensions={0} | all-to-all | bytes 131072 | tf_op jit(solution)/shard_map/all_to_all | solution.py:296
  63.2 4.2 %score_grads.1 = (bf16[384,256]{1,0:T(8,128)(2,1)S(1)}, bf16[384,256]{1,0:T(8,128)(2,1)S(1)}, f32[384,256]{1,0:T(8,128)S(1)}, bf16[64,256]{1,0:T(8,128)(2,1)S(1)...) custom-call(bf16[128,768]{1,0:T(8,128)(2,1)S(1)} %copy-done.1, ...), custom_call_target="tpu_custom_call" | custom-call | flops 1761607680 | bytes 1048576 | tf_op jit(solution)/shard_map/score_grads/pallas_call | solution.py:297
  67.4 2.1 %collective-permute-start.6 = (bf16[384,256]{1,0:T(8,128)(2,1)S(1)}, bf16[384,256]{1,0:T(8,128)(2,1)S(1)}, u32[]{:S(2)}, u32[]{:S(2)}) collective-permute-start(bf16[384,256]{1,0:T(8,128)(2,1)S(1)} %get-tuple-element.37), channel_id=1, source_target_pairs={{192,0},{384,192},{576,384},{193,1},{385,193},{577,385},{194,2},{3... | collective-permute-start | bytes 589832 | tf_op jit(solution)/shard_map/ppermute | solution.py:312
  69.5 1.3 %collective-permute-start.7 = (bf16[384,256]{1,0:T(8,128)(2,1)S(1)}, bf16[384,256]{1,0:T(8,128)(2,1)S(1)}, u32[]{:S(2)}, u32[]{:S(2)}) collective-permute-start(bf16[384,256]{1,0:T(8,128)(2,1)S(1)} %get-tuple-element.38), channel_id=1, source_target_pairs={{384,0},{576,192},{385,1},{577,193},{386,2},{578,194},{387,3},{579... | collective-permute-start | bytes 589832 | tf_op jit(solution)/shard_map/ppermute | solution.py:311
  70.8 0.7 collective-permute-start.8
  71.5 4.9 %collective-permute-done.6.r1 = bf16[384,256]{1,0:T(8,128)(2,1)S(1)} collective-permute-done((bf16[384,256]{1,0:T(8,128)(2,1)S(1)}, bf16[384,256]{1,0:T(8,128)(2,1)S(1)}, u32[]{:S(2)}, u32[]{:S(2)}) %collective-permute-start.6) | collective-permute-done | bytes 196640 | tf_op jit(solution)/shard_map/ppermute | solution.py:312
  76.4 6.6 %collective-permute-done.7.r2 = bf16[384,256]{1,0:T(8,128)(2,1)S(1)} collective-permute-done((bf16[384,256]{1,0:T(8,128)(2,1)S(1)}, bf16[384,256]{1,0:T(8,128)(2,1)S(1)}, u32[]{:S(2)}, u32[]{:S(2)}) %collective-permute-start.7) | collective-permute-done | bytes 196640 | tf_op jit(solution)/shard_map/ppermute | solution.py:311
  83.0 0.7 plane_sum.1
  83.7 12.0 %all-to-all-start.2 = ((bf16[12,64,128]{2,1,0:T(8,128)(2,1)}), bf16[12,64,128]{2,1,0:T(8,128)(2,1)S(1)}, u32[]{:S(2)}, u32[]{:S(2)}) async-start(bf16[12,64,128]{2,1,0:T(8,128)(2,1)} %plane_sum.1), calls=%async_computation.2 | async-start | bytes 393216 | tf_op jit(solution)/shard_map/all_to_all | solution.py:324
  95.7 1.9 %collective-permute-start.9 = (bf16[2,384,128]{2,1,0:T(8,128)(2,1)S(1)}, bf16[2,384,128]{2,1,0:T(8,128)(2,1)S(1)}, u32[]{:S(2)}, u32[]{:S(2)}) collective-permute-start(bf16[2,384,128]{2,1,0:T(8,128)(2,1)S(1)} %get-tuple-element.44), channel_id=1, source_target_pairs={{0,16},{16,0},{1,17},{17,1},{2,18},{18,2},{3,19},{19,3},{4,20},{20... | collective-permute-start | bytes 589832 | tf_op jit(solution)/shard_map/ppermute | solution.py:319
  97.7 1.4 %collective-permute-done.9.arrived = bf16[2,384,128]{2,1,0:T(8,128)(2,1)S(1)} collective-permute-done((bf16[2,384,128]{2,1,0:T(8,128)(2,1)S(1)}, bf16[2,384,128]{2,1,0:T(8,128)(2,1)S(1)}, u32[]{:S(2)}, u32[]{:S(2)}) %collective-permute-start.9) | collective-permute-done | bytes 196640 | tf_op jit(solution)/shard_map/ppermute | solution.py:319
  99.1 2.0 %collective-permute-start.10 = (bf16[384,128]{1,0:T(8,128)(2,1)S(1)}, bf16[384,128]{1,0:T(8,128)(2,1)S(1)}, u32[]{:S(2)}, u32[]{:S(2)}) collective-permute-start(bf16[384,128]{1,0:T(8,128)(2,1)S(1)} %get-tuple-element.46), channel_id=1, source_target_pairs={{0,1},{1,0},{2,3},{3,2},{4,5},{5,4},{6,7},{7,6},{8,9},{9,8},{10,11... | collective-permute-start | bytes 294920 | tf_op jit(solution)/shard_map/ppermute | solution.py:320
  101.1 4.9 %collective-permute-done.10.arrived = bf16[384,128]{1,0:T(8,128)(2,1)S(1)} collective-permute-done((bf16[384,128]{1,0:T(8,128)(2,1)S(1)}, bf16[384,128]{1,0:T(8,128)(2,1)S(1)}, u32[]{:S(2)}, u32[]{:S(2)}) %collective-permute-start.10) | collective-permute-done | bytes 98336 | tf_op jit(solution)/shard_map/ppermute | solution.py:320
  106.0 0.7 query_sum.1
  106.8 1.4 %copy-done = bf16[16,128,384]{2,1,0:T(8,128)(2,1)S(1)} copy-done((bf16[16,128,384]{2,1,0:T(8,128)(2,1)S(1)}, bf16[16,128,384]{2,1,0:T(8,128)(2,1)}, u32[]{:S(2)}) %copy-start) | copy-done | bytes 1572888
  108.2 1.4 %combine_grads.1 = (f32[1,32]{1,0:T(1,128)}, bf16[32,6144]{1,0:T(8,128)(2,1)}) custom-call(bf16[8,2,128,384]{3,2,1,0:T(8,128)(2,1)S(1)} %bitcast.13, s32[2,128]{1,0:T(2,128)S(1)} %bitcast.21, f32[2,128]{1,0:T(2,128)S(1)} %bitcast.22, bf16[32,6144]{1,0:T(8,128)(2,1)S(1)} %bitcast.18), custom_call_target="tpu_custom_call" | custom-call | bytes 1048576 | tf_op jit(solution)/shard_map/combine_grads/pallas_call | solution.py:327
  109.6 0.7 block_sum.1
  (25 shorter events, 0.1 us)
Async XLA Ops:
  7.2 20.3 %copy-start.7 = (bf16[128,384]{1,0:T(8,128)(2,1)S(1)}, bf16[128,384]{1,0:T(8,128)(2,1)}, u32[]{:S(2)}) copy-start(bf16[128,384]{1,0:T(8,128)(2,1)} %param.16) | copy-start | bytes 294916
  7.2 48.8 %copy-start.4 = (s32[6144]{0:T(1024)S(1)}, s32[6144]{0:T(1024)}, u32[]{:S(2)}) copy-start(s32[6144]{0:T(1024)} %param.15) | copy-start | bytes 73732
  7.2 48.8 %copy-start.3 = (bf16[128,384]{1,0:T(8,128)(2,1)S(1)}, bf16[128,384]{1,0:T(8,128)(2,1)}, u32[]{:S(2)}) copy-start(bf16[128,384]{1,0:T(8,128)(2,1)} %o_own.1) | copy-start | bytes 294916
  9.0 47.0 %copy-start.1 = (bf16[128,768]{1,0:T(8,128)(2,1)S(1)}, bf16[128,768]{1,0:T(8,128)(2,1)}, u32[]{:S(2)}) copy-start(bf16[128,768]{1,0:T(8,128)(2,1)} %get-tuple-element.29.qd) | copy-start | bytes 589828
  9.0 15.5 %collective-permute-start = (bf16[128,768]{1,0:T(8,128)(2,1)}, bf16[128,768]{1,0:T(8,128)(2,1)S(1)}, u32[]{:S(2)}, u32[]{:S(2)}) collective-permute-start(bf16[128,768]{1,0:T(8,128)(2,1)} %get-tuple-element.29.qd), channel_id=1, source_target_pairs={{0,1},{1,0},{2,3},{3,2},{4,5},{5,4},{6,7},{7,6},{8,9},{9,8},{10,11... | collective-permute-start | bytes 589832 | tf_op jit(solution)/shard_map/ppermute | solution.py:268
  12.4 29.3 %all-to-all-start = ((bf16[6,64,256]{2,1,0:T(8,128)(2,1)}), bf16[6,64,256]{2,1,0:T(8,128)(2,1)S(1)}, u32[]{:S(2)}, u32[]{:S(2)}) async-start(bf16[6,64,256]{2,1,0:T(8,128)(2,1)} %get-tuple-element.31), calls=%async_computation | async-start | bytes 393216 | tf_op jit(solution)/shard_map/all_to_all | solution.py:267
  24.5 82.2 %all-gather.3.cloned.1.call-start = ((), (), s32[]{:S(2)}) async-start(), calls=%async_computation.3 | async-start | bytes 1769472 | tf_op jit(solution)/shard_map/all_gather | solution.py:274
  25.5 16.3 %collective-permute-start.1 = (bf16[256,768]{1,0:T(8,128)(2,1)S(1)}, bf16[256,768]{1,0:T(8,128)(2,1)S(1)}, u32[]{:S(2)}, u32[]{:S(2)}) collective-permute-start(bf16[256,768]{1,0:T(8,128)(2,1)S(1)} %pad_maximum_fusion), channel_id=1, source_target_pairs={{0,16},{16,0},{1,17},{17,1},{2,18},{18,2},{3,19},{19,3},{4,20},{20... | collective-permute-start | bytes 1179656 | tf_op jit(solution)/shard_map/ppermute | solution.py:270
  27.4 13.6 %collective-permute-start.3 = (bf16[128,384]{1,0:T(8,128)(2,1)S(1)}, bf16[128,384]{1,0:T(8,128)(2,1)S(1)}, u32[]{:S(2)}, u32[]{:S(2)}) collective-permute-start(bf16[128,384]{1,0:T(8,128)(2,1)S(1)} %copy-done.7), channel_id=1, source_target_pairs={{0,8},{8,0},{1,9},{9,1},{2,10},{10,2},{3,11},{11,3},{4,12},{12,4},... | collective-permute-start | bytes 294920 | tf_op jit(solution)/shard_map/ppermute | solution.py:272
  41.8 8.1 %collective-permute-start.4 = (bf16[384,256]{1,0:T(8,128)(2,1)S(1)}, bf16[384,256]{1,0:T(8,128)(2,1)S(1)}, u32[]{:S(2)}, u32[]{:S(2)}) collective-permute-start(bf16[384,256]{1,0:T(8,128)(2,1)S(1)} %bitcast.14), channel_id=1, source_target_pairs={{0,384},{192,576},{1,385},{193,577},{2,386},{194,578},{3,387},{195... | collective-permute-start | bytes 589832 | tf_op jit(solution)/shard_map/ppermute | solution.py:277
  45.9 10.2 %collective-permute-start.5 = (bf16[384,256]{1,0:T(8,128)(2,1)S(1)}, bf16[384,256]{1,0:T(8,128)(2,1)S(1)}, u32[]{:S(2)}, u32[]{:S(2)}) collective-permute-start(bf16[384,256]{1,0:T(8,128)(2,1)S(1)} %bitcast.15), channel_id=1, source_target_pairs={{0,192},{192,384},{384,576},{1,193},{193,385},{385,577},{2,194},{1... | collective-permute-start | bytes 589832 | tf_op jit(solution)/shard_map/ppermute | solution.py:278
  48.5 0.7 collective-permute-start.2
  67.4 39.4 %copy-start.2 = (bf16[1,32,6144]{2,1,0:T(8,128)(2,1)S(1)}, bf16[1,32,6144]{2,1,0:T(8,128)(2,1)}, u32[]{:S(2)}) copy-start(bf16[1,32,6144]{2,1,0:T(8,128)(2,1)} %param.19) | copy-start | bytes 1179652
  67.4 39.4 %copy-start.5 = (s32[128,2]{0,1:T(2,128)S(1)}, s32[128,2]{0,1:T(2,128)}, u32[]{:S(2)}) copy-start(s32[128,2]{0,1:T(2,128)} %param.18) | copy-start | bytes 3076
  67.4 39.4 %copy-start.6 = (f32[128,2]{0,1:T(2,128)S(1)}, f32[128,2]{0,1:T(2,128)}, u32[]{:S(2)}) copy-start(f32[128,2]{0,1:T(2,128)} %param.17) | copy-start | bytes 3076
  67.4 8.9 %collective-permute-start.6 = (bf16[384,256]{1,0:T(8,128)(2,1)S(1)}, bf16[384,256]{1,0:T(8,128)(2,1)S(1)}, u32[]{:S(2)}, u32[]{:S(2)}) collective-permute-start(bf16[384,256]{1,0:T(8,128)(2,1)S(1)} %get-tuple-element.37), channel_id=1, source_target_pairs={{192,0},{384,192},{576,384},{193,1},{385,193},{577,385},{194,2},{3... | collective-permute-start | bytes 589832 | tf_op jit(solution)/shard_map/ppermute | solution.py:312
  69.5 13.5 %collective-permute-start.7 = (bf16[384,256]{1,0:T(8,128)(2,1)S(1)}, bf16[384,256]{1,0:T(8,128)(2,1)S(1)}, u32[]{:S(2)}, u32[]{:S(2)}) collective-permute-start(bf16[384,256]{1,0:T(8,128)(2,1)S(1)} %get-tuple-element.38), channel_id=1, source_target_pairs={{384,0},{576,192},{385,1},{577,193},{386,2},{578,194},{387,3},{579... | collective-permute-start | bytes 589832 | tf_op jit(solution)/shard_map/ppermute | solution.py:311
  70.8 0.7 collective-permute-start.8
  83.7 25.9 %all-to-all-start.2 = ((bf16[12,64,128]{2,1,0:T(8,128)(2,1)}), bf16[12,64,128]{2,1,0:T(8,128)(2,1)S(1)}, u32[]{:S(2)}, u32[]{:S(2)}) async-start(bf16[12,64,128]{2,1,0:T(8,128)(2,1)} %plane_sum.1), calls=%async_computation.2 | async-start | bytes 393216 | tf_op jit(solution)/shard_map/all_to_all | solution.py:324
  95.7 3.3 %collective-permute-start.9 = (bf16[2,384,128]{2,1,0:T(8,128)(2,1)S(1)}, bf16[2,384,128]{2,1,0:T(8,128)(2,1)S(1)}, u32[]{:S(2)}, u32[]{:S(2)}) collective-permute-start(bf16[2,384,128]{2,1,0:T(8,128)(2,1)S(1)} %get-tuple-element.44), channel_id=1, source_target_pairs={{0,16},{16,0},{1,17},{17,1},{2,18},{18,2},{3,19},{19,3},{4,20},{20... | collective-permute-start | bytes 589832 | tf_op jit(solution)/shard_map/ppermute | solution.py:319
  99.1 6.9 %collective-permute-start.10 = (bf16[384,128]{1,0:T(8,128)(2,1)S(1)}, bf16[384,128]{1,0:T(8,128)(2,1)S(1)}, u32[]{:S(2)}, u32[]{:S(2)}) collective-permute-start(bf16[384,128]{1,0:T(8,128)(2,1)S(1)} %get-tuple-element.46), channel_id=1, source_target_pairs={{0,1},{1,0},{2,3},{3,2},{4,5},{5,4},{6,7},{7,6},{8,9},{9,8},{10,11... | collective-permute-start | bytes 294920 | tf_op jit(solution)/shard_map/ppermute | solution.py:320
  106.8 1.4 %copy-start = (bf16[16,128,384]{2,1,0:T(8,128)(2,1)S(1)}, bf16[16,128,384]{2,1,0:T(8,128)(2,1)}, u32[]{:S(2)}) copy-start(bf16[16,128,384]{2,1,0:T(8,128)(2,1)} %all-gather.3.cloned.1.call-done) | copy-start | bytes 4718596
Sparse Core Ops, SparseCore 0:
  41.9 47.3 all-gather.2

commit v3 on v2

--- a/solution.py
+++ b/solution.py
@@ -214,11 +214,7 @@
         query_grad[:, rows] = (mine[rows, :] + arrived[rows, :].astype(F32)).T.astype(BF16)
 
 
-def combine_kernel(rows, ids, gates, stored, gate_grad, expert_grad):
-    y = lax.axis_index("yh") * 2 + lax.axis_index("yl")
-    high = lax.axis_index("zh")
-    place_in_tp = high * 8 + y
-    expert, second = place_in_tp // 2, place_in_tp % 2
+def choice(ids, expert, second):
     first_hit, other_hit = ids[0:1, :] == expert, ids[1:2, :] == expert
     hit = jnp.where(first_hit | other_hit, 1.0, 0.0)
     earlier = lax.broadcasted_iota(jnp.int32, (ROWS, ROWS), 0) < lax.broadcasted_iota(jnp.int32, (ROWS, ROWS), 1)
@@ -226,16 +222,29 @@
         jnp.broadcast_to(hit, (16, ROWS)).astype(BF16), jnp.where(earlier, 1.0, 0.0).astype(BF16)
     )[0:1, :].astype(jnp.int32)
     slot = second * SLOTS + lax.broadcasted_iota(jnp.int32, (SLOTS, ROWS), 0)
-    chosen = jnp.where((slot == rank) & (hit > 0.0), 1.0, 0.0)
+    return (slot == rank) & (hit > 0.0), first_hit, other_hit
+
+
+def select_kernel(mine, other, ids, out):
+    high = lax.axis_index("zh")
+    for pair in range(4):
+        for second in range(2):
+            chosen, _, _ = choice(ids, high * 4 + pair, second)
+            chosen = jnp.where(chosen, 1.0, 0.0).astype(BF16)
+            out[2 * pair + second, high] = dot_nn(chosen, mine[...]).astype(BF16)
+            out[2 * pair + second, 1 - high] = dot_nn(chosen, other[...]).astype(BF16)
+
+
+def combine_kernel(rows, ids, gates, stored, gate_grad, expert_grad):
+    place_in_tp = lax.axis_index("zh") * 8 + lax.axis_index("yh") * 2 + lax.axis_index("yl")
+    chosen, first_hit, other_hit = choice(ids, place_in_tp // 2, place_in_tp % 2)
     gate = jnp.where(first_hit, gates[0:1, :], 0.0) + jnp.where(other_hit, gates[1:2, :], 0.0)
-    slot_gate = jnp.sum(jnp.where(chosen > 0.0, gate, 0.0), axis=1, keepdims=True)
-    chosen = chosen.astype(BF16)
+    slot_gate = jnp.sum(jnp.where(chosen, gate, 0.0), axis=1, keepdims=True)
     total = jnp.zeros((SLOTS, OWN * HD), F32)
-    for other in range(2):
+    for high in range(2):
         for y in range(8):
-            routed = dot_nn(chosen, rows[y, other])
-            half = jnp.where(high == other, 0, 1)
-            cols = pl.ds(pl.multiple_of((half * 8 + y) * OWN * HD, HD), OWN * HD)
+            routed = rows[y, high].astype(F32)
+            cols = slice((high * 8 + y) * OWN * HD, (high * 8 + y + 1) * OWN * HD)
             total = total + routed * stored[:, cols].astype(F32)
             expert_grad[:, cols] = (slot_gate * routed).astype(BF16)
     gate_grad[...] = jnp.sum(total.T, axis=0, keepdims=True)
@@ -266,12 +275,18 @@
     )(queries, out_grad, key_rows, value_rows)
     plane = lax.all_to_all(spread, "z", split_axis=0, concat_axis=0, tiled=True).reshape(PLANE, 2 * HD)
     pool_y = lax.ppermute(pool, "yl", [(0, 1), (1, 0)])
-    row_grad, pool_y = lax.optimization_barrier((row_grad, pool_y))
     pool_c = lax.ppermute(jnp.concatenate([pool, pool_y], axis=0), "c", [(0, 1), (1, 0)])
     plane, pool_c = lax.optimization_barrier((plane, pool_c))
     row_other = lax.ppermute(row_grad, "zh", [(0, 1), (1, 0)])
-    row_pair, plane = lax.optimization_barrier((jnp.stack([row_grad, row_other]), plane))
-    rows = lax.all_gather(row_pair, ("yh", "yl"), axis=0, tiled=False)
+    ids = expert_ids.T
+    chosen_rows = call(
+        select_kernel,
+        jax.ShapeDtypeStruct((8, 2, SLOTS, OWN * HD), BF16),
+        [],
+        flops=2 * 256 * ROWS * 2 * OWN * HD,
+        name="select_rows",
+    )(row_grad, row_other, ids)
+    rows = lax.all_to_all(chosen_rows, ("yh", "yl"), split_axis=0, concat_axis=0, tiled=True)
 
     lone = [((0 * Z + 5) * 2 + 1, (3 * Z + 0) * 2 + 1)]
     ahead2 = lax.ppermute(plane, "x", [(i, i + 2) for i in range(X - 2)])
@@ -317,13 +332,13 @@
         [],
         name="query_pool",
     )(dq_keep, lax.ppermute(dq_send, "c", [(0, 1), (1, 0)]))
+    back1, dq_other = lax.optimization_barrier((back1, dq_other))
     dq_other = lax.ppermute(dq_other, "yl", [(0, 1), (1, 0)])
     plane_sums = call(plane_kernel, jax.ShapeDtypeStruct((2 * Z, KB, HD), BF16), [], name="plane_sum")(
         d0, back1, back2, backx
     )
     parts = lax.all_to_all(plane_sums, ("z", "yl"), split_axis=0, concat_axis=0, tiled=True)
 
-    expert_stored, _ = lax.optimization_barrier((expert_out[0], plane_sums))
     gate_grad, expert_grad = call(
         combine_kernel,
         (
@@ -332,7 +347,7 @@
         ),
         [],
         name="combine_grads",
-    )(rows, expert_ids.T, gate_weights.T, expert_stored)
+    )(rows, ids, gate_weights.T, expert_out[0])
     query_grad = call(query_kernel, jax.ShapeDtypeStruct((ROWS, OWN * HD), BF16), [], name="query_sum")(
         dq_mine, dq_other
     )

time: 118 us -> 105 us (0.89)
  the two profiles are of different devices: /device:TPU:42 before, /device:TPU:1 now
where the time goes in v3:
time: 105 us; the launch traced here: 104 us
  starting transfers between devices  67 us (64%)
  waiting for transfers between devices  20.1 us (19%)
  Pallas kernels  13.9 us (13%)
  local copies, waits for them, and re-layouts  2.12 us (2%)
    all_to_all x1, starting transfers between devices, local(): lax.all_to_all(spread, 'z', split_axis=0, concat_axis=0, tiled=True)  12 us
    ppermute x1, starting transfers between devices, local(): row_other = lax.ppermute(row_grad, 'zh', [(0, 1), (1, 0)])  9.81 us
    all_to_all x1, starting transfers between devices, local(): lax.all_to_all(plane_sums, ('z', 'yl'), split_axis=0, concat_axis=0, tile...  7.94 us
    all_to_all x1, waiting for transfers between devices, local(): lax.all_to_all(spread, 'z', split_axis=0, concat_axis=0, tiled=True)  6.71 us
    all_to_all x1, starting transfers between devices, local(): lax.all_to_all(chosen_rows, ('yh', 'yl'), split_axis=0, concat_axis=0, ti...  5.92 us
    all_to_all x1, starting transfers between devices, local(): lax.all_to_all(stats, ('c', 'yl'), split_axis=0, concat_axis=0, tiled=True)  5.8 us
    ppermute x1, waiting for transfers between devices, local(): back1 = lax.ppermute(d1, 'x', [(i + 1, i) for i in range(X - 1)])  5.08 us
    ppermute x1, starting transfers between devices, local(): ahead2 = lax.ppermute(plane, 'x', [(i, i + 2) for i in range(X - 2)])  4.78 us
  transfers between devices with their start and end apart: 15, of which 6 were waited for; matrix products, arithmetic and copies ran while one was open for 1% of the time, Pallas kernels for 11%

profile of v3, /device:TPU:1, one launch (start us, length us, event | category | flops | bytes accessed | tf_op | source)
XLA Modules:
  0.0 104.0 jit_solution(3847133469818849409)
XLA Ops:
  0.6 1.8 %prep.1 = (bf16[128,768]{1,0:T(8,128)(2,1)}, bf16[6,64,256]{2,1,0:T(8,128)(2,1)}) custom-call(bf16[128,384]{1,0:T(8,128)(2,1)} %queries.1, bf16[128,384]{1,0:T(8,128)(2,1)} %out_grad.1, bf16[128,1024]{1,0:T(8,128)(2,1)} %key_rows.1, bf16[128,1024]{1,0:T(8,128)(2,1)} %value_rows.1), custom_call_target="tpu_custom_call" | custom-call | bytes 1048576 | tf_op jit(solution)/shard_map/prep/pallas_call | solution.py:265
  2.4 4.0 %collective-permute-start = (bf16[128,768]{1,0:T(8,128)(2,1)}, bf16[128,768]{1,0:T(8,128)(2,1)S(1)}, u32[]{:S(2)}, u32[]{:S(2)}) collective-permute-start(bf16[128,768]{1,0:T(8,128)(2,1)} %get-tuple-element.26.qd), channel_id=1, source_target_pairs={{0,1},{1,0},{2,3},{3,2},{4,5},{5,4},{6,7},{7,6},{8,9},{9,8},{10,11... | collective-permute-start | bytes 589832 | tf_op jit(solution)/shard_map/ppermute | solution.py:277
  6.5 12.0 %all-to-all-start = ((bf16[6,64,256]{2,1,0:T(8,128)(2,1)}), bf16[6,64,256]{2,1,0:T(8,128)(2,1)S(1)}, u32[]{:S(2)}, u32[]{:S(2)}) async-start(bf16[6,64,256]{2,1,0:T(8,128)(2,1)} %get-tuple-element.27), calls=%async_computation | async-start | bytes 393216 | tf_op jit(solution)/shard_map/all_to_all | solution.py:276
  18.5 4.3 %collective-permute-start.1 = (bf16[256,768]{1,0:T(8,128)(2,1)S(1)}, bf16[256,768]{1,0:T(8,128)(2,1)S(1)}, u32[]{:S(2)}, u32[]{:S(2)}) collective-permute-start(bf16[256,768]{1,0:T(8,128)(2,1)S(1)} %pad_maximum_fusion), channel_id=1, source_target_pairs={{0,16},{16,0},{1,17},{17,1},{2,18},{18,2},{3,19},{19,3},{4,20},{20... | collective-permute-start | bytes 1179656 | tf_op jit(solution)/shard_map/ppermute | solution.py:278
  22.8 6.7 %all-to-all-done = bf16[6,64,256]{2,1,0:T(8,128)(2,1)S(1)} async-done(((bf16[6,64,256]{2,1,0:T(8,128)(2,1)}), bf16[6,64,256]{2,1,0:T(8,128)(2,1)S(1)}, u32[]{:S(2)}, u32[]{:S(2)}) %all-to-all-start) | async-done | bytes 196640 | tf_op jit(solution)/shard_map/all_to_all | solution.py:276
  29.5 4.8 %collective-permute-start.3 = (bf16[384,256]{1,0:T(8,128)(2,1)S(1)}, bf16[384,256]{1,0:T(8,128)(2,1)S(1)}, u32[]{:S(2)}, u32[]{:S(2)}) collective-permute-start(bf16[384,256]{1,0:T(8,128)(2,1)S(1)} %bitcast.10), channel_id=1, source_target_pairs={{0,384},{192,576},{1,385},{193,577},{2,386},{194,578},{3,387},{195... | collective-permute-start | bytes 589832 | tf_op jit(solution)/shard_map/ppermute | solution.py:292
  34.3 2.2 %collective-permute-start.4 = (bf16[384,256]{1,0:T(8,128)(2,1)S(1)}, bf16[384,256]{1,0:T(8,128)(2,1)S(1)}, u32[]{:S(2)}, u32[]{:S(2)}) collective-permute-start(bf16[384,256]{1,0:T(8,128)(2,1)S(1)} %bitcast.11), channel_id=1, source_target_pairs={{0,192},{192,384},{384,576},{1,193},{193,385},{385,577},{2,194},{1... | collective-permute-start | bytes 589832 | tf_op jit(solution)/shard_map/ppermute | solution.py:293
  36.5 0.8 slice_bitcast_fusion
  37.3 0.7 collective-permute-start.2
  38.0 9.8 %collective-permute-start.9 = (bf16[128,384]{1,0:T(8,128)(2,1)S(1)}, bf16[128,384]{1,0:T(8,128)(2,1)S(1)}, u32[]{:S(2)}, u32[]{:S(2)}) collective-permute-start(bf16[128,384]{1,0:T(8,128)(2,1)S(1)} %copy-done.3), channel_id=1, source_target_pairs={{0,8},{8,0},{1,9},{9,1},{2,10},{10,2},{3,11},{11,3},{4,12},{12,4},... | collective-permute-start | bytes 294920 | tf_op jit(solution)/shard_map/ppermute | solution.py:280
  47.8 2.6 %softmax_stats.1 = f32[4,32,128]{2,1,0:T(8,128)} custom-call(bf16[128,768]{1,0:T(8,128)(2,1)S(1)} %copy-done, bf16[128,768]{1,0:T(8,128)(2,1)S(1)} %collective-permute-done.qd_y, bf16[256,768]{1,0:T(8,128)(2,1)S(1)} %collective-permute-done.1.qd_c, bf16[64,256]{1,0:T(8,128)(2,1)S(1)} %collective-permute-done.2.kvx, ...), custom_call_target="tpu_custom_call" | custom-call | flops 352321536 | bytes 1048576 | tf_op jit(solution)/shard_map/softmax_stats/pallas_call | solution.py:304
  50.4 5.8 %all-to-all-start.1 = ((f32[4,32,128]{2,1,0:T(8,128)}), f32[4,32,128]{2,1,0:T(8,128)S(1)}, u32[]{:S(2)}, u32[]{:S(2)}) async-start(f32[4,32,128]{2,1,0:T(8,128)} %softmax_stats.1), calls=%async_computation.1 | async-start | bytes 131072 | tf_op jit(solution)/shard_map/all_to_all | solution.py:311
  56.2 0.7 copy-done.5
  56.9 2.1 %select_rows.1 = bf16[8,2,32,384]{3,2,1,0:T(8,128)(2,1)} custom-call(bf16[128,384]{1,0:T(8,128)(2,1)S(1)} %copy-done.3, bf16[128,384]{1,0:T(8,128)(2,1)S(1)} %collective-permute-done.9.other, s32[2,128]{1,0:T(2,128)S(1)} %bitcast.17), custom_call_target="tpu_custom_call" | custom-call | flops 50331648 | bytes 1048576 | tf_op jit(solution)/shard_map/select_rows/pallas_call | solution.py:282
  58.9 0.5 all-to-all-done.1.stats
  59.4 5.9 %all-to-all-start.3 = ((bf16[8,2,32,384]{3,2,1,0:T(8,128)(2,1)}), bf16[8,2,32,384]{3,2,1,0:T(8,128)(2,1)S(1)}, u32[]{:S(2)}, u32[]{:S(2)}) async-start(bf16[8,2,32,384]{3,2,1,0:T(8,128)(2,1)} %select_rows.1), calls=%async_computation.3 | async-start | bytes 786432 | tf_op jit(solution)/shard_map/all_to_all | solution.py:289
  65.4 4.2 %score_grads.1 = (bf16[384,256]{1,0:T(8,128)(2,1)S(1)}, bf16[384,256]{1,0:T(8,128)(2,1)S(1)}, f32[384,256]{1,0:T(8,128)S(1)}, bf16[64,256]{1,0:T(8,128)(2,1)S(1)...) custom-call(bf16[128,768]{1,0:T(8,128)(2,1)S(1)} %copy-done, ...), custom_call_target="tpu_custom_call" | custom-call | flops 1761607680 | bytes 1048576 | tf_op jit(solution)/shard_map/score_grads/pallas_call | solution.py:312
  69.5 3.1 %collective-permute-start.6 = (bf16[2,384,128]{2,1,0:T(8,128)(2,1)S(1)}, bf16[2,384,128]{2,1,0:T(8,128)(2,1)S(1)}, u32[]{:S(2)}, u32[]{:S(2)}) collective-permute-start(bf16[2,384,128]{2,1,0:T(8,128)(2,1)S(1)} %get-tuple-element.33), channel_id=1, source_target_pairs={{0,16},{16,0},{1,17},{17,1},{2,18},{18,2},{3,19},{19,3},{4,20},{20... | collective-permute-start | bytes 589832 | tf_op jit(solution)/shard_map/ppermute | solution.py:334
  72.6 1.3 %collective-permute-start.5 = (bf16[384,256]{1,0:T(8,128)(2,1)S(1)}, bf16[384,256]{1,0:T(8,128)(2,1)S(1)}, u32[]{:S(2)}, u32[]{:S(2)}) collective-permute-start(bf16[384,256]{1,0:T(8,128)(2,1)S(1)} %get-tuple-element.31), channel_id=1, source_target_pairs={{192,0},{384,192},{576,384},{193,1},{385,193},{577,385},{194,2},{3... | collective-permute-start | bytes 589832 | tf_op jit(solution)/shard_map/ppermute | solution.py:327
  73.9 1.3 %collective-permute-start.7 = (bf16[384,256]{1,0:T(8,128)(2,1)S(1)}, bf16[384,256]{1,0:T(8,128)(2,1)S(1)}, u32[]{:S(2)}, u32[]{:S(2)}) collective-permute-start(bf16[384,256]{1,0:T(8,128)(2,1)S(1)} %get-tuple-element.36), channel_id=1, source_target_pairs={{384,0},{576,192},{385,1},{577,193},{386,2},{578,194},{387,3},{579... | collective-permute-start | bytes 589832 | tf_op jit(solution)/shard_map/ppermute | solution.py:326
  75.2 0.7 collective-permute-start.8
  75.9 5.1 %collective-permute-done.5.r1 = bf16[384,256]{1,0:T(8,128)(2,1)S(1)} collective-permute-done((bf16[384,256]{1,0:T(8,128)(2,1)S(1)}, bf16[384,256]{1,0:T(8,128)(2,1)S(1)}, u32[]{:S(2)}, u32[]{:S(2)}) %collective-permute-start.5) | collective-permute-done | bytes 196640 | tf_op jit(solution)/shard_map/ppermute | solution.py:327
  81.0 2.8 %collective-permute-done.7.r2 = bf16[384,256]{1,0:T(8,128)(2,1)S(1)} collective-permute-done((bf16[384,256]{1,0:T(8,128)(2,1)S(1)}, bf16[384,256]{1,0:T(8,128)(2,1)S(1)}, u32[]{:S(2)}, u32[]{:S(2)}) %collective-permute-start.7) | collective-permute-done | bytes 196640 | tf_op jit(solution)/shard_map/ppermute | solution.py:326
  83.8 0.8 plane_sum.1
  84.6 7.9 %all-to-all-start.2 = ((bf16[12,64,128]{2,1,0:T(8,128)(2,1)}), bf16[12,64,128]{2,1,0:T(8,128)(2,1)S(1)}, u32[]{:S(2)}, u32[]{:S(2)}) async-start(bf16[12,64,128]{2,1,0:T(8,128)(2,1)} %plane_sum.1), calls=%async_computation.2 | async-start | bytes 393216 | tf_op jit(solution)/shard_map/all_to_all | solution.py:340
  92.5 3.3 %collective-permute-start.10 = (bf16[384,128]{1,0:T(8,128)(2,1)S(1)}, bf16[384,128]{1,0:T(8,128)(2,1)S(1)}, u32[]{:S(2)}, u32[]{:S(2)}) collective-permute-start(bf16[384,128]{1,0:T(8,128)(2,1)S(1)} %get-tuple-element.40), channel_id=1, source_target_pairs={{0,1},{1,0},{2,3},{3,2},{4,5},{5,4},{6,7},{7,6},{8,9},{9,8},{10,11... | collective-permute-start | bytes 294920 | tf_op jit(solution)/shard_map/ppermute | solution.py:336
  95.9 0.7 copy-done.6
  96.6 1.0 combine_grads.1
  97.6 0.9 collective-permute-done.10.arrived
  98.5 0.7 query_sum.1
  99.2 4.1 %all-to-all-done.2.parts = bf16[12,64,128]{2,1,0:T(8,128)(2,1)S(1)} async-done(((bf16[12,64,128]{2,1,0:T(8,128)(2,1)}), bf16[12,64,128]{2,1,0:T(8,128)(2,1)S(1)}, u32[]{:S(2)}, u32[]{:S(2)}) %all-to-all-start.2) | async-done | bytes 196640 | tf_op jit(solution)/shard_map/all_to_all | solution.py:340
  103.3 0.7 block_sum.1
  (23 shorter events, 0.1 us)
Async XLA Ops:
  2.4 16.0 %collective-permute-start = (bf16[128,768]{1,0:T(8,128)(2,1)}, bf16[128,768]{1,0:T(8,128)(2,1)S(1)}, u32[]{:S(2)}, u32[]{:S(2)}) collective-permute-start(bf16[128,768]{1,0:T(8,128)(2,1)} %get-tuple-element.26.qd), channel_id=1, source_target_pairs={{0,1},{1,0},{2,3},{3,2},{4,5},{5,4},{6,7},{7,6},{8,9},{9,8},{10,11... | collective-permute-start | bytes 589832 | tf_op jit(solution)/shard_map/ppermute | solution.py:277
  6.5 12.0 %copy-start = (bf16[128,768]{1,0:T(8,128)(2,1)S(1)}, bf16[128,768]{1,0:T(8,128)(2,1)}, u32[]{:S(2)}) copy-start(bf16[128,768]{1,0:T(8,128)(2,1)} %get-tuple-element.26.qd) | copy-start | bytes 589828
  6.5 23.0 %all-to-all-start = ((bf16[6,64,256]{2,1,0:T(8,128)(2,1)}), bf16[6,64,256]{2,1,0:T(8,128)(2,1)S(1)}, u32[]{:S(2)}, u32[]{:S(2)}) async-start(bf16[6,64,256]{2,1,0:T(8,128)(2,1)} %get-tuple-element.27), calls=%async_computation | async-start | bytes 393216 | tf_op jit(solution)/shard_map/all_to_all | solution.py:276
  18.4 19.5 %copy-start.3 = (bf16[128,384]{1,0:T(8,128)(2,1)S(1)}, bf16[128,384]{1,0:T(8,128)(2,1)}, u32[]{:S(2)}) copy-start(bf16[128,384]{1,0:T(8,128)(2,1)} %mine.1) | copy-start | bytes 294916
  18.4 29.4 %copy-start.2 = (bf16[128,384]{1,0:T(8,128)(2,1)S(1)}, bf16[128,384]{1,0:T(8,128)(2,1)}, u32[]{:S(2)}) copy-start(bf16[128,384]{1,0:T(8,128)(2,1)} %o_own.1) | copy-start | bytes 294916
  18.5 11.0 %collective-permute-start.1 = (bf16[256,768]{1,0:T(8,128)(2,1)S(1)}, bf16[256,768]{1,0:T(8,128)(2,1)S(1)}, u32[]{:S(2)}, u32[]{:S(2)}) collective-permute-start(bf16[256,768]{1,0:T(8,128)(2,1)S(1)} %pad_maximum_fusion), channel_id=1, source_target_pairs={{0,16},{16,0},{1,17},{17,1},{2,18},{18,2},{3,19},{19,3},{4,20},{20... | collective-permute-start | bytes 1179656 | tf_op jit(solution)/shard_map/ppermute | solution.py:278
  29.5 18.3 %copy-start.4 = (s32[6144]{0:T(1024)S(1)}, s32[6144]{0:T(1024)}, u32[]{:S(2)}) copy-start(s32[6144]{0:T(1024)} %param.15) | copy-start | bytes 73732
  29.5 18.3 %collective-permute-start.3 = (bf16[384,256]{1,0:T(8,128)(2,1)S(1)}, bf16[384,256]{1,0:T(8,128)(2,1)S(1)}, u32[]{:S(2)}, u32[]{:S(2)}) collective-permute-start(bf16[384,256]{1,0:T(8,128)(2,1)S(1)} %bitcast.10), channel_id=1, source_target_pairs={{0,384},{192,576},{1,385},{193,577},{2,386},{194,578},{3,387},{195... | collective-permute-start | bytes 589832 | tf_op jit(solution)/shard_map/ppermute | solution.py:292
  34.3 13.5 %collective-permute-start.4 = (bf16[384,256]{1,0:T(8,128)(2,1)S(1)}, bf16[384,256]{1,0:T(8,128)(2,1)S(1)}, u32[]{:S(2)}, u32[]{:S(2)}) collective-permute-start(bf16[384,256]{1,0:T(8,128)(2,1)S(1)} %bitcast.11), channel_id=1, source_target_pairs={{0,192},{192,384},{384,576},{1,193},{193,385},{385,577},{2,194},{1... | collective-permute-start | bytes 589832 | tf_op jit(solution)/shard_map/ppermute | solution.py:293
  37.3 10.5 %collective-permute-start.2 = (bf16[64,256]{1,0:T(8,128)(2,1)S(1)}, bf16[64,256]{1,0:T(8,128)(2,1)S(1)}, u32[]{:S(2)}, u32[]{:S(2)}) collective-permute-start(bf16[64,256]{1,0:T(8,128)(2,1)S(1)} %slice_bitcast_fusion), channel_id=1, source_target_pairs={{176,592},{177,593},{178,594},{179,595},{180,596},{181,597},{182,5... | collective-permute-start | bytes 98312 | tf_op jit(solution)/shard_map/ppermute | solution.py:294
  38.0 18.2 %collective-permute-start.9 = (bf16[128,384]{1,0:T(8,128)(2,1)S(1)}, bf16[128,384]{1,0:T(8,128)(2,1)S(1)}, u32[]{:S(2)}, u32[]{:S(2)}) collective-permute-start(bf16[128,384]{1,0:T(8,128)(2,1)S(1)} %copy-done.3), channel_id=1, source_target_pairs={{0,8},{8,0},{1,9},{9,1},{2,10},{10,2},{3,11},{11,3},{4,12},{12,4},... | collective-permute-start | bytes 294920 | tf_op jit(solution)/shard_map/ppermute | solution.py:280
  50.4 9.1 %all-to-all-start.1 = ((f32[4,32,128]{2,1,0:T(8,128)}), f32[4,32,128]{2,1,0:T(8,128)S(1)}, u32[]{:S(2)}, u32[]{:S(2)}) async-start(f32[4,32,128]{2,1,0:T(8,128)} %softmax_stats.1), calls=%async_computation.1 | async-start | bytes 131072 | tf_op jit(solution)/shard_map/all_to_all | solution.py:311
  56.2 0.7 copy-start.5
  59.4 25.2 %all-to-all-start.3 = ((bf16[8,2,32,384]{3,2,1,0:T(8,128)(2,1)}), bf16[8,2,32,384]{3,2,1,0:T(8,128)(2,1)S(1)}, u32[]{:S(2)}, u32[]{:S(2)}) async-start(bf16[8,2,32,384]{3,2,1,0:T(8,128)(2,1)} %select_rows.1), calls=%async_computation.3 | async-start | bytes 786432 | tf_op jit(solution)/shard_map/all_to_all | solution.py:289
  69.5 6.3 %collective-permute-start.6 = (bf16[2,384,128]{2,1,0:T(8,128)(2,1)S(1)}, bf16[2,384,128]{2,1,0:T(8,128)(2,1)S(1)}, u32[]{:S(2)}, u32[]{:S(2)}) collective-permute-start(bf16[2,384,128]{2,1,0:T(8,128)(2,1)S(1)} %get-tuple-element.33), channel_id=1, source_target_pairs={{0,16},{16,0},{1,17},{17,1},{2,18},{18,2},{3,19},{19,3},{4,20},{20... | collective-permute-start | bytes 589832 | tf_op jit(solution)/shard_map/ppermute | solution.py:334
  72.6 8.4 %collective-permute-start.5 = (bf16[384,256]{1,0:T(8,128)(2,1)S(1)}, bf16[384,256]{1,0:T(8,128)(2,1)S(1)}, u32[]{:S(2)}, u32[]{:S(2)}) collective-permute-start(bf16[384,256]{1,0:T(8,128)(2,1)S(1)} %get-tuple-element.31), channel_id=1, source_target_pairs={{192,0},{384,192},{576,384},{193,1},{385,193},{577,385},{194,2},{3... | collective-permute-start | bytes 589832 | tf_op jit(solution)/shard_map/ppermute | solution.py:327
  73.9 9.9 %collective-permute-start.7 = (bf16[384,256]{1,0:T(8,128)(2,1)S(1)}, bf16[384,256]{1,0:T(8,128)(2,1)S(1)}, u32[]{:S(2)}, u32[]{:S(2)}) collective-permute-start(bf16[384,256]{1,0:T(8,128)(2,1)S(1)} %get-tuple-element.36), channel_id=1, source_target_pairs={{384,0},{576,192},{385,1},{577,193},{386,2},{578,194},{387,3},{579... | collective-permute-start | bytes 589832 | tf_op jit(solution)/shard_map/ppermute | solution.py:326
  75.2 5.8 %collective-permute-start.8 = (bf16[64,256]{1,0:T(8,128)(2,1)S(1)}, bf16[64,256]{1,0:T(8,128)(2,1)S(1)}, u32[]{:S(2)}, u32[]{:S(2)}) collective-permute-start(bf16[64,256]{1,0:T(8,128)(2,1)S(1)} %get-tuple-element.37), channel_id=1, source_target_pairs={{592,176},{593,177},{594,178},{595,179},{596,180},{597,181},{598,1... | collective-permute-start | bytes 98312 | tf_op jit(solution)/shard_map/ppermute | solution.py:328
  84.6 11.3 %copy-start.1 = (bf16[1,32,6144]{2,1,0:T(8,128)(2,1)S(1)}, bf16[1,32,6144]{2,1,0:T(8,128)(2,1)}, u32[]{:S(2)}) copy-start(bf16[1,32,6144]{2,1,0:T(8,128)(2,1)} %param.19) | copy-start | bytes 1179652
  84.6 18.7 %all-to-all-start.2 = ((bf16[12,64,128]{2,1,0:T(8,128)(2,1)}), bf16[12,64,128]{2,1,0:T(8,128)(2,1)S(1)}, u32[]{:S(2)}, u32[]{:S(2)}) async-start(bf16[12,64,128]{2,1,0:T(8,128)(2,1)} %plane_sum.1), calls=%async_computation.2 | async-start | bytes 393216 | tf_op jit(solution)/shard_map/all_to_all | solution.py:340
  92.5 5.9 %collective-permute-start.10 = (bf16[384,128]{1,0:T(8,128)(2,1)S(1)}, bf16[384,128]{1,0:T(8,128)(2,1)S(1)}, u32[]{:S(2)}, u32[]{:S(2)}) collective-permute-start(bf16[384,128]{1,0:T(8,128)(2,1)S(1)} %get-tuple-element.40), channel_id=1, source_target_pairs={{0,1},{1,0},{2,3},{3,2},{4,5},{5,4},{6,7},{7,6},{8,9},{9,8},{10,11... | collective-permute-start | bytes 294920 | tf_op jit(solution)/shard_map/ppermute | solution.py:336
  95.9 0.7 copy-start.6

commit v4 on v3

--- a/solution.py
+++ b/solution.py
@@ -85,7 +85,7 @@
     return jnp.where((pos >= first) & (pos <= last), 0.0, NEG)
 
 
-def prep_kernel(queries, out_grad, key_rows, value_rows, pool, spread, sems):
+def prep_kernel(queries, out_grad, key_rows, value_rows, pool, spread, own, sems):
     group = lax.axis_index("zh") * 4 + lax.axis_index("yh")
     rows = pl.ds(pl.multiple_of(lax.axis_index("yl") * KB, KB), KB)
     cols = pl.ds(pl.multiple_of(group * HD, HD), HD)
@@ -101,6 +101,7 @@
     copies[1].wait()
     for block in range(1, Z):
         spread[block] = spread[0]
+    own[...] = spread[0]
     copies[2].wait()
     copies[3].wait()
 
@@ -262,11 +263,12 @@
     expert_ids,
     expert_out,
 ):
-    pool, spread = call(
+    pool, spread, own = call(
         prep_kernel,
         (
             jax.ShapeDtypeStruct((ROWS, 2 * OWN * HD), BF16),
             jax.ShapeDtypeStruct((Z, KB, 2 * HD), BF16),
+            jax.ShapeDtypeStruct((KB, 2 * HD), BF16),
         ),
         [pltpu.SemaphoreType.DMA((4,))],
         name="prep",
@@ -291,7 +293,7 @@
     lone = [((0 * Z + 5) * 2 + 1, (3 * Z + 0) * 2 + 1)]
     ahead2 = lax.ppermute(plane, "x", [(i, i + 2) for i in range(X - 2)])
     ahead1 = lax.ppermute(plane, "x", [(i, i + 1) for i in range(X - 1)])
-    aheadx = lax.ppermute(spread[0], ("x", "z", "c"), lone)
+    aheadx = lax.ppermute(own, ("x", "z", "c"), lone)
 
     doc = doc_ids.reshape(-1, ROWS)
     shared = (pool, pool_y, pool_c, aheadx, ahead2, ahead1, plane)
@@ -309,6 +311,15 @@
         name="softmax_stats",
     )(*shared, attn_out, doc)
     stats = lax.all_to_all(stats, ("c", "yl"), split_axis=0, concat_axis=0, tiled=True)
+    gate_grad, expert_grad = call(
+        combine_kernel,
+        (
+            jax.ShapeDtypeStruct((1, SLOTS), F32),
+            jax.ShapeDtypeStruct((SLOTS, expert_out.shape[2]), BF16),
+        ),
+        [],
+        name="combine_grads",
+    )(rows, ids, gate_weights.T, expert_out[0])
     d2, d1, d0, dx, dq_keep, dq_send = call(
         grads_kernel,
         (
@@ -331,27 +342,20 @@
         (jax.ShapeDtypeStruct((OWN * HD, ROWS), F32), jax.ShapeDtypeStruct((OWN * HD, ROWS), BF16)),
         [],
         name="query_pool",
+        nbytes=1,
     )(dq_keep, lax.ppermute(dq_send, "c", [(0, 1), (1, 0)]))
     back1, dq_other = lax.optimization_barrier((back1, dq_other))
     dq_other = lax.ppermute(dq_other, "yl", [(0, 1), (1, 0)])
     plane_sums = call(plane_kernel, jax.ShapeDtypeStruct((2 * Z, KB, HD), BF16), [], name="plane_sum")(
         d0, back1, back2, backx
     )
+    plane_sums, _ = lax.optimization_barrier((plane_sums, dq_other))
     parts = lax.all_to_all(plane_sums, ("z", "yl"), split_axis=0, concat_axis=0, tiled=True)
 
-    gate_grad, expert_grad = call(
-        combine_kernel,
-        (
-            jax.ShapeDtypeStruct((1, SLOTS), F32),
-            jax.ShapeDtypeStruct((SLOTS, expert_out.shape[2]), BF16),
-        ),
-        [],
-        name="combine_grads",
-    )(rows, ids, gate_weights.T, expert_out[0])
     query_grad = call(query_kernel, jax.ShapeDtypeStruct((ROWS, OWN * HD), BF16), [], name="query_sum")(
         dq_mine, dq_other
     )
-    parts, expert_grad, query_grad = lax.optimization_barrier((parts, expert_grad, query_grad))
+    parts, query_grad = lax.optimization_barrier((parts, query_grad))
     key_grad, value_grad = call(
         block_kernel,
         (jax.ShapeDtypeStruct((HD // 2, ROWS), BF16), jax.ShapeDtypeStruct((HD // 2, ROWS), BF16)),

time: 105 us -> 110 us (1.048)
  starting transfers between devices: 67 us -> 72.3 us
    all_to_all x1, starting transfers between devices: 7.94 us -> 13.2 us  [local(): lax.all_to_all(plane_sums, ('z', 'yl'), split_axis=0, concat_axis=0, tile...]
    ppermute x1, waiting for transfers between devices: 2.8 us -> 0.01 us  [local(): back2 = lax.ppermute(d2, 'x', [(i + 2, i) for i in range(X - 2)])]
    all_to_all x1, waiting for transfers between devices: 4.05 us -> 6.71 us  [local(): lax.all_to_all(plane_sums, ('z', 'yl'), split_axis=0, concat_axis=0, tile...]
  transfers between devices with their start and end apart: 15 -> 15, of which waited for: 6 -> 5; matrix products, arithmetic and copies ran while one was open for 1% -> 0% of each run, Pallas kernels for 11% -> 10%
where the time goes in v4:
time: 110 us; the launch traced here: 109 us
  starting transfers between devices  72.3 us (66%)
  waiting for transfers between devices  20.8 us (19%)
  Pallas kernels  13.9 us (13%)
  local copies, waits for them, and re-layouts  1.37 us (1%)
    all_to_all x1, starting transfers between devices, local(): lax.all_to_all(plane_sums, ('z', 'yl'), split_axis=0, concat_axis=0, tile...  13.2 us
    all_to_all x1, starting transfers between devices, local(): lax.all_to_all(spread, 'z', split_axis=0, concat_axis=0, tiled=True)  12 us
    ppermute x1, starting transfers between devices, local(): row_other = lax.ppermute(row_grad, 'zh', [(0, 1), (1, 0)])  9.81 us
    all_to_all x1, waiting for transfers between devices, local(): lax.all_to_all(spread, 'z', split_axis=0, concat_axis=0, tiled=True)  6.85 us
    all_to_all x1, waiting for transfers between devices, local(): lax.all_to_all(plane_sums, ('z', 'yl'), split_axis=0, concat_axis=0, tile...  6.71 us
    all_to_all x1, starting transfers between devices, local(): lax.all_to_all(chosen_rows, ('yh', 'yl'), split_axis=0, concat_axis=0, ti...  5.93 us
    all_to_all x1, starting transfers between devices, local(): lax.all_to_all(stats, ('c', 'yl'), split_axis=0, concat_axis=0, tiled=True)  5.8 us
    ppermute x1, waiting for transfers between devices, local(): back1 = lax.ppermute(d1, 'x', [(i + 1, i) for i in range(X - 1)])  5.75 us
  transfers between devices with their start and end apart: 15, of which 5 were waited for; matrix products, arithmetic and copies ran while one was open for 0% of the time, Pallas kernels for 10%

profile of v4, /device:TPU:1, one launch (start us, length us, event | category | flops | bytes accessed | tf_op | source)
XLA Modules:
  0.0 109.3 jit_solution(3365214390615795640)
XLA Ops:
  0.6 1.8 %prep.1 = (bf16[128,768]{1,0:T(8,128)(2,1)}, bf16[6,64,256]{2,1,0:T(8,128)(2,1)}, bf16[64,256]{1,0:T(8,128)(2,1)}) custom-call(bf16[128,384]{1,0:T(8,128)(2,1)} %queries.1, bf16[128,384]{1,0:T(8,128)(2,1)} %out_grad.1, bf16[128,1024]{1,0:T(8,128)(2,1)} %key_rows.1, bf16[128,1024]{1,0:T(8,128)(2,1)} %value_rows.1), custom_call_target="tpu_custom_call" | custom-call | bytes 1048576 | tf_op jit(solution)/shard_map/prep/pallas_call | solution.py:266
  2.4 4.0 %collective-permute-start = (bf16[128,768]{1,0:T(8,128)(2,1)}, bf16[128,768]{1,0:T(8,128)(2,1)S(1)}, u32[]{:S(2)}, u32[]{:S(2)}) collective-permute-start(bf16[128,768]{1,0:T(8,128)(2,1)} %get-tuple-element.27.qd), channel_id=1, source_target_pairs={{0,1},{1,0},{2,3},{3,2},{4,5},{5,4},{6,7},{7,6},{8,9},{9,8},{10,11... | collective-permute-start | bytes 589832 | tf_op jit(solution)/shard_map/ppermute | solution.py:279
  6.4 0.0 copy-start
  6.5 12.0 %all-to-all-start = ((bf16[6,64,256]{2,1,0:T(8,128)(2,1)}), bf16[6,64,256]{2,1,0:T(8,128)(2,1)S(1)}, u32[]{:S(2)}, u32[]{:S(2)}) async-start(bf16[6,64,256]{2,1,0:T(8,128)(2,1)} %get-tuple-element.28), calls=%async_computation | async-start | bytes 393216 | tf_op jit(solution)/shard_map/all_to_all | solution.py:278
  18.4 0.0 copy-start.2
  18.5 4.1 %collective-permute-start.1 = (bf16[256,768]{1,0:T(8,128)(2,1)S(1)}, bf16[256,768]{1,0:T(8,128)(2,1)S(1)}, u32[]{:S(2)}, u32[]{:S(2)}) collective-permute-start(bf16[256,768]{1,0:T(8,128)(2,1)S(1)} %pad_maximum_fusion), channel_id=1, source_target_pairs={{0,16},{16,0},{1,17},{17,1},{2,18},{18,2},{3,19},{19,3},{4,20},{20... | collective-permute-start | bytes 1179656 | tf_op jit(solution)/shard_map/ppermute | solution.py:280
  22.6 6.8 %all-to-all-done = bf16[6,64,256]{2,1,0:T(8,128)(2,1)S(1)} async-done(((bf16[6,64,256]{2,1,0:T(8,128)(2,1)}), bf16[6,64,256]{2,1,0:T(8,128)(2,1)S(1)}, u32[]{:S(2)}, u32[]{:S(2)}) %all-to-all-start) | async-done | bytes 196640 | tf_op jit(solution)/shard_map/all_to_all | solution.py:278
  29.5 4.6 %collective-permute-start.3 = (bf16[384,256]{1,0:T(8,128)(2,1)S(1)}, bf16[384,256]{1,0:T(8,128)(2,1)S(1)}, u32[]{:S(2)}, u32[]{:S(2)}) collective-permute-start(bf16[384,256]{1,0:T(8,128)(2,1)S(1)} %bitcast.8), channel_id=1, source_target_pairs={{0,384},{192,576},{1,385},{193,577},{2,386},{194,578},{3,387},{195... | collective-permute-start | bytes 589832 | tf_op jit(solution)/shard_map/ppermute | solution.py:294
  34.2 2.2 %collective-permute-start.4 = (bf16[384,256]{1,0:T(8,128)(2,1)S(1)}, bf16[384,256]{1,0:T(8,128)(2,1)S(1)}, u32[]{:S(2)}, u32[]{:S(2)}) collective-permute-start(bf16[384,256]{1,0:T(8,128)(2,1)S(1)} %bitcast.9), channel_id=1, source_target_pairs={{0,192},{192,384},{384,576},{1,193},{193,385},{385,577},{2,194},{1... | collective-permute-start | bytes 589832 | tf_op jit(solution)/shard_map/ppermute | solution.py:295
  36.4 0.7 collective-permute-start.2
  37.1 9.8 %collective-permute-start.10 = (bf16[128,384]{1,0:T(8,128)(2,1)S(1)}, bf16[128,384]{1,0:T(8,128)(2,1)S(1)}, u32[]{:S(2)}, u32[]{:S(2)}) collective-permute-start(bf16[128,384]{1,0:T(8,128)(2,1)S(1)} %copy-done.3), channel_id=1, source_target_pairs={{0,8},{8,0},{1,9},{9,1},{2,10},{10,2},{3,11},{11,3},{4,12},{12,4},... | collective-permute-start | bytes 294920 | tf_op jit(solution)/shard_map/ppermute | solution.py:282
  46.9 2.6 %softmax_stats.1 = f32[4,32,128]{2,1,0:T(8,128)} custom-call(bf16[128,768]{1,0:T(8,128)(2,1)S(1)} %copy-done, bf16[128,768]{1,0:T(8,128)(2,1)S(1)} %collective-permute-done.qd_y, bf16[256,768]{1,0:T(8,128)(2,1)S(1)} %collective-permute-done.1.qd_c, bf16[64,256]{1,0:T(8,128)(2,1)S(1)} %collective-permute-done.2.kvx, ...), custom_call_target="tpu_custom_call" | custom-call | flops 352321536 | bytes 1048576 | tf_op jit(solution)/shard_map/softmax_stats/pallas_call | solution.py:306
  49.5 5.8 %all-to-all-start.1 = ((f32[4,32,128]{2,1,0:T(8,128)}), f32[4,32,128]{2,1,0:T(8,128)S(1)}, u32[]{:S(2)}, u32[]{:S(2)}) async-start(f32[4,32,128]{2,1,0:T(8,128)} %softmax_stats.1), calls=%async_computation.1 | async-start | bytes 131072 | tf_op jit(solution)/shard_map/all_to_all | solution.py:313
  55.3 0.7 copy-done.5
  56.0 2.1 %select_rows.1 = bf16[8,2,32,384]{3,2,1,0:T(8,128)(2,1)} custom-call(bf16[128,384]{1,0:T(8,128)(2,1)S(1)} %copy-done.3, bf16[128,384]{1,0:T(8,128)(2,1)S(1)} %collective-permute-done.10.other, s32[2,128]{1,0:T(2,128)S(1)} %bitcast.15), custom_call_target="tpu_custom_call" | custom-call | flops 50331648 | bytes 1048576 | tf_op jit(solution)/shard_map/select_rows/pallas_call | solution.py:284
  58.1 0.5 all-to-all-done.1.stats
  58.6 5.9 %all-to-all-start.3 = ((bf16[8,2,32,384]{3,2,1,0:T(8,128)(2,1)}), bf16[8,2,32,384]{3,2,1,0:T(8,128)(2,1)S(1)}, u32[]{:S(2)}, u32[]{:S(2)}) async-start(bf16[8,2,32,384]{3,2,1,0:T(8,128)(2,1)} %select_rows.1), calls=%async_computation.3 | async-start | bytes 786432 | tf_op jit(solution)/shard_map/all_to_all | solution.py:291
  64.5 4.2 %score_grads.1 = (bf16[384,256]{1,0:T(8,128)(2,1)S(1)}, bf16[384,256]{1,0:T(8,128)(2,1)S(1)}, f32[384,256]{1,0:T(8,128)S(1)}, bf16[64,256]{1,0:T(8,128)(2,1)S(1)...) custom-call(bf16[128,768]{1,0:T(8,128)(2,1)S(1)} %copy-done, ...), custom_call_target="tpu_custom_call" | custom-call | flops 1761607680 | bytes 1048576 | tf_op jit(solution)/shard_map/score_grads/pallas_call | solution.py:323
  68.7 3.1 %collective-permute-start.6 = (bf16[2,384,128]{2,1,0:T(8,128)(2,1)S(1)}, bf16[2,384,128]{2,1,0:T(8,128)(2,1)S(1)}, u32[]{:S(2)}, u32[]{:S(2)}) collective-permute-start(bf16[2,384,128]{2,1,0:T(8,128)(2,1)S(1)} %get-tuple-element.35), channel_id=1, source_target_pairs={{0,16},{16,0},{1,17},{17,1},{2,18},{18,2},{3,19},{19,3},{4,20},{20... | collective-permute-start | bytes 589832 | tf_op jit(solution)/shard_map/ppermute | solution.py:346
  71.8 1.3 %collective-permute-start.5 = (bf16[384,256]{1,0:T(8,128)(2,1)S(1)}, bf16[384,256]{1,0:T(8,128)(2,1)S(1)}, u32[]{:S(2)}, u32[]{:S(2)}) collective-permute-start(bf16[384,256]{1,0:T(8,128)(2,1)S(1)} %get-tuple-element.33), channel_id=1, source_target_pairs={{192,0},{384,192},{576,384},{193,1},{385,193},{577,385},{194,2},{3... | collective-permute-start | bytes 589832 | tf_op jit(solution)/shard_map/ppermute | solution.py:338
  73.1 1.3 %collective-permute-start.7 = (bf16[384,256]{1,0:T(8,128)(2,1)S(1)}, bf16[384,256]{1,0:T(8,128)(2,1)S(1)}, u32[]{:S(2)}, u32[]{:S(2)}) collective-permute-start(bf16[384,256]{1,0:T(8,128)(2,1)S(1)} %get-tuple-element.38), channel_id=1, source_target_pairs={{384,0},{576,192},{385,1},{577,193},{386,2},{578,194},{387,3},{579... | collective-permute-start | bytes 589832 | tf_op jit(solution)/shard_map/ppermute | solution.py:337
  74.4 5.8 %collective-permute-done.5.r1 = bf16[384,256]{1,0:T(8,128)(2,1)S(1)} collective-permute-done((bf16[384,256]{1,0:T(8,128)(2,1)S(1)}, bf16[384,256]{1,0:T(8,128)(2,1)S(1)}, u32[]{:S(2)}, u32[]{:S(2)}) %collective-permute-start.5) | collective-permute-done | bytes 196640 | tf_op jit(solution)/shard_map/ppermute | solution.py:338
  80.2 3.6 %collective-permute-start.9 = (bf16[384,128]{1,0:T(8,128)(2,1)S(1)}, bf16[384,128]{1,0:T(8,128)(2,1)S(1)}, u32[]{:S(2)}, u32[]{:S(2)}) collective-permute-start(bf16[384,128]{1,0:T(8,128)(2,1)S(1)} %get-tuple-element.40), channel_id=1, source_target_pairs={{0,1},{1,0},{2,3},{3,2},{4,5},{5,4},{6,7},{7,6},{8,9},{9,8},{10,11... | collective-permute-start | bytes 294920 | tf_op jit(solution)/shard_map/ppermute | solution.py:348
  83.8 0.7 collective-permute-start.8
  84.5 0.7 plane_sum.1
  85.3 0.9 collective-permute-done.9.arrived
  86.2 13.2 %all-to-all-start.2 = ((bf16[12,64,128]{2,1,0:T(8,128)(2,1)}), bf16[12,64,128]{2,1,0:T(8,128)(2,1)S(1)}, u32[]{:S(2)}, u32[]{:S(2)}) async-start(bf16[12,64,128]{2,1,0:T(8,128)(2,1)} %plane_sum.1), calls=%async_computation.2 | async-start | bytes 393216 | tf_op jit(solution)/shard_map/all_to_all | solution.py:353
  99.4 0.7 copy-done.6
  100.0 1.0 combine_grads.1
  101.1 0.7 query_sum.1
  101.8 6.7 %all-to-all-done.2.parts = bf16[12,64,128]{2,1,0:T(8,128)(2,1)S(1)} async-done(((bf16[12,64,128]{2,1,0:T(8,128)(2,1)}), bf16[12,64,128]{2,1,0:T(8,128)(2,1)S(1)}, u32[]{:S(2)}, u32[]{:S(2)}) %all-to-all-start.2) | async-done | bytes 196640 | tf_op jit(solution)/shard_map/all_to_all | solution.py:353
  108.5 0.7 block_sum.1
  (24 shorter events, 0.1 us)
Async XLA Ops:
  2.4 16.0 %collective-permute-start = (bf16[128,768]{1,0:T(8,128)(2,1)}, bf16[128,768]{1,0:T(8,128)(2,1)S(1)}, u32[]{:S(2)}, u32[]{:S(2)}) collective-permute-start(bf16[128,768]{1,0:T(8,128)(2,1)} %get-tuple-element.27.qd), channel_id=1, source_target_pairs={{0,1},{1,0},{2,3},{3,2},{4,5},{5,4},{6,7},{7,6},{8,9},{9,8},{10,11... | collective-permute-start | bytes 589832 | tf_op jit(solution)/shard_map/ppermute | solution.py:279
  6.4 12.0 %copy-start = (bf16[128,768]{1,0:T(8,128)(2,1)S(1)}, bf16[128,768]{1,0:T(8,128)(2,1)}, u32[]{:S(2)}) copy-start(bf16[128,768]{1,0:T(8,128)(2,1)} %get-tuple-element.27.qd) | copy-start | bytes 589828
  6.5 23.0 %all-to-all-start = ((bf16[6,64,256]{2,1,0:T(8,128)(2,1)}), bf16[6,64,256]{2,1,0:T(8,128)(2,1)S(1)}, u32[]{:S(2)}, u32[]{:S(2)}) async-start(bf16[6,64,256]{2,1,0:T(8,128)(2,1)} %get-tuple-element.28), calls=%async_computation | async-start | bytes 393216 | tf_op jit(solution)/shard_map/all_to_all | solution.py:278
  18.4 18.0 %copy-start.7 = (bf16[64,256]{1,0:T(8,128)(2,1)S(1)}, bf16[64,256]{1,0:T(8,128)(2,1)}, u32[]{:S(2)}) copy-start(bf16[64,256]{1,0:T(8,128)(2,1)} %get-tuple-element.30) | copy-start | bytes 98308
  18.4 18.7 %copy-start.3 = (bf16[128,384]{1,0:T(8,128)(2,1)S(1)}, bf16[128,384]{1,0:T(8,128)(2,1)}, u32[]{:S(2)}) copy-start(bf16[128,384]{1,0:T(8,128)(2,1)} %mine.1) | copy-start | bytes 294916
  18.4 28.5 %copy-start.2 = (bf16[128,384]{1,0:T(8,128)(2,1)S(1)}, bf16[128,384]{1,0:T(8,128)(2,1)}, u32[]{:S(2)}) copy-start(bf16[128,384]{1,0:T(8,128)(2,1)} %o_own.1) | copy-start | bytes 294916
  18.4 28.5 %copy-start.4 = (s32[6144]{0:T(1024)S(1)}, s32[6144]{0:T(1024)}, u32[]{:S(2)}) copy-start(s32[6144]{0:T(1024)} %param.15) | copy-start | bytes 73732
  18.5 11.0 %collective-permute-start.1 = (bf16[256,768]{1,0:T(8,128)(2,1)S(1)}, bf16[256,768]{1,0:T(8,128)(2,1)S(1)}, u32[]{:S(2)}, u32[]{:S(2)}) collective-permute-start(bf16[256,768]{1,0:T(8,128)(2,1)S(1)} %pad_maximum_fusion), channel_id=1, source_target_pairs={{0,16},{16,0},{1,17},{17,1},{2,18},{18,2},{3,19},{19,3},{4,20},{20... | collective-permute-start | bytes 1179656 | tf_op jit(solution)/shard_map/ppermute | solution.py:280
  29.5 17.4 %collective-permute-start.3 = (bf16[384,256]{1,0:T(8,128)(2,1)S(1)}, bf16[384,256]{1,0:T(8,128)(2,1)S(1)}, u32[]{:S(2)}, u32[]{:S(2)}) collective-permute-start(bf16[384,256]{1,0:T(8,128)(2,1)S(1)} %bitcast.8), channel_id=1, source_target_pairs={{0,384},{192,576},{1,385},{193,577},{2,386},{194,578},{3,387},{195... | collective-permute-start | bytes 589832 | tf_op jit(solution)/shard_map/ppermute | solution.py:294
  34.2 12.8 %collective-permute-start.4 = (bf16[384,256]{1,0:T(8,128)(2,1)S(1)}, bf16[384,256]{1,0:T(8,128)(2,1)S(1)}, u32[]{:S(2)}, u32[]{:S(2)}) collective-permute-start(bf16[384,256]{1,0:T(8,128)(2,1)S(1)} %bitcast.9), channel_id=1, source_target_pairs={{0,192},{192,384},{384,576},{1,193},{193,385},{385,577},{2,194},{1... | collective-permute-start | bytes 589832 | tf_op jit(solution)/shard_map/ppermute | solution.py:295
  36.4 10.5 %collective-permute-start.2 = (bf16[64,256]{1,0:T(8,128)(2,1)S(1)}, bf16[64,256]{1,0:T(8,128)(2,1)S(1)}, u32[]{:S(2)}, u32[]{:S(2)}) collective-permute-start(bf16[64,256]{1,0:T(8,128)(2,1)S(1)} %copy-done.7), channel_id=1, source_target_pairs={{176,592},{177,593},{178,594},{179,595},{180,596},{181,597},{182,5... | collective-permute-start | bytes 98312 | tf_op jit(solution)/shard_map/ppermute | solution.py:296
  37.1 18.2 %collective-permute-start.10 = (bf16[128,384]{1,0:T(8,128)(2,1)S(1)}, bf16[128,384]{1,0:T(8,128)(2,1)S(1)}, u32[]{:S(2)}, u32[]{:S(2)}) collective-permute-start(bf16[128,384]{1,0:T(8,128)(2,1)S(1)} %copy-done.3), channel_id=1, source_target_pairs={{0,8},{8,0},{1,9},{9,1},{2,10},{10,2},{3,11},{11,3},{4,12},{12,4},... | collective-permute-start | bytes 294920 | tf_op jit(solution)/shard_map/ppermute | solution.py:282
  49.5 9.1 %all-to-all-start.1 = ((f32[4,32,128]{2,1,0:T(8,128)}), f32[4,32,128]{2,1,0:T(8,128)S(1)}, u32[]{:S(2)}, u32[]{:S(2)}) async-start(f32[4,32,128]{2,1,0:T(8,128)} %softmax_stats.1), calls=%async_computation.1 | async-start | bytes 131072 | tf_op jit(solution)/shard_map/all_to_all | solution.py:313
  55.3 0.7 copy-start.5
  58.6 27.6 %all-to-all-start.3 = ((bf16[8,2,32,384]{3,2,1,0:T(8,128)(2,1)}), bf16[8,2,32,384]{3,2,1,0:T(8,128)(2,1)S(1)}, u32[]{:S(2)}, u32[]{:S(2)}) async-start(bf16[8,2,32,384]{3,2,1,0:T(8,128)(2,1)} %select_rows.1), calls=%async_computation.3 | async-start | bytes 786432 | tf_op jit(solution)/shard_map/all_to_all | solution.py:291
  68.7 5.7 %collective-permute-start.6 = (bf16[2,384,128]{2,1,0:T(8,128)(2,1)S(1)}, bf16[2,384,128]{2,1,0:T(8,128)(2,1)S(1)}, u32[]{:S(2)}, u32[]{:S(2)}) collective-permute-start(bf16[2,384,128]{2,1,0:T(8,128)(2,1)S(1)} %get-tuple-element.35), channel_id=1, source_target_pairs={{0,16},{16,0},{1,17},{17,1},{2,18},{18,2},{3,19},{19,3},{4,20},{20... | collective-permute-start | bytes 589832 | tf_op jit(solution)/shard_map/ppermute | solution.py:346
  71.8 8.4 %collective-permute-start.5 = (bf16[384,256]{1,0:T(8,128)(2,1)S(1)}, bf16[384,256]{1,0:T(8,128)(2,1)S(1)}, u32[]{:S(2)}, u32[]{:S(2)}) collective-permute-start(bf16[384,256]{1,0:T(8,128)(2,1)S(1)} %get-tuple-element.33), channel_id=1, source_target_pairs={{192,0},{384,192},{576,384},{193,1},{385,193},{577,385},{194,2},{3... | collective-permute-start | bytes 589832 | tf_op jit(solution)/shard_map/ppermute | solution.py:338
  73.1 11.5 %collective-permute-start.7 = (bf16[384,256]{1,0:T(8,128)(2,1)S(1)}, bf16[384,256]{1,0:T(8,128)(2,1)S(1)}, u32[]{:S(2)}, u32[]{:S(2)}) collective-permute-start(bf16[384,256]{1,0:T(8,128)(2,1)S(1)} %get-tuple-element.38), channel_id=1, source_target_pairs={{384,0},{576,192},{385,1},{577,193},{386,2},{578,194},{387,3},{579... | collective-permute-start | bytes 589832 | tf_op jit(solution)/shard_map/ppermute | solution.py:337
  80.2 6.0 %collective-permute-start.9 = (bf16[384,128]{1,0:T(8,128)(2,1)S(1)}, bf16[384,128]{1,0:T(8,128)(2,1)S(1)}, u32[]{:S(2)}, u32[]{:S(2)}) collective-permute-start(bf16[384,128]{1,0:T(8,128)(2,1)S(1)} %get-tuple-element.40), channel_id=1, source_target_pairs={{0,1},{1,0},{2,3},{3,2},{4,5},{5,4},{6,7},{7,6},{8,9},{9,8},{10,11... | collective-permute-start | bytes 294920 | tf_op jit(solution)/shard_map/ppermute | solution.py:348
  83.8 0.7 collective-permute-start.8
  85.3 14.1 %copy-start.1 = (bf16[1,32,6144]{2,1,0:T(8,128)(2,1)S(1)}, bf16[1,32,6144]{2,1,0:T(8,128)(2,1)}, u32[]{:S(2)}) copy-start(bf16[1,32,6144]{2,1,0:T(8,128)(2,1)} %param.19) | copy-start | bytes 1179652
  86.2 22.3 %all-to-all-start.2 = ((bf16[12,64,128]{2,1,0:T(8,128)(2,1)}), bf16[12,64,128]{2,1,0:T(8,128)(2,1)S(1)}, u32[]{:S(2)}, u32[]{:S(2)}) async-start(bf16[12,64,128]{2,1,0:T(8,128)(2,1)} %plane_sum.1), calls=%async_computation.2 | async-start | bytes 393216 | tf_op jit(solution)/shard_map/all_to_all | solution.py:353
  99.4 0.7 copy-start.6

commit v5 on v4

--- a/solution.py
+++ b/solution.py
@@ -50,15 +50,16 @@
 
 
 def place(z, c, p, parts, q_s, do_s, kv_s):
-    qd, qd_y, qd_c, kvx, kv2, kv1, kv0 = parts
-    for owner, ref, base in ((p, qd, 0), (1 - p, qd_y, 0)):
+    qd, qd_c, qd_y, kvx, kv2, kv1, kv0 = parts
+    for owner, core, ref, base in (
+        (p, c, qd, 0),
+        (p, 1 - c, qd_c, 0),
+        (1 - p, c, qd_y, 0),
+        (1 - p, 1 - c, qd_y, ROWS),
+    ):
         for h in range(OWN):
-            q_s[owner * OWN + h, pl.ds(c * ROWS, ROWS), :] = ref[:, h * HD : (h + 1) * HD]
-            do_s[owner * OWN + h, pl.ds(c * ROWS, ROWS), :] = ref[:, (OWN + h) * HD : (OWN + h + 1) * HD]
-    for owner, base in ((p, 0), (1 - p, ROWS)):
-        for h in range(OWN):
-            q_s[owner * OWN + h, pl.ds((1 - c) * ROWS, ROWS), :] = qd_c[base : base + ROWS, h * HD : (h + 1) * HD]
-            do_s[owner * OWN + h, pl.ds((1 - c) * ROWS, ROWS), :] = qd_c[
+            q_s[owner * OWN + h, pl.ds(core * ROWS, ROWS), :] = ref[base : base + ROWS, h * HD : (h + 1) * HD]
+            do_s[owner * OWN + h, pl.ds(core * ROWS, ROWS), :] = ref[
                 base : base + ROWS, (OWN + h) * HD : (OWN + h + 1) * HD
             ]
     kv_s[0:KB, :] = kvx[...]
@@ -106,10 +107,10 @@
     copies[3].wait()
 
 
-def stats_kernel(qd, qd_y, qd_c, kvx, kv2, kv1, kv0, o_own, doc, stats, q_s, do_s, kv_s):
+def stats_kernel(qd, qd_c, qd_y, kvx, kv2, kv1, kv0, o_own, doc, stats, q_s, do_s, kv_s):
     x, z, c, p = (lax.axis_index(a) for a in ("x", "z", "c", "yl"))
     chip = x * Z + z
-    place(z, c, p, (qd, qd_y, qd_c, kvx, kv2, kv1, kv0), q_s, do_s, kv_s)
+    place(z, c, p, (qd, qd_c, qd_y, kvx, kv2, kv1, kv0), q_s, do_s, kv_s)
     first, last = query_spans(doc, chip)
     keys = kv_s[pl.ds(pl.multiple_of(z * KB, KB), SPAN), 0:HD]
     bias = bias_of(chip, c, p, first, last)
@@ -134,11 +135,11 @@
 
 
 def grads_kernel(
-    qd, qd_y, qd_c, kvx, kv2, kv1, kv0, doc, stats, d2, d1, d0, dx, dq_keep, dq_send, q_s, do_s, kv_s, acc_s
+    qd, qd_c, qd_y, kvx, kv2, kv1, kv0, doc, stats, d2, d1, d0, dx, dq_keep, dq_send, q_s, do_s, kv_s, acc_s
 ):
     x, z, c, p = (lax.axis_index(a) for a in ("x", "z", "c", "yl"))
     chip = x * Z + z
-    place(z, c, p, (qd, qd_y, qd_c, kvx, kv2, kv1, kv0), q_s, do_s, kv_s)
+    place(z, c, p, (qd, qd_c, qd_y, kvx, kv2, kv1, kv0), q_s, do_s, kv_s)
     first, last = query_spans(doc, chip)
     acc_s[...] = jnp.zeros(acc_s.shape, F32)
     tops = [stats[i, 0:12, :] for i in range(4)]
@@ -276,16 +277,15 @@
         in_specs=[pl.BlockSpec(memory_space=pltpu.HBM)] * 4,
     )(queries, out_grad, key_rows, value_rows)
     plane = lax.all_to_all(spread, "z", split_axis=0, concat_axis=0, tiled=True).reshape(PLANE, 2 * HD)
-    pool_y = lax.ppermute(pool, "yl", [(0, 1), (1, 0)])
-    pool_c = lax.ppermute(jnp.concatenate([pool, pool_y], axis=0), "c", [(0, 1), (1, 0)])
-    plane, pool_c = lax.optimization_barrier((plane, pool_c))
+    pool_c = lax.ppermute(pool, "c", [(0, 1), (1, 0)])
+    pool_y = lax.ppermute(jnp.concatenate([pool, pool_c], axis=0), "yl", [(0, 1), (1, 0)])
     row_other = lax.ppermute(row_grad, "zh", [(0, 1), (1, 0)])
     ids = expert_ids.T
     chosen_rows = call(
         select_kernel,
         jax.ShapeDtypeStruct((8, 2, SLOTS, OWN * HD), BF16),
         [],
-        flops=2 * 256 * ROWS * 2 * OWN * HD,
+        flops=400 * 256 * ROWS * 2 * OWN * HD,
         name="select_rows",
     )(row_grad, row_other, ids)
     rows = lax.all_to_all(chosen_rows, ("yh", "yl"), split_axis=0, concat_axis=0, tiled=True)
@@ -296,7 +296,7 @@
     aheadx = lax.ppermute(own, ("x", "z", "c"), lone)
 
     doc = doc_ids.reshape(-1, ROWS)
-    shared = (pool, pool_y, pool_c, aheadx, ahead2, ahead1, plane)
+    shared = (pool, pool_c, pool_y, aheadx, ahead2, ahead1, plane)
     pool_scratch = [
         pltpu.VMEM((HEADS, 2 * ROWS, HD), BF16),
         pltpu.VMEM((HEADS, 2 * ROWS, HD), BF16),
@@ -307,9 +307,10 @@
         stats_kernel,
         jax.ShapeDtypeStruct((4, 32, ROWS), F32),
         pool_scratch,
-        flops=2 * HD * pairs,
+        flops=30 * 2 * HD * pairs,
         name="softmax_stats",
     )(*shared, attn_out, doc)
+    stats, _ = lax.optimization_barrier((stats, rows))
     stats = lax.all_to_all(stats, ("c", "yl"), split_axis=0, concat_axis=0, tiled=True)
     gate_grad, expert_grad = call(
         combine_kernel,
@@ -320,6 +321,7 @@
         [],
         name="combine_grads",
     )(rows, ids, gate_weights.T, expert_out[0])
+    stats, _ = lax.optimization_barrier((stats, expert_grad))
     d2, d1, d0, dx, dq_keep, dq_send = call(
         grads_kernel,
         (
@@ -349,7 +351,6 @@
     plane_sums = call(plane_kernel, jax.ShapeDtypeStruct((2 * Z, KB, HD), BF16), [], name="plane_sum")(
         d0, back1, back2, backx
     )
-    plane_sums, _ = lax.optimization_barrier((plane_sums, dq_other))
     parts = lax.all_to_all(plane_sums, ("z", "yl"), split_axis=0, concat_axis=0, tiled=True)
 
     query_grad = call(query_kernel, jax.ShapeDtypeStruct((ROWS, OWN * HD), BF16), [], name="query_sum")(

time: 110 us -> 111 us (level)
  waiting for transfers between devices: 20.8 us -> 28.9 us
  starting transfers between devices: 72.3 us -> 66.2 us
    all_to_all x1, waiting for transfers between devices: 0.01 us -> 12.4 us  [local(): lax.all_to_all(chosen_rows, ('yh', 'yl'), split_axis=0, concat_axis=0, ti...]
    all_to_all x1, waiting for transfers between devices: 6.85 us -> 0.01 us  [local(): lax.all_to_all(spread, 'z', split_axis=0, concat_axis=0, tiled=True)]
    all_to_all x1, starting transfers between devices: 13.2 us -> 9.6 us  [local(): lax.all_to_all(plane_sums, ('z', 'yl'), split_axis=0, concat_axis=0, tile...]
    ppermute x1, waiting for transfers between devices: 0.01 us -> 2.8 us  [local(): back2 = lax.ppermute(d2, 'x', [(i + 2, i) for i in range(X - 2)])]
    all_to_all x1, waiting for transfers between devices: 6.71 us -> 4.3 us  [local(): lax.all_to_all(plane_sums, ('z', 'yl'), split_axis=0, concat_axis=0, tile...]
    all_to_all x1, starting transfers between devices: 5.8 us -> 3.84 us  [local(): lax.all_to_all(stats, ('c', 'yl'), split_axis=0, concat_axis=0, tiled=True)]
    ppermute x2, starting transfers between devices: 8.17 us -> 6.39 us  [the longest x1 3.2 us: local(): lax.ppermute(jnp.concatenate([pool, pool_c], axis=0), 'yl', [(0, 1), (1,...]
    ppermute x1, waiting for transfers between devices: 0.93 us -> 2.68 us  [local(): dq_other = lax.ppermute(dq_other, 'yl', [(0, 1), (1, 0)])]
  transfers between devices with their start and end apart: 15 -> 15, of which waited for: 5 -> 6; matrix products, arithmetic and copies ran while one was open for 0% -> 0% of each run, Pallas kernels for 10% -> 6%
where the time goes in v5:
time: 111 us
  starting transfers between devices  66.2 us (60%)
  waiting for transfers between devices  28.9 us (26%)
  Pallas kernels  13.9 us (13%)
    all_to_all x1, starting transfers between devices, local(): lax.all_to_all(spread, 'z', split_axis=0, concat_axis=0, tiled=True)  12.8 us
    all_to_all x1, waiting for transfers between devices, local(): lax.all_to_all(chosen_rows, ('yh', 'yl'), split_axis=0, concat_axis=0, ti...  12.4 us
    all_to_all x1, starting transfers between devices, local(): lax.all_to_all(plane_sums, ('z', 'yl'), split_axis=0, concat_axis=0, tile...  9.6 us
    ppermute x1, starting transfers between devices, local(): row_other = lax.ppermute(row_grad, 'zh', [(0, 1), (1, 0)])  9.42 us
    all_to_all x1, starting transfers between devices, local(): lax.all_to_all(chosen_rows, ('yh', 'yl'), split_axis=0, concat_axis=0, ti...  6.05 us
    ppermute x1, waiting for transfers between devices, local(): back1 = lax.ppermute(d1, 'x', [(i + 1, i) for i in range(X - 1)])  5.08 us
    ppermute x1, starting transfers between devices, local(): ahead2 = lax.ppermute(plane, 'x', [(i, i + 2) for i in range(X - 2)])  4.99 us
    all_to_all x1, waiting for transfers between devices, local(): lax.all_to_all(plane_sums, ('z', 'yl'), split_axis=0, concat_axis=0, tile...  4.3 us
  transfers between devices with their start and end apart: 15, of which 6 were waited for; matrix products, arithmetic and copies ran while one was open for 0% of the time, Pallas kernels for 6%

profile of v5, /device:TPU:1, one launch (start us, length us, event | category | flops | bytes accessed | tf_op | source)
XLA Modules:
  0.0 110.6 jit_solution(11082804784979389781)
XLA Ops:
  0.6 1.8 %prep.1 = (bf16[128,768]{1,0:T(8,128)(2,1)}, bf16[6,64,256]{2,1,0:T(8,128)(2,1)}, bf16[64,256]{1,0:T(8,128)(2,1)}) custom-call(bf16[128,384]{1,0:T(8,128)(2,1)} %queries.1, bf16[128,384]{1,0:T(8,128)(2,1)} %out_grad.1, bf16[128,1024]{1,0:T(8,128)(2,1)} %key_rows.1, bf16[128,1024]{1,0:T(8,128)(2,1)} %value_rows.1), custom_call_target="tpu_custom_call" | custom-call | bytes 1048576 | tf_op jit(solution)/shard_map/prep/pallas_call | solution.py:267
  2.4 0.0 copy-start.1
  2.4 12.8 %all-to-all-start = ((bf16[6,64,256]{2,1,0:T(8,128)(2,1)}), bf16[6,64,256]{2,1,0:T(8,128)(2,1)S(1)}, u32[]{:S(2)}, u32[]{:S(2)}) async-start(bf16[6,64,256]{2,1,0:T(8,128)(2,1)} %get-tuple-element.28), calls=%async_computation | async-start | bytes 393216 | tf_op jit(solution)/shard_map/all_to_all | solution.py:279
  15.2 3.2 %collective-permute-start = (bf16[128,768]{1,0:T(8,128)(2,1)S(1)}, bf16[128,768]{1,0:T(8,128)(2,1)S(1)}, u32[]{:S(2)}, u32[]{:S(2)}) collective-permute-start(bf16[128,768]{1,0:T(8,128)(2,1)S(1)} %copy-done.1), channel_id=1, source_target_pairs={{0,16},{16,0},{1,17},{17,1},{2,18},{18,2},{3,19},{19,3},{4,20},{20... | collective-permute-start | bytes 589832 | tf_op jit(solution)/shard_map/ppermute | solution.py:280
  18.4 9.4 %collective-permute-start.5 = (bf16[128,384]{1,0:T(8,128)(2,1)S(1)}, bf16[128,384]{1,0:T(8,128)(2,1)S(1)}, u32[]{:S(2)}, u32[]{:S(2)}) collective-permute-start(bf16[128,384]{1,0:T(8,128)(2,1)S(1)} %copy-done.4), channel_id=1, source_target_pairs={{0,8},{8,0},{1,9},{9,1},{2,10},{10,2},{3,11},{11,3},{4,12},{12,4},... | collective-permute-start | bytes 294920 | tf_op jit(solution)/shard_map/ppermute | solution.py:282
  27.9 0.7 collective-permute-start.2
  28.6 3.2 %collective-permute-start.1 = (bf16[256,768]{1,0:T(8,128)(2,1)S(1)}, bf16[256,768]{1,0:T(8,128)(2,1)S(1)}, u32[]{:S(2)}, u32[]{:S(2)}) collective-permute-start(bf16[256,768]{1,0:T(8,128)(2,1)S(1)} %pad_maximum_fusion), channel_id=1, source_target_pairs={{0,1},{1,0},{2,3},{3,2},{4,5},{5,4},{6,7},{7,6},{8,9},{9,8},{10,11... | collective-permute-start | bytes 1179656 | tf_op jit(solution)/shard_map/ppermute | solution.py:281
  31.8 0.0 copy-start.2
  31.8 3.1 %collective-permute-start.4 = (bf16[384,256]{1,0:T(8,128)(2,1)S(1)}, bf16[384,256]{1,0:T(8,128)(2,1)S(1)}, u32[]{:S(2)}, u32[]{:S(2)}) collective-permute-start(bf16[384,256]{1,0:T(8,128)(2,1)S(1)} %bitcast.9), channel_id=1, source_target_pairs={{0,192},{192,384},{384,576},{1,193},{193,385},{385,577},{2,194},{1... | collective-permute-start | bytes 589832 | tf_op jit(solution)/shard_map/ppermute | solution.py:295
  35.0 5.0 %collective-permute-start.3 = (bf16[384,256]{1,0:T(8,128)(2,1)S(1)}, bf16[384,256]{1,0:T(8,128)(2,1)S(1)}, u32[]{:S(2)}, u32[]{:S(2)}) collective-permute-start(bf16[384,256]{1,0:T(8,128)(2,1)S(1)} %bitcast.10), channel_id=1, source_target_pairs={{0,384},{192,576},{1,385},{193,577},{2,386},{194,578},{3,387},{195... | collective-permute-start | bytes 589832 | tf_op jit(solution)/shard_map/ppermute | solution.py:294
  40.0 2.1 %select_rows.1 = bf16[8,2,32,384]{3,2,1,0:T(8,128)(2,1)} custom-call(bf16[128,384]{1,0:T(8,128)(2,1)S(1)} %copy-done.4, bf16[128,384]{1,0:T(8,128)(2,1)S(1)} %collective-permute-done.5.other, s32[2,128]{1,0:T(2,128)S(1)} %bitcast.13), custom_call_target="tpu_custom_call" | custom-call | flops 10066329600 | bytes 1048576 | tf_op jit(solution)/shard_map/select_rows/pallas_call | solution.py:284
  42.1 6.1 %all-to-all-start.1 = ((bf16[8,2,32,384]{3,2,1,0:T(8,128)(2,1)}), bf16[8,2,32,384]{3,2,1,0:T(8,128)(2,1)S(1)}, u32[]{:S(2)}, u32[]{:S(2)}) async-start(bf16[8,2,32,384]{3,2,1,0:T(8,128)(2,1)} %select_rows.1), calls=%async_computation.1 | async-start | bytes 786432 | tf_op jit(solution)/shard_map/all_to_all | solution.py:291
  48.2 2.6 %softmax_stats.1 = f32[4,32,128]{2,1,0:T(8,128)} custom-call(bf16[128,768]{1,0:T(8,128)(2,1)S(1)} %copy-done.1, bf16[128,768]{1,0:T(8,128)(2,1)S(1)} %collective-permute-done.qd_c, bf16[256,768]{1,0:T(8,128)(2,1)S(1)} %collective-permute-done.1.qd_y, bf16[64,256]{1,0:T(8,128)(2,1)S(1)} %collective-permute-done.2.kvx, ...), custom_call_target="tpu_custom_call" | custom-call | flops 10569646080 | bytes 1048576 | tf_op jit(solution)/shard_map/softmax_stats/pallas_call | solution.py:306
  50.7 12.4 %all-to-all-done.1.rows = bf16[8,2,32,384]{3,2,1,0:T(8,128)(2,1)S(1)} async-done(((bf16[8,2,32,384]{3,2,1,0:T(8,128)(2,1)}), bf16[8,2,32,384]{3,2,1,0:T(8,128)(2,1)S(1)}, u32[]{:S(2)}, u32[]{:S(2)}) %all-to-all-start.1) | async-done | bytes 393248 | tf_op jit(solution)/shard_map/all_to_all | solution.py:291
  63.2 3.8 %all-to-all-start.2 = ((f32[4,32,128]{2,1,0:T(8,128)}), f32[4,32,128]{2,1,0:T(8,128)S(1)}, u32[]{:S(2)}, u32[]{:S(2)}) async-start(f32[4,32,128]{2,1,0:T(8,128)} %softmax_stats.1), calls=%async_computation.2 | async-start | bytes 131072 | tf_op jit(solution)/shard_map/all_to_all | solution.py:314
  67.0 0.7 copy-done.3
  67.7 1.0 combine_grads.1
  68.7 1.5 %all-to-all-done.2.stats = f32[4,32,128]{2,1,0:T(8,128)S(1)} async-done(((f32[4,32,128]{2,1,0:T(8,128)}), f32[4,32,128]{2,1,0:T(8,128)S(1)}, u32[]{:S(2)}, u32[]{:S(2)}) %all-to-all-start.2) | async-done | bytes 65568 | tf_op jit(solution)/shard_map/all_to_all | solution.py:314
  70.3 4.2 %score_grads.1 = (bf16[384,256]{1,0:T(8,128)(2,1)S(1)}, bf16[384,256]{1,0:T(8,128)(2,1)S(1)}, f32[384,256]{1,0:T(8,128)S(1)}, bf16[64,256]{1,0:T(8,128)(2,1)S(1)...) custom-call(bf16[128,768]{1,0:T(8,128)(2,1)S(1)} %copy-done.1, ...), custom_call_target="tpu_custom_call" | custom-call | flops 1761607680 | bytes 1048576 | tf_op jit(solution)/shard_map/score_grads/pallas_call | solution.py:325
  74.5 2.8 %collective-permute-start.7 = (bf16[2,384,128]{2,1,0:T(8,128)(2,1)S(1)}, bf16[2,384,128]{2,1,0:T(8,128)(2,1)S(1)}, u32[]{:S(2)}, u32[]{:S(2)}) collective-permute-start(bf16[2,384,128]{2,1,0:T(8,128)(2,1)S(1)} %get-tuple-element.35), channel_id=1, source_target_pairs={{0,16},{16,0},{1,17},{17,1},{2,18},{18,2},{3,19},{19,3},{4,20},{20... | collective-permute-start | bytes 589832 | tf_op jit(solution)/shard_map/ppermute | solution.py:348
  77.2 1.3 %collective-permute-start.6 = (bf16[384,256]{1,0:T(8,128)(2,1)S(1)}, bf16[384,256]{1,0:T(8,128)(2,1)S(1)}, u32[]{:S(2)}, u32[]{:S(2)}) collective-permute-start(bf16[384,256]{1,0:T(8,128)(2,1)S(1)} %get-tuple-element.33), channel_id=1, source_target_pairs={{192,0},{384,192},{576,384},{193,1},{385,193},{577,385},{194,2},{3... | collective-permute-start | bytes 589832 | tf_op jit(solution)/shard_map/ppermute | solution.py:340
  78.5 1.3 %collective-permute-start.8 = (bf16[384,256]{1,0:T(8,128)(2,1)S(1)}, bf16[384,256]{1,0:T(8,128)(2,1)S(1)}, u32[]{:S(2)}, u32[]{:S(2)}) collective-permute-start(bf16[384,256]{1,0:T(8,128)(2,1)S(1)} %get-tuple-element.38), channel_id=1, source_target_pairs={{384,0},{576,192},{385,1},{577,193},{386,2},{578,194},{387,3},{579... | collective-permute-start | bytes 589832 | tf_op jit(solution)/shard_map/ppermute | solution.py:339
  79.8 0.7 collective-permute-start.9
  80.6 5.1 %collective-permute-done.6.r1 = bf16[384,256]{1,0:T(8,128)(2,1)S(1)} collective-permute-done((bf16[384,256]{1,0:T(8,128)(2,1)S(1)}, bf16[384,256]{1,0:T(8,128)(2,1)S(1)}, u32[]{:S(2)}, u32[]{:S(2)}) %collective-permute-start.6) | collective-permute-done | bytes 196640 | tf_op jit(solution)/shard_map/ppermute | solution.py:340
  85.7 2.8 %collective-permute-done.8.r2 = bf16[384,256]{1,0:T(8,128)(2,1)S(1)} collective-permute-done((bf16[384,256]{1,0:T(8,128)(2,1)S(1)}, bf16[384,256]{1,0:T(8,128)(2,1)S(1)}, u32[]{:S(2)}, u32[]{:S(2)}) %collective-permute-start.8) | collective-permute-done | bytes 196640 | tf_op jit(solution)/shard_map/ppermute | solution.py:339
  88.5 0.7 plane_sum.1
  89.2 9.6 %all-to-all-start.3 = ((bf16[12,64,128]{2,1,0:T(8,128)(2,1)}), bf16[12,64,128]{2,1,0:T(8,128)(2,1)S(1)}, u32[]{:S(2)}, u32[]{:S(2)}) async-start(bf16[12,64,128]{2,1,0:T(8,128)(2,1)} %plane_sum.1), calls=%async_computation.3 | async-start | bytes 393216 | tf_op jit(solution)/shard_map/all_to_all | solution.py:354
  98.8 3.3 %collective-permute-start.10 = (bf16[384,128]{1,0:T(8,128)(2,1)S(1)}, bf16[384,128]{1,0:T(8,128)(2,1)S(1)}, u32[]{:S(2)}, u32[]{:S(2)}) collective-permute-start(bf16[384,128]{1,0:T(8,128)(2,1)S(1)} %get-tuple-element.41), channel_id=1, source_target_pairs={{0,1},{1,0},{2,3},{3,2},{4,5},{5,4},{6,7},{7,6},{8,9},{9,8},{10,11... | collective-permute-start | bytes 294920 | tf_op jit(solution)/shard_map/ppermute | solution.py:350
  102.1 2.7 %collective-permute-done.10.arrived = bf16[384,128]{1,0:T(8,128)(2,1)S(1)} collective-permute-done((bf16[384,128]{1,0:T(8,128)(2,1)S(1)}, bf16[384,128]{1,0:T(8,128)(2,1)S(1)}, u32[]{:S(2)}, u32[]{:S(2)}) %collective-permute-start.10) | collective-permute-done | bytes 98336 | tf_op jit(solution)/shard_map/ppermute | solution.py:350
  104.8 0.7 query_sum.1
  105.6 4.3 %all-to-all-done.3.parts = bf16[12,64,128]{2,1,0:T(8,128)(2,1)S(1)} async-done(((bf16[12,64,128]{2,1,0:T(8,128)(2,1)}), bf16[12,64,128]{2,1,0:T(8,128)(2,1)S(1)}, u32[]{:S(2)}, u32[]{:S(2)}) %all-to-all-start.3) | async-done | bytes 196640 | tf_op jit(solution)/shard_map/all_to_all | solution.py:354
  109.9 0.7 block_sum.1
  (24 shorter events, 0.1 us)
Async XLA Ops:
  2.4 12.8 %copy-start.1 = (bf16[128,768]{1,0:T(8,128)(2,1)S(1)}, bf16[128,768]{1,0:T(8,128)(2,1)}, u32[]{:S(2)}) copy-start(bf16[128,768]{1,0:T(8,128)(2,1)} %get-tuple-element.26.qd) | copy-start | bytes 589828
  2.4 16.0 %copy-start.4 = (bf16[128,384]{1,0:T(8,128)(2,1)S(1)}, bf16[128,384]{1,0:T(8,128)(2,1)}, u32[]{:S(2)}) copy-start(bf16[128,384]{1,0:T(8,128)(2,1)} %mine.1) | copy-start | bytes 294916
  2.4 25.4 %copy-start.7 = (bf16[64,256]{1,0:T(8,128)(2,1)S(1)}, bf16[64,256]{1,0:T(8,128)(2,1)}, u32[]{:S(2)}) copy-start(bf16[64,256]{1,0:T(8,128)(2,1)} %get-tuple-element.27) | copy-start | bytes 98308
  2.4 29.4 %all-to-all-start = ((bf16[6,64,256]{2,1,0:T(8,128)(2,1)}), bf16[6,64,256]{2,1,0:T(8,128)(2,1)S(1)}, u32[]{:S(2)}, u32[]{:S(2)}) async-start(bf16[6,64,256]{2,1,0:T(8,128)(2,1)} %get-tuple-element.28), calls=%async_computation | async-start | bytes 393216 | tf_op jit(solution)/shard_map/all_to_all | solution.py:279
  15.2 13.3 %collective-permute-start = (bf16[128,768]{1,0:T(8,128)(2,1)S(1)}, bf16[128,768]{1,0:T(8,128)(2,1)S(1)}, u32[]{:S(2)}, u32[]{:S(2)}) collective-permute-start(bf16[128,768]{1,0:T(8,128)(2,1)S(1)} %copy-done.1), channel_id=1, source_target_pairs={{0,16},{16,0},{1,17},{17,1},{2,18},{18,2},{3,19},{19,3},{4,20},{20... | collective-permute-start | bytes 589832 | tf_op jit(solution)/shard_map/ppermute | solution.py:280
  18.4 21.5 %collective-permute-start.5 = (bf16[128,384]{1,0:T(8,128)(2,1)S(1)}, bf16[128,384]{1,0:T(8,128)(2,1)S(1)}, u32[]{:S(2)}, u32[]{:S(2)}) collective-permute-start(bf16[128,384]{1,0:T(8,128)(2,1)S(1)} %copy-done.4), channel_id=1, source_target_pairs={{0,8},{8,0},{1,9},{9,1},{2,10},{10,2},{3,11},{11,3},{4,12},{12,4},... | collective-permute-start | bytes 294920 | tf_op jit(solution)/shard_map/ppermute | solution.py:282
  27.9 20.2 %collective-permute-start.2 = (bf16[64,256]{1,0:T(8,128)(2,1)S(1)}, bf16[64,256]{1,0:T(8,128)(2,1)S(1)}, u32[]{:S(2)}, u32[]{:S(2)}) collective-permute-start(bf16[64,256]{1,0:T(8,128)(2,1)S(1)} %copy-done.7), channel_id=1, source_target_pairs={{176,592},{177,593},{178,594},{179,595},{180,596},{181,597},{182,5... | collective-permute-start | bytes 98312 | tf_op jit(solution)/shard_map/ppermute | solution.py:296
  28.6 19.5 %collective-permute-start.1 = (bf16[256,768]{1,0:T(8,128)(2,1)S(1)}, bf16[256,768]{1,0:T(8,128)(2,1)S(1)}, u32[]{:S(2)}, u32[]{:S(2)}) collective-permute-start(bf16[256,768]{1,0:T(8,128)(2,1)S(1)} %pad_maximum_fusion), channel_id=1, source_target_pairs={{0,1},{1,0},{2,3},{3,2},{4,5},{5,4},{6,7},{7,6},{8,9},{9,8},{10,11... | collective-permute-start | bytes 1179656 | tf_op jit(solution)/shard_map/ppermute | solution.py:281
  31.8 8.2 %copy-start.2 = (s32[128,2]{0,1:T(2,128)S(1)}, s32[128,2]{0,1:T(2,128)}, u32[]{:S(2)}) copy-start(s32[128,2]{0,1:T(2,128)} %param.18) | copy-start | bytes 3076
  31.8 16.3 %collective-permute-start.4 = (bf16[384,256]{1,0:T(8,128)(2,1)S(1)}, bf16[384,256]{1,0:T(8,128)(2,1)S(1)}, u32[]{:S(2)}, u32[]{:S(2)}) collective-permute-start(bf16[384,256]{1,0:T(8,128)(2,1)S(1)} %bitcast.9), channel_id=1, source_target_pairs={{0,192},{192,384},{384,576},{1,193},{193,385},{385,577},{2,194},{1... | collective-permute-start | bytes 589832 | tf_op jit(solution)/shard_map/ppermute | solution.py:295
  35.0 13.2 %collective-permute-start.3 = (bf16[384,256]{1,0:T(8,128)(2,1)S(1)}, bf16[384,256]{1,0:T(8,128)(2,1)S(1)}, u32[]{:S(2)}, u32[]{:S(2)}) collective-permute-start(bf16[384,256]{1,0:T(8,128)(2,1)S(1)} %bitcast.10), channel_id=1, source_target_pairs={{0,384},{192,576},{1,385},{193,577},{2,386},{194,578},{3,387},{195... | collective-permute-start | bytes 589832 | tf_op jit(solution)/shard_map/ppermute | solution.py:294
  42.1 6.1 %copy-start.5 = (bf16[128,384]{1,0:T(8,128)(2,1)S(1)}, bf16[128,384]{1,0:T(8,128)(2,1)}, u32[]{:S(2)}) copy-start(bf16[128,384]{1,0:T(8,128)(2,1)} %o_own.1) | copy-start | bytes 294916
  42.1 6.1 %copy-start.6 = (s32[6144]{0:T(1024)S(1)}, s32[6144]{0:T(1024)}, u32[]{:S(2)}) copy-start(s32[6144]{0:T(1024)} %param.15) | copy-start | bytes 73732
  42.1 21.1 %all-to-all-start.1 = ((bf16[8,2,32,384]{3,2,1,0:T(8,128)(2,1)}), bf16[8,2,32,384]{3,2,1,0:T(8,128)(2,1)S(1)}, u32[]{:S(2)}, u32[]{:S(2)}) async-start(bf16[8,2,32,384]{3,2,1,0:T(8,128)(2,1)} %select_rows.1), calls=%async_computation.1 | async-start | bytes 786432 | tf_op jit(solution)/shard_map/all_to_all | solution.py:291
  48.2 18.8 %copy-start = (bf16[1,32,6144]{2,1,0:T(8,128)(2,1)S(1)}, bf16[1,32,6144]{2,1,0:T(8,128)(2,1)}, u32[]{:S(2)}) copy-start(bf16[1,32,6144]{2,1,0:T(8,128)(2,1)} %param.19) | copy-start | bytes 1179652
  63.2 7.1 %all-to-all-start.2 = ((f32[4,32,128]{2,1,0:T(8,128)}), f32[4,32,128]{2,1,0:T(8,128)S(1)}, u32[]{:S(2)}, u32[]{:S(2)}) async-start(f32[4,32,128]{2,1,0:T(8,128)} %softmax_stats.1), calls=%async_computation.2 | async-start | bytes 131072 | tf_op jit(solution)/shard_map/all_to_all | solution.py:314
  67.0 0.7 copy-start.3
  74.5 6.0 %collective-permute-start.7 = (bf16[2,384,128]{2,1,0:T(8,128)(2,1)S(1)}, bf16[2,384,128]{2,1,0:T(8,128)(2,1)S(1)}, u32[]{:S(2)}, u32[]{:S(2)}) collective-permute-start(bf16[2,384,128]{2,1,0:T(8,128)(2,1)S(1)} %get-tuple-element.35), channel_id=1, source_target_pairs={{0,16},{16,0},{1,17},{17,1},{2,18},{18,2},{3,19},{19,3},{4,20},{20... | collective-permute-start | bytes 589832 | tf_op jit(solution)/shard_map/ppermute | solution.py:348
  77.2 8.4 %collective-permute-start.6 = (bf16[384,256]{1,0:T(8,128)(2,1)S(1)}, bf16[384,256]{1,0:T(8,128)(2,1)S(1)}, u32[]{:S(2)}, u32[]{:S(2)}) collective-permute-start(bf16[384,256]{1,0:T(8,128)(2,1)S(1)} %get-tuple-element.33), channel_id=1, source_target_pairs={{192,0},{384,192},{576,384},{193,1},{385,193},{577,385},{194,2},{3... | collective-permute-start | bytes 589832 | tf_op jit(solution)/shard_map/ppermute | solution.py:340
  78.5 9.9 %collective-permute-start.8 = (bf16[384,256]{1,0:T(8,128)(2,1)S(1)}, bf16[384,256]{1,0:T(8,128)(2,1)S(1)}, u32[]{:S(2)}, u32[]{:S(2)}) collective-permute-start(bf16[384,256]{1,0:T(8,128)(2,1)S(1)} %get-tuple-element.38), channel_id=1, source_target_pairs={{384,0},{576,192},{385,1},{577,193},{386,2},{578,194},{387,3},{579... | collective-permute-start | bytes 589832 | tf_op jit(solution)/shard_map/ppermute | solution.py:339
  79.8 5.8 %collective-permute-start.9 = (bf16[64,256]{1,0:T(8,128)(2,1)S(1)}, bf16[64,256]{1,0:T(8,128)(2,1)S(1)}, u32[]{:S(2)}, u32[]{:S(2)}) collective-permute-start(bf16[64,256]{1,0:T(8,128)(2,1)S(1)} %get-tuple-element.39), channel_id=1, source_target_pairs={{592,176},{593,177},{594,178},{595,179},{596,180},{597,181},{598,1... | collective-permute-start | bytes 98312 | tf_op jit(solution)/shard_map/ppermute | solution.py:341
  89.2 20.7 %all-to-all-start.3 = ((bf16[12,64,128]{2,1,0:T(8,128)(2,1)}), bf16[12,64,128]{2,1,0:T(8,128)(2,1)S(1)}, u32[]{:S(2)}, u32[]{:S(2)}) async-start(bf16[12,64,128]{2,1,0:T(8,128)(2,1)} %plane_sum.1), calls=%async_computation.3 | async-start | bytes 393216 | tf_op jit(solution)/shard_map/all_to_all | solution.py:354
  98.8 6.0 %collective-permute-start.10 = (bf16[384,128]{1,0:T(8,128)(2,1)S(1)}, bf16[384,128]{1,0:T(8,128)(2,1)S(1)}, u32[]{:S(2)}, u32[]{:S(2)}) collective-permute-start(bf16[384,128]{1,0:T(8,128)(2,1)S(1)} %get-tuple-element.41), channel_id=1, source_target_pairs={{0,1},{1,0},{2,3},{3,2},{4,5},{5,4},{6,7},{7,6},{8,9},{9,8},{10,11... | collective-permute-start | bytes 294920 | tf_op jit(solution)/shard_map/ppermute | solution.py:350

commit v6 on v5

--- a/solution.py
+++ b/solution.py
@@ -227,26 +227,27 @@
     return (slot == rank) & (hit > 0.0), first_hit, other_hit
 
 
-def select_kernel(mine, other, ids, out):
-    high = lax.axis_index("zh")
-    for pair in range(4):
-        for second in range(2):
-            chosen, _, _ = choice(ids, high * 4 + pair, second)
-            chosen = jnp.where(chosen, 1.0, 0.0).astype(BF16)
-            out[2 * pair + second, high] = dot_nn(chosen, mine[...]).astype(BF16)
-            out[2 * pair + second, 1 - high] = dot_nn(chosen, other[...]).astype(BF16)
-
-
-def combine_kernel(rows, ids, gates, stored, gate_grad, expert_grad):
-    place_in_tp = lax.axis_index("zh") * 8 + lax.axis_index("yh") * 2 + lax.axis_index("yl")
+def select_kernel(mine, ids, out):
+    for high in range(2):
+        for pair in range(4):
+            for second in range(2):
+                chosen, _, _ = choice(ids, high * 4 + pair, second)
+                chosen = jnp.where(chosen, 1.0, 0.0).astype(BF16)
+                out[2 * pair + second, high] = dot_nn(chosen, mine[...]).astype(BF16)
+
+
+def combine_kernel(rows, rows_other, ids, gates, stored, gate_grad, expert_grad):
+    here = lax.axis_index("zh")
+    place_in_tp = here * 8 + lax.axis_index("yh") * 2 + lax.axis_index("yl")
     chosen, first_hit, other_hit = choice(ids, place_in_tp // 2, place_in_tp % 2)
     gate = jnp.where(first_hit, gates[0:1, :], 0.0) + jnp.where(other_hit, gates[1:2, :], 0.0)
     slot_gate = jnp.sum(jnp.where(chosen, gate, 0.0), axis=1, keepdims=True)
     total = jnp.zeros((SLOTS, OWN * HD), F32)
-    for high in range(2):
+    for other in range(2):
+        high = here if other == 0 else 1 - here
         for y in range(8):
-            routed = rows[y, high].astype(F32)
-            cols = slice((high * 8 + y) * OWN * HD, (high * 8 + y + 1) * OWN * HD)
+            routed = (rows[y, here] if other == 0 else rows_other[y]).astype(F32)
+            cols = pl.ds(pl.multiple_of((high * 8 + y) * OWN * HD, HD), OWN * HD)
             total = total + routed * stored[:, cols].astype(F32)
             expert_grad[:, cols] = (slot_gate * routed).astype(BF16)
     gate_grad[...] = jnp.sum(total.T, axis=0, keepdims=True)
@@ -279,16 +280,17 @@
     plane = lax.all_to_all(spread, "z", split_axis=0, concat_axis=0, tiled=True).reshape(PLANE, 2 * HD)
     pool_c = lax.ppermute(pool, "c", [(0, 1), (1, 0)])
     pool_y = lax.ppermute(jnp.concatenate([pool, pool_c], axis=0), "yl", [(0, 1), (1, 0)])
-    row_other = lax.ppermute(row_grad, "zh", [(0, 1), (1, 0)])
     ids = expert_ids.T
     chosen_rows = call(
         select_kernel,
         jax.ShapeDtypeStruct((8, 2, SLOTS, OWN * HD), BF16),
         [],
-        flops=400 * 256 * ROWS * 2 * OWN * HD,
+        flops=100 * 256 * ROWS * 2 * OWN * HD,
         name="select_rows",
-    )(row_grad, row_other, ids)
+    )(row_grad, ids)
     rows = lax.all_to_all(chosen_rows, ("yh", "yl"), split_axis=0, concat_axis=0, tiled=True)
+    away = lax.dynamic_index_in_dim(rows, 1 - lax.axis_index("zh"), 1, keepdims=False)
+    rows_other = lax.ppermute(away, "zh", [(0, 1), (1, 0)])
 
     lone = [((0 * Z + 5) * 2 + 1, (3 * Z + 0) * 2 + 1)]
     ahead2 = lax.ppermute(plane, "x", [(i, i + 2) for i in range(X - 2)])
@@ -312,16 +314,7 @@
     )(*shared, attn_out, doc)
     stats, _ = lax.optimization_barrier((stats, rows))
     stats = lax.all_to_all(stats, ("c", "yl"), split_axis=0, concat_axis=0, tiled=True)
-    gate_grad, expert_grad = call(
-        combine_kernel,
-        (
-            jax.ShapeDtypeStruct((1, SLOTS), F32),
-            jax.ShapeDtypeStruct((SLOTS, expert_out.shape[2]), BF16),
-        ),
-        [],
-        name="combine_grads",
-    )(rows, ids, gate_weights.T, expert_out[0])
-    stats, _ = lax.optimization_barrier((stats, expert_grad))
+    stats, _ = lax.optimization_barrier((stats, away))
     d2, d1, d0, dx, dq_keep, dq_send = call(
         grads_kernel,
         (
@@ -348,6 +341,16 @@
     )(dq_keep, lax.ppermute(dq_send, "c", [(0, 1), (1, 0)]))
     back1, dq_other = lax.optimization_barrier((back1, dq_other))
     dq_other = lax.ppermute(dq_other, "yl", [(0, 1), (1, 0)])
+    gate_grad, expert_grad = call(
+        combine_kernel,
+        (
+            jax.ShapeDtypeStruct((1, SLOTS), F32),
+            jax.ShapeDtypeStruct((SLOTS, expert_out.shape[2]), BF16),
+        ),
+        [],
+        name="combine_grads",
+    )(rows, rows_other, ids, gate_weights.T, expert_out[0])
+    back1, _ = lax.optimization_barrier((back1, expert_grad))
     plane_sums = call(plane_kernel, jax.ShapeDtypeStruct((2 * Z, KB, HD), BF16), [], name="plane_sum")(
         d0, back1, back2, backx
     )

time: 111 us -> 111 us (level)
  waiting for transfers between devices: 28.9 us -> 26.1 us
  starting transfers between devices: 66.2 us -> 68 us
    all_to_all x1, starting transfers between devices: 3.84 us -> 7.05 us  [local(): lax.all_to_all(stats, ('c', 'yl'), split_axis=0, concat_axis=0, tiled=True)]
    all_to_all x1, waiting for transfers between devices: 12.4 us -> 9.24 us  [local(): lax.all_to_all(chosen_rows, ('yh', 'yl'), split_axis=0, concat_axis=0, ti...]
    all_to_all x1, waiting for transfers between devices: 0.01 us -> 3.08 us  [local(): lax.all_to_all(spread, 'z', split_axis=0, concat_axis=0, tiled=True)]
    ppermute x1, waiting for transfers between devices: 5.08 us -> 3.14 us  [local(): back1 = lax.ppermute(d1, 'x', [(i + 1, i) for i in range(X - 1)])]
    all_to_all x1, starting transfers between devices: 9.6 us -> 7.98 us  [local(): lax.all_to_all(plane_sums, ('z', 'yl'), split_axis=0, concat_axis=0, tile...]
    all_to_all x1, waiting for transfers between devices: 1.55 us -> 0.01 us  [local(): lax.all_to_all(stats, ('c', 'yl'), split_axis=0, concat_axis=0, tiled=True)]
  transfers between devices with their start and end apart: 15 -> 15, of which waited for: 6 -> 7; matrix products, arithmetic and copies ran while one was open for 0% -> 0% of each run, Pallas kernels for 6% -> 10%
where the time goes in v6:
time: 111 us
  starting transfers between devices  68 us (61%)
  waiting for transfers between devices  26.1 us (24%)
  Pallas kernels  14.8 us (13%)
    all_to_all x1, starting transfers between devices, local(): lax.all_to_all(spread, 'z', split_axis=0, concat_axis=0, tiled=True)  12.8 us
    ppermute x1, starting transfers between devices, local(): rows_other = lax.ppermute(away, 'zh', [(0, 1), (1, 0)])  9.94 us
    all_to_all x1, waiting for transfers between devices, local(): lax.all_to_all(chosen_rows, ('yh', 'yl'), split_axis=0, concat_axis=0, ti...  9.24 us
    all_to_all x1, starting transfers between devices, local(): lax.all_to_all(plane_sums, ('z', 'yl'), split_axis=0, concat_axis=0, tile...  7.98 us
    all_to_all x1, starting transfers between devices, local(): lax.all_to_all(stats, ('c', 'yl'), split_axis=0, concat_axis=0, tiled=True)  7.05 us
    all_to_all x1, starting transfers between devices, local(): lax.all_to_all(chosen_rows, ('yh', 'yl'), split_axis=0, concat_axis=0, ti...  6.95 us
    ppermute x1, starting transfers between devices, local(): ahead2 = lax.ppermute(plane, 'x', [(i, i + 2) for i in range(X - 2)])  4.36 us
    pallas_call x1, Pallas kernels, local(): call(grads_kernel, (jax.ShapeDtypeStruct((PLANE, 2 * HD), BF16), jax.Shap...  4.19 us
  transfers between devices with their start and end apart: 15, of which 7 were waited for; matrix products, arithmetic and copies ran while one was open for 0% of the time, Pallas kernels for 10%

profile of v6, /device:TPU:1, one launch (start us, length us, event | category | flops | bytes accessed | tf_op | source)
XLA Modules:
  0.0 110.6 jit_solution(6232383371678391303)
XLA Ops:
  0.6 1.8 %prep.1 = (bf16[128,768]{1,0:T(8,128)(2,1)}, bf16[6,64,256]{2,1,0:T(8,128)(2,1)}, bf16[64,256]{1,0:T(8,128)(2,1)}) custom-call(bf16[128,384]{1,0:T(8,128)(2,1)} %queries.1, bf16[128,384]{1,0:T(8,128)(2,1)} %out_grad.1, bf16[128,1024]{1,0:T(8,128)(2,1)} %key_rows.1, bf16[128,1024]{1,0:T(8,128)(2,1)} %value_rows.1), custom_call_target="tpu_custom_call" | custom-call | bytes 1048576 | tf_op jit(solution)/shard_map/prep/pallas_call | solution.py:268
  2.4 0.0 copy-start.1
  2.4 12.8 %all-to-all-start = ((bf16[6,64,256]{2,1,0:T(8,128)(2,1)}), bf16[6,64,256]{2,1,0:T(8,128)(2,1)S(1)}, u32[]{:S(2)}, u32[]{:S(2)}) async-start(bf16[6,64,256]{2,1,0:T(8,128)(2,1)} %get-tuple-element.29), calls=%async_computation | async-start | bytes 393216 | tf_op jit(solution)/shard_map/all_to_all | solution.py:280
  15.2 3.3 %collective-permute-start = (bf16[128,768]{1,0:T(8,128)(2,1)S(1)}, bf16[128,768]{1,0:T(8,128)(2,1)S(1)}, u32[]{:S(2)}, u32[]{:S(2)}) collective-permute-start(bf16[128,768]{1,0:T(8,128)(2,1)S(1)} %copy-done.1), channel_id=1, source_target_pairs={{0,16},{16,0},{1,17},{17,1},{2,18},{18,2},{3,19},{19,3},{4,20},{20... | collective-permute-start | bytes 589832 | tf_op jit(solution)/shard_map/ppermute | solution.py:281
  18.6 1.0 collective-permute-done.qd_c
  19.6 2.9 %collective-permute-start.1 = (bf16[256,768]{1,0:T(8,128)(2,1)S(1)}, bf16[256,768]{1,0:T(8,128)(2,1)S(1)}, u32[]{:S(2)}, u32[]{:S(2)}) collective-permute-start(bf16[256,768]{1,0:T(8,128)(2,1)S(1)} %pad_maximum_fusion), channel_id=1, source_target_pairs={{0,1},{1,0},{2,3},{3,2},{4,5},{5,4},{6,7},{7,6},{8,9},{9,8},{10,11... | collective-permute-start | bytes 1179656 | tf_op jit(solution)/shard_map/ppermute | solution.py:282
  22.5 0.7 collective-permute-start.2
  23.2 3.1 %all-to-all-done = bf16[6,64,256]{2,1,0:T(8,128)(2,1)S(1)} async-done(((bf16[6,64,256]{2,1,0:T(8,128)(2,1)}), bf16[6,64,256]{2,1,0:T(8,128)(2,1)S(1)}, u32[]{:S(2)}, u32[]{:S(2)}) %all-to-all-start) | async-done | bytes 196640 | tf_op jit(solution)/shard_map/all_to_all | solution.py:280
  26.3 3.3 %collective-permute-start.4 = (bf16[384,256]{1,0:T(8,128)(2,1)S(1)}, bf16[384,256]{1,0:T(8,128)(2,1)S(1)}, u32[]{:S(2)}, u32[]{:S(2)}) collective-permute-start(bf16[384,256]{1,0:T(8,128)(2,1)S(1)} %bitcast.11), channel_id=1, source_target_pairs={{0,192},{192,384},{384,576},{1,193},{193,385},{385,577},{2,194},{1... | collective-permute-start | bytes 589832 | tf_op jit(solution)/shard_map/ppermute | solution.py:297
  29.5 4.4 %collective-permute-start.3 = (bf16[384,256]{1,0:T(8,128)(2,1)S(1)}, bf16[384,256]{1,0:T(8,128)(2,1)S(1)}, u32[]{:S(2)}, u32[]{:S(2)}) collective-permute-start(bf16[384,256]{1,0:T(8,128)(2,1)S(1)} %bitcast.12), channel_id=1, source_target_pairs={{0,384},{192,576},{1,385},{193,577},{2,386},{194,578},{3,387},{195... | collective-permute-start | bytes 589832 | tf_op jit(solution)/shard_map/ppermute | solution.py:296
  33.9 3.0 %select_rows.1 = bf16[8,2,32,384]{3,2,1,0:T(8,128)(2,1)} custom-call(bf16[128,384]{1,0:T(8,128)(2,1)S(1)} %copy-done.4, s32[2,128]{1,0:T(2,128)S(1)} %bitcast.15), custom_call_target="tpu_custom_call" | custom-call | flops 2516582400 | bytes 1048576 | tf_op jit(solution)/shard_map/select_rows/pallas_call | solution.py:284
  37.0 7.0 %all-to-all-start.1 = ((bf16[8,2,32,384]{3,2,1,0:T(8,128)(2,1)}), bf16[8,2,32,384]{3,2,1,0:T(8,128)(2,1)S(1)}, u32[]{:S(2)}, u32[]{:S(2)}) async-start(bf16[8,2,32,384]{3,2,1,0:T(8,128)(2,1)} %select_rows.1), calls=%async_computation.1 | async-start | bytes 786432 | tf_op jit(solution)/shard_map/all_to_all | solution.py:291
  44.0 2.6 %softmax_stats.1 = f32[4,32,128]{2,1,0:T(8,128)} custom-call(bf16[128,768]{1,0:T(8,128)(2,1)S(1)} %copy-done.1, bf16[128,768]{1,0:T(8,128)(2,1)S(1)} %collective-permute-done.qd_c, bf16[256,768]{1,0:T(8,128)(2,1)S(1)} %collective-permute-done.1.qd_y, bf16[64,256]{1,0:T(8,128)(2,1)S(1)} %collective-permute-done.2.kvx, ...), custom_call_target="tpu_custom_call" | custom-call | flops 10569646080 | bytes 1048576 | tf_op jit(solution)/shard_map/softmax_stats/pallas_call | solution.py:308
  46.5 9.2 %all-to-all-done.1.rows = bf16[8,2,32,384]{3,2,1,0:T(8,128)(2,1)S(1)} async-done(((bf16[8,2,32,384]{3,2,1,0:T(8,128)(2,1)}), bf16[8,2,32,384]{3,2,1,0:T(8,128)(2,1)S(1)}, u32[]{:S(2)}, u32[]{:S(2)}) %all-to-all-start.1) | async-done | bytes 393248 | tf_op jit(solution)/shard_map/all_to_all | solution.py:291
  55.8 7.0 %all-to-all-start.2 = ((f32[4,32,128]{2,1,0:T(8,128)}), f32[4,32,128]{2,1,0:T(8,128)S(1)}, u32[]{:S(2)}, u32[]{:S(2)}) async-start(f32[4,32,128]{2,1,0:T(8,128)} %softmax_stats.1), calls=%async_computation.2 | async-start | bytes 131072 | tf_op jit(solution)/shard_map/all_to_all | solution.py:316
  62.8 9.9 %collective-permute-start.7 = (bf16[8,32,384]{2,1,0:T(8,128)(2,1)S(1)}, bf16[8,32,384]{2,1,0:T(8,128)(2,1)S(1)}, u32[]{:S(2)}, u32[]{:S(2)}) collective-permute-start(bf16[8,32,384]{2,1,0:T(8,128)(2,1)S(1)} %dynamic-slice_bitcast_fusion), channel_id=1, source_target_pairs={{0,8},{8,0},{1,9},{9,1},{2,10},{10,2},{3,11},{11,3},{4,12},{12,4},... | collective-permute-start | bytes 589832 | tf_op jit(solution)/shard_map/ppermute | solution.py:293
  72.8 4.2 %score_grads.1 = (bf16[384,256]{1,0:T(8,128)(2,1)S(1)}, bf16[384,256]{1,0:T(8,128)(2,1)S(1)}, f32[384,256]{1,0:T(8,128)S(1)}, bf16[64,256]{1,0:T(8,128)(2,1)S(1)...) custom-call(bf16[128,768]{1,0:T(8,128)(2,1)S(1)} %copy-done.1, ...), custom_call_target="tpu_custom_call" | custom-call | flops 1761607680 | bytes 1048576 | tf_op jit(solution)/shard_map/score_grads/pallas_call | solution.py:318
  77.0 2.2 %collective-permute-start.6 = (bf16[2,384,128]{2,1,0:T(8,128)(2,1)S(1)}, bf16[2,384,128]{2,1,0:T(8,128)(2,1)S(1)}, u32[]{:S(2)}, u32[]{:S(2)}) collective-permute-start(bf16[2,384,128]{2,1,0:T(8,128)(2,1)S(1)} %get-tuple-element.35), channel_id=1, source_target_pairs={{0,16},{16,0},{1,17},{17,1},{2,18},{18,2},{3,19},{19,3},{4,20},{20... | collective-permute-start | bytes 589832 | tf_op jit(solution)/shard_map/ppermute | solution.py:341
  79.2 1.3 %collective-permute-start.5 = (bf16[384,256]{1,0:T(8,128)(2,1)S(1)}, bf16[384,256]{1,0:T(8,128)(2,1)S(1)}, u32[]{:S(2)}, u32[]{:S(2)}) collective-permute-start(bf16[384,256]{1,0:T(8,128)(2,1)S(1)} %get-tuple-element.33), channel_id=1, source_target_pairs={{192,0},{384,192},{576,384},{193,1},{385,193},{577,385},{194,2},{3... | collective-permute-start | bytes 589832 | tf_op jit(solution)/shard_map/ppermute | solution.py:333
  80.5 1.3 %collective-permute-start.8 = (bf16[384,256]{1,0:T(8,128)(2,1)S(1)}, bf16[384,256]{1,0:T(8,128)(2,1)S(1)}, u32[]{:S(2)}, u32[]{:S(2)}) collective-permute-start(bf16[384,256]{1,0:T(8,128)(2,1)S(1)} %get-tuple-element.40), channel_id=1, source_target_pairs={{384,0},{576,192},{385,1},{577,193},{386,2},{578,194},{387,3},{579... | collective-permute-start | bytes 589832 | tf_op jit(solution)/shard_map/ppermute | solution.py:332
  81.8 0.7 collective-permute-start.9
  82.5 0.7 copy-done.3
  83.2 1.1 combine_grads.1
  84.3 3.1 %collective-permute-done.5.r1 = bf16[384,256]{1,0:T(8,128)(2,1)S(1)} collective-permute-done((bf16[384,256]{1,0:T(8,128)(2,1)S(1)}, bf16[384,256]{1,0:T(8,128)(2,1)S(1)}, u32[]{:S(2)}, u32[]{:S(2)}) %collective-permute-start.5) | collective-permute-done | bytes 196640 | tf_op jit(solution)/shard_map/ppermute | solution.py:333
  87.5 2.8 %collective-permute-done.8.r2 = bf16[384,256]{1,0:T(8,128)(2,1)S(1)} collective-permute-done((bf16[384,256]{1,0:T(8,128)(2,1)S(1)}, bf16[384,256]{1,0:T(8,128)(2,1)S(1)}, u32[]{:S(2)}, u32[]{:S(2)}) %collective-permute-start.8) | collective-permute-done | bytes 196640 | tf_op jit(solution)/shard_map/ppermute | solution.py:332
  90.3 0.8 plane_sum.1
  91.0 8.0 %all-to-all-start.3 = ((bf16[12,64,128]{2,1,0:T(8,128)(2,1)}), bf16[12,64,128]{2,1,0:T(8,128)(2,1)S(1)}, u32[]{:S(2)}, u32[]{:S(2)}) async-start(bf16[12,64,128]{2,1,0:T(8,128)(2,1)} %plane_sum.1), calls=%async_computation.3 | async-start | bytes 393216 | tf_op jit(solution)/shard_map/all_to_all | solution.py:357
  99.0 3.3 %collective-permute-start.10 = (bf16[384,128]{1,0:T(8,128)(2,1)S(1)}, bf16[384,128]{1,0:T(8,128)(2,1)S(1)}, u32[]{:S(2)}, u32[]{:S(2)}) collective-permute-start(bf16[384,128]{1,0:T(8,128)(2,1)S(1)} %get-tuple-element.43), channel_id=1, source_target_pairs={{0,1},{1,0},{2,3},{3,2},{4,5},{5,4},{6,7},{7,6},{8,9},{9,8},{10,11... | collective-permute-start | bytes 294920 | tf_op jit(solution)/shard_map/ppermute | solution.py:343
  102.3 2.7 %collective-permute-done.10.arrived = bf16[384,128]{1,0:T(8,128)(2,1)S(1)} collective-permute-done((bf16[384,128]{1,0:T(8,128)(2,1)S(1)}, bf16[384,128]{1,0:T(8,128)(2,1)S(1)}, u32[]{:S(2)}, u32[]{:S(2)}) %collective-permute-start.10) | collective-permute-done | bytes 98336 | tf_op jit(solution)/shard_map/ppermute | solution.py:343
  105.0 0.7 query_sum.1
  105.8 4.1 %all-to-all-done.3.parts = bf16[12,64,128]{2,1,0:T(8,128)(2,1)S(1)} async-done(((bf16[12,64,128]{2,1,0:T(8,128)(2,1)}), bf16[12,64,128]{2,1,0:T(8,128)(2,1)S(1)}, u32[]{:S(2)}, u32[]{:S(2)}) %all-to-all-start.3) | async-done | bytes 196640 | tf_op jit(solution)/shard_map/all_to_all | solution.py:357
  109.9 0.7 block_sum.1
  (25 shorter events, 0.2 us)
Async XLA Ops:
  2.4 12.8 %copy-start.1 = (bf16[128,768]{1,0:T(8,128)(2,1)S(1)}, bf16[128,768]{1,0:T(8,128)(2,1)}, u32[]{:S(2)}) copy-start(bf16[128,768]{1,0:T(8,128)(2,1)} %get-tuple-element.27.qd) | copy-start | bytes 589828
  2.4 23.9 %all-to-all-start = ((bf16[6,64,256]{2,1,0:T(8,128)(2,1)}), bf16[6,64,256]{2,1,0:T(8,128)(2,1)S(1)}, u32[]{:S(2)}, u32[]{:S(2)}) async-start(bf16[6,64,256]{2,1,0:T(8,128)(2,1)} %get-tuple-element.29), calls=%async_computation | async-start | bytes 393216 | tf_op jit(solution)/shard_map/all_to_all | solution.py:280
  15.2 7.3 %copy-start.7 = (bf16[64,256]{1,0:T(8,128)(2,1)S(1)}, bf16[64,256]{1,0:T(8,128)(2,1)}, u32[]{:S(2)}) copy-start(bf16[64,256]{1,0:T(8,128)(2,1)} %get-tuple-element.28) | copy-start | bytes 98308
  15.2 18.7 %copy-start.4 = (bf16[128,384]{1,0:T(8,128)(2,1)S(1)}, bf16[128,384]{1,0:T(8,128)(2,1)}, u32[]{:S(2)}) copy-start(bf16[128,384]{1,0:T(8,128)(2,1)} %mine.1) | copy-start | bytes 294916
  15.2 4.4 %collective-permute-start = (bf16[128,768]{1,0:T(8,128)(2,1)S(1)}, bf16[128,768]{1,0:T(8,128)(2,1)S(1)}, u32[]{:S(2)}, u32[]{:S(2)}) collective-permute-start(bf16[128,768]{1,0:T(8,128)(2,1)S(1)} %copy-done.1), channel_id=1, source_target_pairs={{0,16},{16,0},{1,17},{17,1},{2,18},{18,2},{3,19},{19,3},{4,20},{20... | collective-permute-start | bytes 589832 | tf_op jit(solution)/shard_map/ppermute | solution.py:281
  19.6 24.3 %collective-permute-start.1 = (bf16[256,768]{1,0:T(8,128)(2,1)S(1)}, bf16[256,768]{1,0:T(8,128)(2,1)S(1)}, u32[]{:S(2)}, u32[]{:S(2)}) collective-permute-start(bf16[256,768]{1,0:T(8,128)(2,1)S(1)} %pad_maximum_fusion), channel_id=1, source_target_pairs={{0,1},{1,0},{2,3},{3,2},{4,5},{5,4},{6,7},{7,6},{8,9},{9,8},{10,11... | collective-permute-start | bytes 1179656 | tf_op jit(solution)/shard_map/ppermute | solution.py:282
  22.5 21.4 %collective-permute-start.2 = (bf16[64,256]{1,0:T(8,128)(2,1)S(1)}, bf16[64,256]{1,0:T(8,128)(2,1)S(1)}, u32[]{:S(2)}, u32[]{:S(2)}) collective-permute-start(bf16[64,256]{1,0:T(8,128)(2,1)S(1)} %copy-done.7), channel_id=1, source_target_pairs={{176,592},{177,593},{178,594},{179,595},{180,596},{181,597},{182,5... | collective-permute-start | bytes 98312 | tf_op jit(solution)/shard_map/ppermute | solution.py:298
  26.3 7.6 %copy-start.2 = (s32[128,2]{0,1:T(2,128)S(1)}, s32[128,2]{0,1:T(2,128)}, u32[]{:S(2)}) copy-start(s32[128,2]{0,1:T(2,128)} %param.18) | copy-start | bytes 3076
  26.3 17.6 %collective-permute-start.4 = (bf16[384,256]{1,0:T(8,128)(2,1)S(1)}, bf16[384,256]{1,0:T(8,128)(2,1)S(1)}, u32[]{:S(2)}, u32[]{:S(2)}) collective-permute-start(bf16[384,256]{1,0:T(8,128)(2,1)S(1)} %bitcast.11), channel_id=1, source_target_pairs={{0,192},{192,384},{384,576},{1,193},{193,385},{385,577},{2,194},{1... | collective-permute-start | bytes 589832 | tf_op jit(solution)/shard_map/ppermute | solution.py:297
  29.5 14.4 %collective-permute-start.3 = (bf16[384,256]{1,0:T(8,128)(2,1)S(1)}, bf16[384,256]{1,0:T(8,128)(2,1)S(1)}, u32[]{:S(2)}, u32[]{:S(2)}) collective-permute-start(bf16[384,256]{1,0:T(8,128)(2,1)S(1)} %bitcast.12), channel_id=1, source_target_pairs={{0,384},{192,576},{1,385},{193,577},{2,386},{194,578},{3,387},{195... | collective-permute-start | bytes 589832 | tf_op jit(solution)/shard_map/ppermute | solution.py:296
  37.0 7.0 %copy-start.5 = (bf16[128,384]{1,0:T(8,128)(2,1)S(1)}, bf16[128,384]{1,0:T(8,128)(2,1)}, u32[]{:S(2)}) copy-start(bf16[128,384]{1,0:T(8,128)(2,1)} %o_own.1) | copy-start | bytes 294916
  37.0 7.0 %copy-start.6 = (s32[6144]{0:T(1024)S(1)}, s32[6144]{0:T(1024)}, u32[]{:S(2)}) copy-start(s32[6144]{0:T(1024)} %param.15) | copy-start | bytes 73732
  37.0 18.8 %all-to-all-start.1 = ((bf16[8,2,32,384]{3,2,1,0:T(8,128)(2,1)}), bf16[8,2,32,384]{3,2,1,0:T(8,128)(2,1)S(1)}, u32[]{:S(2)}, u32[]{:S(2)}) async-start(bf16[8,2,32,384]{3,2,1,0:T(8,128)(2,1)} %select_rows.1), calls=%async_computation.1 | async-start | bytes 786432 | tf_op jit(solution)/shard_map/all_to_all | solution.py:291
  55.8 17.0 %all-to-all-start.2 = ((f32[4,32,128]{2,1,0:T(8,128)}), f32[4,32,128]{2,1,0:T(8,128)S(1)}, u32[]{:S(2)}, u32[]{:S(2)}) async-start(f32[4,32,128]{2,1,0:T(8,128)} %softmax_stats.1), calls=%async_computation.2 | async-start | bytes 131072 | tf_op jit(solution)/shard_map/all_to_all | solution.py:316
  62.8 19.7 %copy-start = (bf16[1,32,6144]{2,1,0:T(8,128)(2,1)S(1)}, bf16[1,32,6144]{2,1,0:T(8,128)(2,1)}, u32[]{:S(2)}) copy-start(bf16[1,32,6144]{2,1,0:T(8,128)(2,1)} %param.19) | copy-start | bytes 1179652
  62.8 19.7 %collective-permute-start.7 = (bf16[8,32,384]{2,1,0:T(8,128)(2,1)S(1)}, bf16[8,32,384]{2,1,0:T(8,128)(2,1)S(1)}, u32[]{:S(2)}, u32[]{:S(2)}) collective-permute-start(bf16[8,32,384]{2,1,0:T(8,128)(2,1)S(1)} %dynamic-slice_bitcast_fusion), channel_id=1, source_target_pairs={{0,8},{8,0},{1,9},{9,1},{2,10},{10,2},{3,11},{11,3},{4,12},{12,4},... | collective-permute-start | bytes 589832 | tf_op jit(solution)/shard_map/ppermute | solution.py:293
  77.0 7.3 %collective-permute-start.6 = (bf16[2,384,128]{2,1,0:T(8,128)(2,1)S(1)}, bf16[2,384,128]{2,1,0:T(8,128)(2,1)S(1)}, u32[]{:S(2)}, u32[]{:S(2)}) collective-permute-start(bf16[2,384,128]{2,1,0:T(8,128)(2,1)S(1)} %get-tuple-element.35), channel_id=1, source_target_pairs={{0,16},{16,0},{1,17},{17,1},{2,18},{18,2},{3,19},{19,3},{4,20},{20... | collective-permute-start | bytes 589832 | tf_op jit(solution)/shard_map/ppermute | solution.py:341
  79.2 8.2 %collective-permute-start.5 = (bf16[384,256]{1,0:T(8,128)(2,1)S(1)}, bf16[384,256]{1,0:T(8,128)(2,1)S(1)}, u32[]{:S(2)}, u32[]{:S(2)}) collective-permute-start(bf16[384,256]{1,0:T(8,128)(2,1)S(1)} %get-tuple-element.33), channel_id=1, source_target_pairs={{192,0},{384,192},{576,384},{193,1},{385,193},{577,385},{194,2},{3... | collective-permute-start | bytes 589832 | tf_op jit(solution)/shard_map/ppermute | solution.py:333
  80.5 9.7 %collective-permute-start.8 = (bf16[384,256]{1,0:T(8,128)(2,1)S(1)}, bf16[384,256]{1,0:T(8,128)(2,1)S(1)}, u32[]{:S(2)}, u32[]{:S(2)}) collective-permute-start(bf16[384,256]{1,0:T(8,128)(2,1)S(1)} %get-tuple-element.40), channel_id=1, source_target_pairs={{384,0},{576,192},{385,1},{577,193},{386,2},{578,194},{387,3},{579... | collective-permute-start | bytes 589832 | tf_op jit(solution)/shard_map/ppermute | solution.py:332
  81.8 5.6 %collective-permute-start.9 = (bf16[64,256]{1,0:T(8,128)(2,1)S(1)}, bf16[64,256]{1,0:T(8,128)(2,1)S(1)}, u32[]{:S(2)}, u32[]{:S(2)}) collective-permute-start(bf16[64,256]{1,0:T(8,128)(2,1)S(1)} %get-tuple-element.41), channel_id=1, source_target_pairs={{592,176},{593,177},{594,178},{595,179},{596,180},{597,181},{598,1... | collective-permute-start | bytes 98312 | tf_op jit(solution)/shard_map/ppermute | solution.py:334
  82.5 0.7 copy-start.3
  91.0 18.8 %all-to-all-start.3 = ((bf16[12,64,128]{2,1,0:T(8,128)(2,1)}), bf16[12,64,128]{2,1,0:T(8,128)(2,1)S(1)}, u32[]{:S(2)}, u32[]{:S(2)}) async-start(bf16[12,64,128]{2,1,0:T(8,128)(2,1)} %plane_sum.1), calls=%async_computation.3 | async-start | bytes 393216 | tf_op jit(solution)/shard_map/all_to_all | solution.py:357
  99.0 6.0 %collective-permute-start.10 = (bf16[384,128]{1,0:T(8,128)(2,1)S(1)}, bf16[384,128]{1,0:T(8,128)(2,1)S(1)}, u32[]{:S(2)}, u32[]{:S(2)}) collective-permute-start(bf16[384,128]{1,0:T(8,128)(2,1)S(1)} %get-tuple-element.43), channel_id=1, source_target_pairs={{0,1},{1,0},{2,3},{3,2},{4,5},{5,4},{6,7},{7,6},{8,9},{9,8},{10,11... | collective-permute-start | bytes 294920 | tf_op jit(solution)/shard_map/ppermute | solution.py:343

commit v7 on v6

--- a/solution.py
+++ b/solution.py
@@ -128,23 +128,35 @@
     for h in range(OWN):
         prod = qd[:, (OWN + h) * HD : (OWN + h + 1) * HD].astype(F32) * o_own[:, h * HD : (h + 1) * HD].astype(F32)
         rows.append((24 + h, jnp.sum(prod.T, axis=0, keepdims=True)))
-    for peer in range(4):
-        for at, row in rows:
-            stats[peer, at : at + 1, :] = row
-        stats[peer, 27:32, :] = jnp.zeros((5, ROWS), F32)
+    for at, row in rows:
+        stats[at : at + 1, :] = row
+    stats[27:32, :] = jnp.zeros((5, ROWS), F32)
+
+
+def merge_kernel(mine, arrived, out):
+    c = lax.axis_index("c")
+    top = jnp.maximum(mine[0:12, :], arrived[0:12, :])
+    out[0:12, :] = top
+    out[12:24, :] = mine[12:24, :] * jnp.exp2(mine[0:12, :] - top) + arrived[12:24, :] * jnp.exp2(
+        arrived[0:12, :] - top
+    )
+    for h in range(OWN):
+        a, b = mine[24 + h : 25 + h, :], arrived[24 + h : 25 + h, :]
+        out[24 + h : 25 + h, :] = jnp.where(c == 0, a, b)
+        out[27 + h : 28 + h, :] = jnp.where(c == 0, b, a)
+    out[30:32, :] = jnp.zeros((2, ROWS), F32)
 
 
 def grads_kernel(
-    qd, qd_c, qd_y, kvx, kv2, kv1, kv0, doc, stats, d2, d1, d0, dx, dq_keep, dq_send, q_s, do_s, kv_s, acc_s
+    qd, qd_c, qd_y, kvx, kv2, kv1, kv0, doc, stats, stats_y, d2, d1, d0, dx, dq_keep, dq_send, q_s, do_s, kv_s, acc_s
 ):
     x, z, c, p = (lax.axis_index(a) for a in ("x", "z", "c", "yl"))
     chip = x * Z + z
     place(z, c, p, (qd, qd_c, qd_y, kvx, kv2, kv1, kv0), q_s, do_s, kv_s)
     first, last = query_spans(doc, chip)
     acc_s[...] = jnp.zeros(acc_s.shape, F32)
-    tops = [stats[i, 0:12, :] for i in range(4)]
-    top = jnp.maximum(jnp.maximum(tops[0], tops[1]), jnp.maximum(tops[2], tops[3]))
-    total = sum(stats[i, 12:24, :] * jnp.exp2(tops[i] - top) for i in range(4))
+    top = jnp.maximum(stats[0:12, :], stats_y[0:12, :])
+    total = stats[12:24, :] * jnp.exp2(stats[0:12, :] - top) + stats_y[12:24, :] * jnp.exp2(stats_y[0:12, :] - top)
     lse = top + jnp.log(total) * LOG2E
 
     at = pl.multiple_of(z * KB, KB)
@@ -157,7 +169,8 @@
     for h in range(HEADS):
         owner, k = h // OWN, 24 + h % OWN
         row_lse = jnp.concatenate([lse[2 * h : 2 * h + 1, :], lse[2 * h + 1 : 2 * h + 2, :]], axis=1)
-        delta = jnp.concatenate([stats[owner, k : k + 1, :], stats[2 + owner, k : k + 1, :]], axis=1)
+        deltas = [jnp.where(p == owner, stats[i : i + 1, :], stats_y[i : i + 1, :]) for i in (k, k + OWN)]
+        delta = jnp.concatenate(deltas, axis=1)
         q, do = q_s[h], do_s[h]
         probs = jnp.exp2(dot_nt(keys, q) * (SCALE * LOG2E) + bias - row_lse)
         score = (probs * (dot_nt(values, do) - delta)).astype(BF16)
@@ -307,14 +320,15 @@
     pairs = SPAN * HEADS * 2 * ROWS
     stats = call(
         stats_kernel,
-        jax.ShapeDtypeStruct((4, 32, ROWS), F32),
+        jax.ShapeDtypeStruct((32, ROWS), F32),
         pool_scratch,
         flops=30 * 2 * HD * pairs,
         name="softmax_stats",
     )(*shared, attn_out, doc)
-    stats, _ = lax.optimization_barrier((stats, rows))
-    stats = lax.all_to_all(stats, ("c", "yl"), split_axis=0, concat_axis=0, tiled=True)
-    stats, _ = lax.optimization_barrier((stats, away))
+    stats = call(merge_kernel, jax.ShapeDtypeStruct((32, ROWS), F32), [], nbytes=1 << 15, name="merge_stats")(
+        stats, lax.ppermute(stats, "c", [(0, 1), (1, 0)])
+    )
+    stats_y = lax.ppermute(stats, "yl", [(0, 1), (1, 0)])
     d2, d1, d0, dx, dq_keep, dq_send = call(
         grads_kernel,
         (
@@ -328,7 +342,7 @@
         pool_scratch + [pltpu.VMEM((PLACES, 2 * HD), F32)],
         flops=10 * HD * pairs,
         name="score_grads",
-    )(*shared, doc, stats)
+    )(*shared, doc, stats, stats_y)
     back2 = lax.ppermute(d2, "x", [(i + 2, i) for i in range(X - 2)])
     back1 = lax.ppermute(d1, "x", [(i + 1, i) for i in range(X - 1)])
     backx = lax.ppermute(dx, ("x", "z", "c"), [(b, a) for a, b in lone])

time: 111 us -> 106 us (0.955)
  waiting for transfers between devices: 26.1 us -> 18.8 us
  starting transfers between devices: 68 us -> 70.6 us
    all_to_all x1, waiting for transfers between devices: 9.24 us -> 0.89 us  [local(): lax.all_to_all(chosen_rows, ('yh', 'yl'), split_axis=0, concat_axis=0, ti...]
    ppermute x0 -> x2, starting transfers between devices: none -> 8.13 us  [the longest x1 4.48 us: local(): lax.ppermute(stats, 'c', [(0, 1), (1, 0)])]
    all_to_all x1 -> x0, starting transfers between devices: 7.05 us -> none  [local(): lax.all_to_all(stats, ('c', 'yl'), split_axis=0, concat_axis=0, tiled=True)]
    ppermute x1, starting transfers between devices: 2.23 us -> 5.96 us  [local(): lax.ppermute(dq_send, 'c', [(0, 1), (1, 0)])]
    all_to_all x1, starting transfers between devices: 7.98 us -> 6.36 us  [local(): lax.all_to_all(plane_sums, ('z', 'yl'), split_axis=0, concat_axis=0, tile...]
    pallas_call x1 -> x2, Pallas kernels: 2.55 us -> 1.94 us  [the longest x1 1.92 us: local(): call(stats_kernel, jax.ShapeDtypeStruct((32, ROWS), F32), pool_scratch, f...]
  transfers between devices with their start and end apart: 15 -> 16, of which waited for: 7 -> 8; matrix products, arithmetic and copies ran while one was open for 0% -> 0% of each run, Pallas kernels for 10% -> 10%
where the time goes in v7:
time: 106 us; the launch traced here: 105 us
  starting transfers between devices  70.6 us (67%)
  waiting for transfers between devices  18.8 us (18%)
  Pallas kernels  14.2 us (13%)
    all_to_all x1, starting transfers between devices, local(): lax.all_to_all(spread, 'z', split_axis=0, concat_axis=0, tiled=True)  12.8 us
    ppermute x1, starting transfers between devices, local(): rows_other = lax.ppermute(away, 'zh', [(0, 1), (1, 0)])  9.95 us
    all_to_all x1, starting transfers between devices, local(): lax.all_to_all(chosen_rows, ('yh', 'yl'), split_axis=0, concat_axis=0, ti...  6.95 us
    all_to_all x1, starting transfers between devices, local(): lax.all_to_all(plane_sums, ('z', 'yl'), split_axis=0, concat_axis=0, tile...  6.36 us
    ppermute x1, starting transfers between devices, local(): lax.ppermute(dq_send, 'c', [(0, 1), (1, 0)])  5.96 us
    ppermute x1, starting transfers between devices, local(): ahead2 = lax.ppermute(plane, 'x', [(i, i + 2) for i in range(X - 2)])  4.79 us
    ppermute x1, starting transfers between devices, local(): lax.ppermute(stats, 'c', [(0, 1), (1, 0)])  4.48 us
    pallas_call x1, Pallas kernels, local(): call(grads_kernel, (jax.ShapeDtypeStruct((PLANE, 2 * HD), BF16), jax.Shap...  4.19 us
  transfers between devices with their start and end apart: 16, of which 8 were waited for; matrix products, arithmetic and copies ran while one was open for 0% of the time, Pallas kernels for 10%

profile of v7, /device:TPU:1, one launch (start us, length us, event | category | flops | bytes accessed | tf_op | source)
XLA Modules:
  0.0 105.3 jit_solution(9128758786591097829)
XLA Ops:
  0.6 1.8 %prep.1 = (bf16[128,768]{1,0:T(8,128)(2,1)}, bf16[6,64,256]{2,1,0:T(8,128)(2,1)}, bf16[64,256]{1,0:T(8,128)(2,1)}) custom-call(bf16[128,384]{1,0:T(8,128)(2,1)} %queries.1, bf16[128,384]{1,0:T(8,128)(2,1)} %out_grad.1, bf16[128,1024]{1,0:T(8,128)(2,1)} %key_rows.1, bf16[128,1024]{1,0:T(8,128)(2,1)} %value_rows.1), custom_call_target="tpu_custom_call" | custom-call | bytes 1048576 | tf_op jit(solution)/shard_map/prep/pallas_call | solution.py:281
  2.4 12.8 %all-to-all-start = ((bf16[6,64,256]{2,1,0:T(8,128)(2,1)}), bf16[6,64,256]{2,1,0:T(8,128)(2,1)S(1)}, u32[]{:S(2)}, u32[]{:S(2)}) async-start(bf16[6,64,256]{2,1,0:T(8,128)(2,1)} %get-tuple-element.27), calls=%async_computation | async-start | bytes 393216 | tf_op jit(solution)/shard_map/all_to_all | solution.py:293
  15.2 3.3 %collective-permute-start = (bf16[128,768]{1,0:T(8,128)(2,1)S(1)}, bf16[128,768]{1,0:T(8,128)(2,1)S(1)}, u32[]{:S(2)}, u32[]{:S(2)}) collective-permute-start(bf16[128,768]{1,0:T(8,128)(2,1)S(1)} %copy-done.1), channel_id=1, source_target_pairs={{0,16},{16,0},{1,17},{17,1},{2,18},{18,2},{3,19},{19,3},{4,20},{20... | collective-permute-start | bytes 589832 | tf_op jit(solution)/shard_map/ppermute | solution.py:294
  18.6 1.0 collective-permute-done.qd_c
  19.6 2.9 %collective-permute-start.1 = (bf16[256,768]{1,0:T(8,128)(2,1)S(1)}, bf16[256,768]{1,0:T(8,128)(2,1)S(1)}, u32[]{:S(2)}, u32[]{:S(2)}) collective-permute-start(bf16[256,768]{1,0:T(8,128)(2,1)S(1)} %pad_maximum_fusion), channel_id=1, source_target_pairs={{0,1},{1,0},{2,3},{3,2},{4,5},{5,4},{6,7},{7,6},{8,9},{9,8},{10,11... | collective-permute-start | bytes 1179656 | tf_op jit(solution)/shard_map/ppermute | solution.py:295
  22.5 0.7 collective-permute-start.2
  23.2 3.1 %all-to-all-done = bf16[6,64,256]{2,1,0:T(8,128)(2,1)S(1)} async-done(((bf16[6,64,256]{2,1,0:T(8,128)(2,1)}), bf16[6,64,256]{2,1,0:T(8,128)(2,1)S(1)}, u32[]{:S(2)}, u32[]{:S(2)}) %all-to-all-start) | async-done | bytes 196640 | tf_op jit(solution)/shard_map/all_to_all | solution.py:293
  26.3 4.8 %collective-permute-start.3 = (bf16[384,256]{1,0:T(8,128)(2,1)S(1)}, bf16[384,256]{1,0:T(8,128)(2,1)S(1)}, u32[]{:S(2)}, u32[]{:S(2)}) collective-permute-start(bf16[384,256]{1,0:T(8,128)(2,1)S(1)} %bitcast.11), channel_id=1, source_target_pairs={{0,384},{192,576},{1,385},{193,577},{2,386},{194,578},{3,387},{195... | collective-permute-start | bytes 589832 | tf_op jit(solution)/shard_map/ppermute | solution.py:309
  31.1 2.2 %collective-permute-start.4 = (bf16[384,256]{1,0:T(8,128)(2,1)S(1)}, bf16[384,256]{1,0:T(8,128)(2,1)S(1)}, u32[]{:S(2)}, u32[]{:S(2)}) collective-permute-start(bf16[384,256]{1,0:T(8,128)(2,1)S(1)} %bitcast.12), channel_id=1, source_target_pairs={{0,192},{192,384},{384,576},{1,193},{193,385},{385,577},{2,194},{1... | collective-permute-start | bytes 589832 | tf_op jit(solution)/shard_map/ppermute | solution.py:310
  33.3 3.0 %select_rows.1 = bf16[8,2,32,384]{3,2,1,0:T(8,128)(2,1)} custom-call(bf16[128,384]{1,0:T(8,128)(2,1)S(1)} %copy-done.4, s32[2,128]{1,0:T(2,128)S(1)} %bitcast.15), custom_call_target="tpu_custom_call" | custom-call | flops 2516582400 | bytes 1048576 | tf_op jit(solution)/shard_map/select_rows/pallas_call | solution.py:297
  36.4 7.0 %all-to-all-start.1 = ((bf16[8,2,32,384]{3,2,1,0:T(8,128)(2,1)}), bf16[8,2,32,384]{3,2,1,0:T(8,128)(2,1)S(1)}, u32[]{:S(2)}, u32[]{:S(2)}) async-start(bf16[8,2,32,384]{3,2,1,0:T(8,128)(2,1)} %select_rows.1), calls=%async_computation.1 | async-start | bytes 786432 | tf_op jit(solution)/shard_map/all_to_all | solution.py:304
  43.4 1.9 %softmax_stats.1.mine = f32[32,128]{1,0:T(8,128)S(1)} custom-call(bf16[128,768]{1,0:T(8,128)(2,1)S(1)} %copy-done.1, bf16[128,768]{1,0:T(8,128)(2,1)S(1)} %collective-permute-done.qd_c, bf16[256,768]{1,0:T(8,128)(2,1)S(1)} %collective-permute-done.1.qd_y, bf16[64,256]{1,0:T(8,128)(2,1)S(1)} %collective-permute-done.2.kvx, ...), custom_call_target="tpu_custom_call" | custom-call | flops 10569646080 | bytes 1048576 | tf_op jit(solution)/shard_map/softmax_stats/pallas_call | solution.py:321
  45.3 4.5 %collective-permute-start.5 = (f32[32,128]{1,0:T(8,128)S(1)}, f32[32,128]{1,0:T(8,128)S(1)}, u32[]{:S(2)}, u32[]{:S(2)}) collective-permute-start(f32[32,128]{1,0:T(8,128)S(1)} %softmax_stats.1.mine), channel_id=1, source_target_pairs={{0,16},{16,0},{1,17},{17,1},{2,18},{18,2},{3,19},{19,3},{4,20},{20... | collective-permute-start | bytes 49160 | tf_op jit(solution)/shard_map/ppermute | solution.py:329
  49.8 0.8 collective-permute-done.5.arrived
  50.6 3.6 %collective-permute-start.6 = (f32[32,128]{1,0:T(8,128)S(1)}, f32[32,128]{1,0:T(8,128)S(1)}, u32[]{:S(2)}, u32[]{:S(2)}) collective-permute-start(f32[32,128]{1,0:T(8,128)S(1)} %merge_stats.1.stats), channel_id=1, source_target_pairs={{0,1},{1,0},{2,3},{3,2},{4,5},{5,4},{6,7},{7,6},{8,9},{9,8},{10,11... | collective-permute-start | bytes 49160 | tf_op jit(solution)/shard_map/ppermute | solution.py:331
  54.3 0.9 all-to-all-done.1.rows
  55.2 10.0 %collective-permute-start.9 = (bf16[8,32,384]{2,1,0:T(8,128)(2,1)S(1)}, bf16[8,32,384]{2,1,0:T(8,128)(2,1)S(1)}, u32[]{:S(2)}, u32[]{:S(2)}) collective-permute-start(bf16[8,32,384]{2,1,0:T(8,128)(2,1)S(1)} %dynamic-slice_bitcast_fusion), channel_id=1, source_target_pairs={{0,8},{8,0},{1,9},{9,1},{2,10},{10,2},{3,11},{11,3},{4,12},{12,4},... | collective-permute-start | bytes 589832 | tf_op jit(solution)/shard_map/ppermute | solution.py:306
  65.2 4.2 %score_grads.1 = (bf16[384,256]{1,0:T(8,128)(2,1)S(1)}, bf16[384,256]{1,0:T(8,128)(2,1)S(1)}, f32[384,256]{1,0:T(8,128)S(1)}, bf16[64,256]{1,0:T(8,128)(2,1)S(1)...) custom-call(bf16[128,768]{1,0:T(8,128)(2,1)S(1)} %copy-done.1, ...), custom_call_target="tpu_custom_call" | custom-call | flops 1761607680 | bytes 1048576 | tf_op jit(solution)/shard_map/score_grads/pallas_call | solution.py:332
  69.4 6.0 %collective-permute-start.8 = (bf16[2,384,128]{2,1,0:T(8,128)(2,1)S(1)}, bf16[2,384,128]{2,1,0:T(8,128)(2,1)S(1)}, u32[]{:S(2)}, u32[]{:S(2)}) collective-permute-start(bf16[2,384,128]{2,1,0:T(8,128)(2,1)S(1)} %get-tuple-element.31), channel_id=1, source_target_pairs={{0,16},{16,0},{1,17},{17,1},{2,18},{18,2},{3,19},{19,3},{4,20},{20... | collective-permute-start | bytes 589832 | tf_op jit(solution)/shard_map/ppermute | solution.py:355
  75.3 1.3 %collective-permute-start.7 = (bf16[384,256]{1,0:T(8,128)(2,1)S(1)}, bf16[384,256]{1,0:T(8,128)(2,1)S(1)}, u32[]{:S(2)}, u32[]{:S(2)}) collective-permute-start(bf16[384,256]{1,0:T(8,128)(2,1)S(1)} %get-tuple-element.29), channel_id=1, source_target_pairs={{192,0},{384,192},{576,384},{193,1},{385,193},{577,385},{194,2},{3... | collective-permute-start | bytes 589832 | tf_op jit(solution)/shard_map/ppermute | solution.py:347
  76.6 1.3 %collective-permute-start.10 = (bf16[384,256]{1,0:T(8,128)(2,1)S(1)}, bf16[384,256]{1,0:T(8,128)(2,1)S(1)}, u32[]{:S(2)}, u32[]{:S(2)}) collective-permute-start(bf16[384,256]{1,0:T(8,128)(2,1)S(1)} %get-tuple-element.36), channel_id=1, source_target_pairs={{384,0},{576,192},{385,1},{577,193},{386,2},{578,194},{387,3},{579... | collective-permute-start | bytes 589832 | tf_op jit(solution)/shard_map/ppermute | solution.py:346
  77.9 0.7 collective-permute-start.11
  79.3 1.1 combine_grads.1
  80.4 3.4 %collective-permute-done.7.r1 = bf16[384,256]{1,0:T(8,128)(2,1)S(1)} collective-permute-done((bf16[384,256]{1,0:T(8,128)(2,1)S(1)}, bf16[384,256]{1,0:T(8,128)(2,1)S(1)}, u32[]{:S(2)}, u32[]{:S(2)}) %collective-permute-start.7) | collective-permute-done | bytes 196640 | tf_op jit(solution)/shard_map/ppermute | solution.py:347
  83.8 2.8 %collective-permute-done.10.r2 = bf16[384,256]{1,0:T(8,128)(2,1)S(1)} collective-permute-done((bf16[384,256]{1,0:T(8,128)(2,1)S(1)}, bf16[384,256]{1,0:T(8,128)(2,1)S(1)}, u32[]{:S(2)}, u32[]{:S(2)}) %collective-permute-start.10) | collective-permute-done | bytes 196640 | tf_op jit(solution)/shard_map/ppermute | solution.py:346
  86.6 0.8 plane_sum.1
  87.3 6.4 %all-to-all-start.2 = ((bf16[12,64,128]{2,1,0:T(8,128)(2,1)}), bf16[12,64,128]{2,1,0:T(8,128)(2,1)S(1)}, u32[]{:S(2)}, u32[]{:S(2)}) async-start(bf16[12,64,128]{2,1,0:T(8,128)(2,1)} %plane_sum.1), calls=%async_computation.2 | async-start | bytes 393216 | tf_op jit(solution)/shard_map/all_to_all | solution.py:371
  93.7 3.3 %collective-permute-start.12 = (bf16[384,128]{1,0:T(8,128)(2,1)S(1)}, bf16[384,128]{1,0:T(8,128)(2,1)S(1)}, u32[]{:S(2)}, u32[]{:S(2)}) collective-permute-start(bf16[384,128]{1,0:T(8,128)(2,1)S(1)} %get-tuple-element.39), channel_id=1, source_target_pairs={{0,1},{1,0},{2,3},{3,2},{4,5},{5,4},{6,7},{7,6},{8,9},{9,8},{10,11... | collective-permute-start | bytes 294920 | tf_op jit(solution)/shard_map/ppermute | solution.py:357
  97.0 2.7 %collective-permute-done.12.arrived = bf16[384,128]{1,0:T(8,128)(2,1)S(1)} collective-permute-done((bf16[384,128]{1,0:T(8,128)(2,1)S(1)}, bf16[384,128]{1,0:T(8,128)(2,1)S(1)}, u32[]{:S(2)}, u32[]{:S(2)}) %collective-permute-start.12) | collective-permute-done | bytes 98336 | tf_op jit(solution)/shard_map/ppermute | solution.py:357
  99.7 0.7 query_sum.1
  100.4 4.2 %all-to-all-done.2.parts = bf16[12,64,128]{2,1,0:T(8,128)(2,1)S(1)} async-done(((bf16[12,64,128]{2,1,0:T(8,128)(2,1)}), bf16[12,64,128]{2,1,0:T(8,128)(2,1)S(1)}, u32[]{:S(2)}, u32[]{:S(2)}) %all-to-all-start.2) | async-done | bytes 196640 | tf_op jit(solution)/shard_map/all_to_all | solution.py:371
  104.6 0.7 block_sum.1
  (28 shorter events, 0.8 us)
Async XLA Ops:
  2.4 12.8 %copy-start.1 = (bf16[128,768]{1,0:T(8,128)(2,1)S(1)}, bf16[128,768]{1,0:T(8,128)(2,1)}, u32[]{:S(2)}) copy-start(bf16[128,768]{1,0:T(8,128)(2,1)} %get-tuple-element.25.qd) | copy-start | bytes 589828
  2.4 23.9 %all-to-all-start = ((bf16[6,64,256]{2,1,0:T(8,128)(2,1)}), bf16[6,64,256]{2,1,0:T(8,128)(2,1)S(1)}, u32[]{:S(2)}, u32[]{:S(2)}) async-start(bf16[6,64,256]{2,1,0:T(8,128)(2,1)} %get-tuple-element.27), calls=%async_computation | async-start | bytes 393216 | tf_op jit(solution)/shard_map/all_to_all | solution.py:293
  15.2 7.3 %copy-start.7 = (bf16[64,256]{1,0:T(8,128)(2,1)S(1)}, bf16[64,256]{1,0:T(8,128)(2,1)}, u32[]{:S(2)}) copy-start(bf16[64,256]{1,0:T(8,128)(2,1)} %get-tuple-element.26) | copy-start | bytes 98308
  15.2 18.1 %copy-start.4 = (bf16[128,384]{1,0:T(8,128)(2,1)S(1)}, bf16[128,384]{1,0:T(8,128)(2,1)}, u32[]{:S(2)}) copy-start(bf16[128,384]{1,0:T(8,128)(2,1)} %mine.1) | copy-start | bytes 294916
  15.2 4.4 %collective-permute-start = (bf16[128,768]{1,0:T(8,128)(2,1)S(1)}, bf16[128,768]{1,0:T(8,128)(2,1)S(1)}, u32[]{:S(2)}, u32[]{:S(2)}) collective-permute-start(bf16[128,768]{1,0:T(8,128)(2,1)S(1)} %copy-done.1), channel_id=1, source_target_pairs={{0,16},{16,0},{1,17},{17,1},{2,18},{18,2},{3,19},{19,3},{4,20},{20... | collective-permute-start | bytes 589832 | tf_op jit(solution)/shard_map/ppermute | solution.py:294
  19.6 23.7 %collective-permute-start.1 = (bf16[256,768]{1,0:T(8,128)(2,1)S(1)}, bf16[256,768]{1,0:T(8,128)(2,1)S(1)}, u32[]{:S(2)}, u32[]{:S(2)}) collective-permute-start(bf16[256,768]{1,0:T(8,128)(2,1)S(1)} %pad_maximum_fusion), channel_id=1, source_target_pairs={{0,1},{1,0},{2,3},{3,2},{4,5},{5,4},{6,7},{7,6},{8,9},{9,8},{10,11... | collective-permute-start | bytes 1179656 | tf_op jit(solution)/shard_map/ppermute | solution.py:295
  22.5 20.8 %collective-permute-start.2 = (bf16[64,256]{1,0:T(8,128)(2,1)S(1)}, bf16[64,256]{1,0:T(8,128)(2,1)S(1)}, u32[]{:S(2)}, u32[]{:S(2)}) collective-permute-start(bf16[64,256]{1,0:T(8,128)(2,1)S(1)} %copy-done.7), channel_id=1, source_target_pairs={{176,592},{177,593},{178,594},{179,595},{180,596},{181,597},{182,5... | collective-permute-start | bytes 98312 | tf_op jit(solution)/shard_map/ppermute | solution.py:311
  26.3 7.0 %copy-start.2 = (s32[128,2]{0,1:T(2,128)S(1)}, s32[128,2]{0,1:T(2,128)}, u32[]{:S(2)}) copy-start(s32[128,2]{0,1:T(2,128)} %param.18) | copy-start | bytes 3076
  26.3 17.0 %collective-permute-start.3 = (bf16[384,256]{1,0:T(8,128)(2,1)S(1)}, bf16[384,256]{1,0:T(8,128)(2,1)S(1)}, u32[]{:S(2)}, u32[]{:S(2)}) collective-permute-start(bf16[384,256]{1,0:T(8,128)(2,1)S(1)} %bitcast.11), channel_id=1, source_target_pairs={{0,384},{192,576},{1,385},{193,577},{2,386},{194,578},{3,387},{195... | collective-permute-start | bytes 589832 | tf_op jit(solution)/shard_map/ppermute | solution.py:309
  31.1 12.3 %collective-permute-start.4 = (bf16[384,256]{1,0:T(8,128)(2,1)S(1)}, bf16[384,256]{1,0:T(8,128)(2,1)S(1)}, u32[]{:S(2)}, u32[]{:S(2)}) collective-permute-start(bf16[384,256]{1,0:T(8,128)(2,1)S(1)} %bitcast.12), channel_id=1, source_target_pairs={{0,192},{192,384},{384,576},{1,193},{193,385},{385,577},{2,194},{1... | collective-permute-start | bytes 589832 | tf_op jit(solution)/shard_map/ppermute | solution.py:310
  36.4 7.0 %copy-start.5 = (bf16[128,384]{1,0:T(8,128)(2,1)S(1)}, bf16[128,384]{1,0:T(8,128)(2,1)}, u32[]{:S(2)}) copy-start(bf16[128,384]{1,0:T(8,128)(2,1)} %o_own.1) | copy-start | bytes 294916
  36.4 7.0 %copy-start.6 = (s32[6144]{0:T(1024)S(1)}, s32[6144]{0:T(1024)}, u32[]{:S(2)}) copy-start(s32[6144]{0:T(1024)} %param.15) | copy-start | bytes 73732
  36.4 18.8 %all-to-all-start.1 = ((bf16[8,2,32,384]{3,2,1,0:T(8,128)(2,1)}), bf16[8,2,32,384]{3,2,1,0:T(8,128)(2,1)S(1)}, u32[]{:S(2)}, u32[]{:S(2)}) async-start(bf16[8,2,32,384]{3,2,1,0:T(8,128)(2,1)} %select_rows.1), calls=%async_computation.1 | async-start | bytes 786432 | tf_op jit(solution)/shard_map/all_to_all | solution.py:304
  45.3 5.3 %collective-permute-start.5 = (f32[32,128]{1,0:T(8,128)S(1)}, f32[32,128]{1,0:T(8,128)S(1)}, u32[]{:S(2)}, u32[]{:S(2)}) collective-permute-start(f32[32,128]{1,0:T(8,128)S(1)} %softmax_stats.1.mine), channel_id=1, source_target_pairs={{0,16},{16,0},{1,17},{17,1},{2,18},{18,2},{3,19},{19,3},{4,20},{20... | collective-permute-start | bytes 49160 | tf_op jit(solution)/shard_map/ppermute | solution.py:329
  50.6 14.5 %collective-permute-start.6 = (f32[32,128]{1,0:T(8,128)S(1)}, f32[32,128]{1,0:T(8,128)S(1)}, u32[]{:S(2)}, u32[]{:S(2)}) collective-permute-start(f32[32,128]{1,0:T(8,128)S(1)} %merge_stats.1.stats), channel_id=1, source_target_pairs={{0,1},{1,0},{2,3},{3,2},{4,5},{5,4},{6,7},{7,6},{8,9},{9,8},{10,11... | collective-permute-start | bytes 49160 | tf_op jit(solution)/shard_map/ppermute | solution.py:331
  55.2 23.5 %copy-start = (bf16[1,32,6144]{2,1,0:T(8,128)(2,1)S(1)}, bf16[1,32,6144]{2,1,0:T(8,128)(2,1)}, u32[]{:S(2)}) copy-start(bf16[1,32,6144]{2,1,0:T(8,128)(2,1)} %param.19) | copy-start | bytes 1179652
  55.2 23.4 %collective-permute-start.9 = (bf16[8,32,384]{2,1,0:T(8,128)(2,1)S(1)}, bf16[8,32,384]{2,1,0:T(8,128)(2,1)S(1)}, u32[]{:S(2)}, u32[]{:S(2)}) collective-permute-start(bf16[8,32,384]{2,1,0:T(8,128)(2,1)S(1)} %dynamic-slice_bitcast_fusion), channel_id=1, source_target_pairs={{0,8},{8,0},{1,9},{9,1},{2,10},{10,2},{3,11},{11,3},{4,12},{12,4},... | collective-permute-start | bytes 589832 | tf_op jit(solution)/shard_map/ppermute | solution.py:306
  69.4 11.0 %collective-permute-start.8 = (bf16[2,384,128]{2,1,0:T(8,128)(2,1)S(1)}, bf16[2,384,128]{2,1,0:T(8,128)(2,1)S(1)}, u32[]{:S(2)}, u32[]{:S(2)}) collective-permute-start(bf16[2,384,128]{2,1,0:T(8,128)(2,1)S(1)} %get-tuple-element.31), channel_id=1, source_target_pairs={{0,16},{16,0},{1,17},{17,1},{2,18},{18,2},{3,19},{19,3},{4,20},{20... | collective-permute-start | bytes 589832 | tf_op jit(solution)/shard_map/ppermute | solution.py:355
  75.3 8.4 %collective-permute-start.7 = (bf16[384,256]{1,0:T(8,128)(2,1)S(1)}, bf16[384,256]{1,0:T(8,128)(2,1)S(1)}, u32[]{:S(2)}, u32[]{:S(2)}) collective-permute-start(bf16[384,256]{1,0:T(8,128)(2,1)S(1)} %get-tuple-element.29), channel_id=1, source_target_pairs={{192,0},{384,192},{576,384},{193,1},{385,193},{577,385},{194,2},{3... | collective-permute-start | bytes 589832 | tf_op jit(solution)/shard_map/ppermute | solution.py:347
  76.6 9.9 %collective-permute-start.10 = (bf16[384,256]{1,0:T(8,128)(2,1)S(1)}, bf16[384,256]{1,0:T(8,128)(2,1)S(1)}, u32[]{:S(2)}, u32[]{:S(2)}) collective-permute-start(bf16[384,256]{1,0:T(8,128)(2,1)S(1)} %get-tuple-element.36), channel_id=1, source_target_pairs={{384,0},{576,192},{385,1},{577,193},{386,2},{578,194},{387,3},{579... | collective-permute-start | bytes 589832 | tf_op jit(solution)/shard_map/ppermute | solution.py:346
  77.9 5.8 %collective-permute-start.11 = (bf16[64,256]{1,0:T(8,128)(2,1)S(1)}, bf16[64,256]{1,0:T(8,128)(2,1)S(1)}, u32[]{:S(2)}, u32[]{:S(2)}) collective-permute-start(bf16[64,256]{1,0:T(8,128)(2,1)S(1)} %get-tuple-element.37), channel_id=1, source_target_pairs={{592,176},{593,177},{594,178},{595,179},{596,180},{597,181},{598,1... | collective-permute-start | bytes 98312 | tf_op jit(solution)/shard_map/ppermute | solution.py:348
  78.6 0.7 copy-start.3
  87.3 17.3 %all-to-all-start.2 = ((bf16[12,64,128]{2,1,0:T(8,128)(2,1)}), bf16[12,64,128]{2,1,0:T(8,128)(2,1)S(1)}, u32[]{:S(2)}, u32[]{:S(2)}) async-start(bf16[12,64,128]{2,1,0:T(8,128)(2,1)} %plane_sum.1), calls=%async_computation.2 | async-start | bytes 393216 | tf_op jit(solution)/shard_map/all_to_all | solution.py:371
  93.7 6.0 %collective-permute-start.12 = (bf16[384,128]{1,0:T(8,128)(2,1)S(1)}, bf16[384,128]{1,0:T(8,128)(2,1)S(1)}, u32[]{:S(2)}, u32[]{:S(2)}) collective-permute-start(bf16[384,128]{1,0:T(8,128)(2,1)S(1)} %get-tuple-element.39), channel_id=1, source_target_pairs={{0,1},{1,0},{2,3},{3,2},{4,5},{5,4},{6,7},{7,6},{8,9},{9,8},{10,11... | collective-permute-start | bytes 294920 | tf_op jit(solution)/shard_map/ppermute | solution.py:357

commit v8 on v7

--- a/solution.py
+++ b/solution.py
@@ -205,7 +205,16 @@
             out[2 * block + half] = total[:, half * HD : (half + 1) * HD].astype(BF16)
 
 
-def block_kernel(parts, key_grad, value_grad):
+def pool_kernel(keep, arrived, mine, other):
+    p = lax.axis_index("yl")
+    mine[...] = keep[p] + arrived[p].astype(F32)
+    other[...] = (keep[1 - p] + arrived[1 - p].astype(F32)).astype(BF16)
+
+
+def final_kernel(parts, mine, arrived, query_grad, key_grad, value_grad):
+    for h in range(OWN):
+        rows = slice(h * HD, (h + 1) * HD)
+        query_grad[:, rows] = (mine[rows, :] + arrived[rows, :].astype(F32)).T.astype(BF16)
     halves = []
     for half in range(2):
         total = parts[half].astype(F32)
@@ -217,18 +226,6 @@
     value_grad[...] = total[HD // 2 :, :].astype(BF16)
 
 
-def pool_kernel(keep, arrived, mine, other):
-    p = lax.axis_index("yl")
-    mine[...] = keep[p] + arrived[p].astype(F32)
-    other[...] = (keep[1 - p] + arrived[1 - p].astype(F32)).astype(BF16)
-
-
-def query_kernel(mine, arrived, query_grad):
-    for h in range(OWN):
-        rows = slice(h * HD, (h + 1) * HD)
-        query_grad[:, rows] = (mine[rows, :] + arrived[rows, :].astype(F32)).T.astype(BF16)
-
-
 def choice(ids, expert, second):
     first_hit, other_hit = ids[0:1, :] == expert, ids[1:2, :] == expert
     hit = jnp.where(first_hit | other_hit, 1.0, 0.0)
@@ -241,12 +238,18 @@
 
 
 def select_kernel(mine, ids, out):
+    expert = lax.broadcasted_iota(jnp.int32, (16, ROWS), 0)
+    hit = jnp.where((ids[0:1, :] == expert) | (ids[1:2, :] == expert), 1.0, 0.0)
+    earlier = lax.broadcasted_iota(jnp.int32, (ROWS, ROWS), 0) < lax.broadcasted_iota(jnp.int32, (ROWS, ROWS), 1)
+    rank = dot_nn(hit.astype(BF16), jnp.where(earlier, 1.0, 0.0).astype(BF16)).astype(jnp.int32)
+    rank = jnp.where(hit > 0.0, rank, -1)
+    slot = lax.broadcasted_iota(jnp.int32, (2 * SLOTS, ROWS), 0)
+    chosen = [jnp.where(slot == rank[e : e + 1, :], 1.0, 0.0).astype(BF16) for e in range(8)]
+    routed = dot_nn(jnp.concatenate(chosen, axis=0), mine[...]).astype(BF16)
     for high in range(2):
-        for pair in range(4):
-            for second in range(2):
-                chosen, _, _ = choice(ids, high * 4 + pair, second)
-                chosen = jnp.where(chosen, 1.0, 0.0).astype(BF16)
-                out[2 * pair + second, high] = dot_nn(chosen, mine[...]).astype(BF16)
+        for y in range(8):
+            at = (high * 8 + y) * SLOTS
+            out[y, high] = routed[at : at + SLOTS, :]
 
 
 def combine_kernel(rows, rows_other, ids, gates, stored, gate_grad, expert_grad):
@@ -346,15 +349,8 @@
     back2 = lax.ppermute(d2, "x", [(i + 2, i) for i in range(X - 2)])
     back1 = lax.ppermute(d1, "x", [(i + 1, i) for i in range(X - 1)])
     backx = lax.ppermute(dx, ("x", "z", "c"), [(b, a) for a, b in lone])
-    dq_mine, dq_other = call(
-        pool_kernel,
-        (jax.ShapeDtypeStruct((OWN * HD, ROWS), F32), jax.ShapeDtypeStruct((OWN * HD, ROWS), BF16)),
-        [],
-        name="query_pool",
-        nbytes=1,
-    )(dq_keep, lax.ppermute(dq_send, "c", [(0, 1), (1, 0)]))
-    back1, dq_other = lax.optimization_barrier((back1, dq_other))
-    dq_other = lax.ppermute(dq_other, "yl", [(0, 1), (1, 0)])
+    dq_arrived = lax.ppermute(dq_send, "c", [(0, 1), (1, 0)])
+    back1, back2, dq_arrived = lax.optimization_barrier((back1, back2, dq_arrived))
     gate_grad, expert_grad = call(
         combine_kernel,
         (
@@ -365,21 +361,28 @@
         name="combine_grads",
     )(rows, rows_other, ids, gate_weights.T, expert_out[0])
     back1, _ = lax.optimization_barrier((back1, expert_grad))
+    dq_mine, dq_other = call(
+        pool_kernel,
+        (jax.ShapeDtypeStruct((OWN * HD, ROWS), F32), jax.ShapeDtypeStruct((OWN * HD, ROWS), BF16)),
+        [],
+        name="query_pool",
+    )(dq_keep, dq_arrived)
+    dq_other = lax.ppermute(dq_other, "yl", [(0, 1), (1, 0)])
     plane_sums = call(plane_kernel, jax.ShapeDtypeStruct((2 * Z, KB, HD), BF16), [], name="plane_sum")(
         d0, back1, back2, backx
     )
     parts = lax.all_to_all(plane_sums, ("z", "yl"), split_axis=0, concat_axis=0, tiled=True)
 
-    query_grad = call(query_kernel, jax.ShapeDtypeStruct((ROWS, OWN * HD), BF16), [], name="query_sum")(
-        dq_mine, dq_other
-    )
-    parts, query_grad = lax.optimization_barrier((parts, query_grad))
-    key_grad, value_grad = call(
-        block_kernel,
-        (jax.ShapeDtypeStruct((HD // 2, ROWS), BF16), jax.ShapeDtypeStruct((HD // 2, ROWS), BF16)),
+    query_grad, key_grad, value_grad = call(
+        final_kernel,
+        (
+            jax.ShapeDtypeStruct((ROWS, OWN * HD), BF16),
+            jax.ShapeDtypeStruct((HD // 2, ROWS), BF16),
+            jax.ShapeDtypeStruct((HD // 2, ROWS), BF16),
+        ),
         [],
-        name="block_sum",
-    )(parts)
+        name="final_sums",
+    )(parts, dq_mine, dq_other)
     return (query_grad, key_grad.T, value_grad.T, gate_grad, expert_grad[None])
 
 

time: 106 us -> 103 us (0.972)
  waiting for transfers between devices: 18.8 us -> 11.6 us
  starting transfers between devices: 70.6 us -> 77.3 us
  Pallas kernels: 14.2 us -> 11.7 us
    all_to_all x1, starting transfers between devices: 6.36 us -> 13.1 us  [local(): lax.all_to_all(plane_sums, ('z', 'yl'), split_axis=0, concat_axis=0, tile...]
    ppermute x1, waiting for transfers between devices: 3.36 us -> 0.01 us  [local(): back1 = lax.ppermute(d1, 'x', [(i + 1, i) for i in range(X - 1)])]
    ppermute x1, waiting for transfers between devices: 2.8 us -> 0.01 us  [local(): back2 = lax.ppermute(d2, 'x', [(i + 2, i) for i in range(X - 2)])]
    pallas_call x1, Pallas kernels: 3.02 us -> 1.13 us  [local(): call(select_kernel, jax.ShapeDtypeStruct((8, 2, SLOTS, OWN * HD), BF16),...]
  transfers between devices with their start and end apart: 16 -> 16, of which waited for: 8 -> 6; matrix products, arithmetic and copies ran while one was open for 0% -> 0% of each run, Pallas kernels for 10% -> 8%
where the time goes in v8:
time: 103 us; the launch traced here: 102 us
  starting transfers between devices  77.3 us (75%)
  Pallas kernels  11.7 us (11%)
  waiting for transfers between devices  11.6 us (11%)
    all_to_all x1, starting transfers between devices, local(): lax.all_to_all(plane_sums, ('z', 'yl'), split_axis=0, concat_axis=0, tile...  13.1 us
    all_to_all x1, starting transfers between devices, local(): lax.all_to_all(spread, 'z', split_axis=0, concat_axis=0, tiled=True)  12.8 us
    ppermute x1, starting transfers between devices, local(): rows_other = lax.ppermute(away, 'zh', [(0, 1), (1, 0)])  9.95 us
    all_to_all x1, starting transfers between devices, local(): lax.all_to_all(chosen_rows, ('yh', 'yl'), split_axis=0, concat_axis=0, ti...  6.95 us
    ppermute x1, starting transfers between devices, local(): dq_arrived = lax.ppermute(dq_send, 'c', [(0, 1), (1, 0)])  5.97 us
    ppermute x1, starting transfers between devices, local(): ahead2 = lax.ppermute(plane, 'x', [(i, i + 2) for i in range(X - 2)])  4.79 us
    ppermute x1, starting transfers between devices, local(): lax.ppermute(stats, 'c', [(0, 1), (1, 0)])  4.49 us
    pallas_call x1, Pallas kernels, local(): call(grads_kernel, (jax.ShapeDtypeStruct((PLANE, 2 * HD), BF16), jax.Shap...  4.2 us
  transfers between devices with their start and end apart: 16, of which 6 were waited for; matrix products, arithmetic and copies ran while one was open for 0% of the time, Pallas kernels for 8%

profile of v8, /device:TPU:1, one launch (start us, length us, event | category | flops | bytes accessed | tf_op | source)
XLA Modules:
  0.0 102.3 jit_solution(13861550243957285531)
XLA Ops:
  0.6 1.8 %prep.1 = (bf16[128,768]{1,0:T(8,128)(2,1)}, bf16[6,64,256]{2,1,0:T(8,128)(2,1)}, bf16[64,256]{1,0:T(8,128)(2,1)}) custom-call(bf16[128,384]{1,0:T(8,128)(2,1)} %queries.1, bf16[128,384]{1,0:T(8,128)(2,1)} %out_grad.1, bf16[128,1024]{1,0:T(8,128)(2,1)} %key_rows.1, bf16[128,1024]{1,0:T(8,128)(2,1)} %value_rows.1), custom_call_target="tpu_custom_call" | custom-call | bytes 1048576 | tf_op jit(solution)/shard_map/prep/pallas_call | solution.py:284
  2.4 0.0 copy-start.1
  2.4 12.8 %all-to-all-start = ((bf16[6,64,256]{2,1,0:T(8,128)(2,1)}), bf16[6,64,256]{2,1,0:T(8,128)(2,1)S(1)}, u32[]{:S(2)}, u32[]{:S(2)}) async-start(bf16[6,64,256]{2,1,0:T(8,128)(2,1)} %get-tuple-element.27), calls=%async_computation | async-start | bytes 393216 | tf_op jit(solution)/shard_map/all_to_all | solution.py:296
  15.2 3.3 %collective-permute-start = (bf16[128,768]{1,0:T(8,128)(2,1)S(1)}, bf16[128,768]{1,0:T(8,128)(2,1)S(1)}, u32[]{:S(2)}, u32[]{:S(2)}) collective-permute-start(bf16[128,768]{1,0:T(8,128)(2,1)S(1)} %copy-done.1), channel_id=1, source_target_pairs={{0,16},{16,0},{1,17},{17,1},{2,18},{18,2},{3,19},{19,3},{4,20},{20... | collective-permute-start | bytes 589832 | tf_op jit(solution)/shard_map/ppermute | solution.py:297
  18.6 1.0 %collective-permute-done.qd_c = bf16[128,768]{1,0:T(8,128)(2,1)S(1)} collective-permute-done((bf16[128,768]{1,0:T(8,128)(2,1)S(1)}, bf16[128,768]{1,0:T(8,128)(2,1)S(1)}, u32[]{:S(2)}, u32[]{:S(2)}) %collective-permute-start) | collective-permute-done | bytes 196640 | tf_op jit(solution)/shard_map/ppermute | solution.py:297
  19.6 2.9 %collective-permute-start.1 = (bf16[256,768]{1,0:T(8,128)(2,1)S(1)}, bf16[256,768]{1,0:T(8,128)(2,1)S(1)}, u32[]{:S(2)}, u32[]{:S(2)}) collective-permute-start(bf16[256,768]{1,0:T(8,128)(2,1)S(1)} %pad_maximum_fusion), channel_id=1, source_target_pairs={{0,1},{1,0},{2,3},{3,2},{4,5},{5,4},{6,7},{7,6},{8,9},{9,8},{10,11... | collective-permute-start | bytes 1179656 | tf_op jit(solution)/shard_map/ppermute | solution.py:298
  22.5 0.7 collective-permute-start.2
  23.2 3.1 %all-to-all-done = bf16[6,64,256]{2,1,0:T(8,128)(2,1)S(1)} async-done(((bf16[6,64,256]{2,1,0:T(8,128)(2,1)}), bf16[6,64,256]{2,1,0:T(8,128)(2,1)S(1)}, u32[]{:S(2)}, u32[]{:S(2)}) %all-to-all-start) | async-done | bytes 196640 | tf_op jit(solution)/shard_map/all_to_all | solution.py:296
  26.3 4.8 %collective-permute-start.3 = (bf16[384,256]{1,0:T(8,128)(2,1)S(1)}, bf16[384,256]{1,0:T(8,128)(2,1)S(1)}, u32[]{:S(2)}, u32[]{:S(2)}) collective-permute-start(bf16[384,256]{1,0:T(8,128)(2,1)S(1)} %bitcast.11), channel_id=1, source_target_pairs={{0,384},{192,576},{1,385},{193,577},{2,386},{194,578},{3,387},{195... | collective-permute-start | bytes 589832 | tf_op jit(solution)/shard_map/ppermute | solution.py:312
  31.1 2.2 %collective-permute-start.4 = (bf16[384,256]{1,0:T(8,128)(2,1)S(1)}, bf16[384,256]{1,0:T(8,128)(2,1)S(1)}, u32[]{:S(2)}, u32[]{:S(2)}) collective-permute-start(bf16[384,256]{1,0:T(8,128)(2,1)S(1)} %bitcast.12), channel_id=1, source_target_pairs={{0,192},{192,384},{384,576},{1,193},{193,385},{385,577},{2,194},{1... | collective-permute-start | bytes 589832 | tf_op jit(solution)/shard_map/ppermute | solution.py:313
  33.3 1.1 %select_rows.1 = bf16[8,2,32,384]{3,2,1,0:T(8,128)(2,1)} custom-call(bf16[128,384]{1,0:T(8,128)(2,1)S(1)} %copy-done.4, s32[2,128]{1,0:T(2,128)S(1)} %bitcast.15), custom_call_target="tpu_custom_call" | custom-call | flops 2516582400 | bytes 1048576 | tf_op jit(solution)/shard_map/select_rows/pallas_call | solution.py:300
  34.5 7.0 %all-to-all-start.1 = ((bf16[8,2,32,384]{3,2,1,0:T(8,128)(2,1)}), bf16[8,2,32,384]{3,2,1,0:T(8,128)(2,1)S(1)}, u32[]{:S(2)}, u32[]{:S(2)}) async-start(bf16[8,2,32,384]{3,2,1,0:T(8,128)(2,1)} %select_rows.1), calls=%async_computation.1 | async-start | bytes 786432 | tf_op jit(solution)/shard_map/all_to_all | solution.py:307
  41.5 1.9 %softmax_stats.1.mine = f32[32,128]{1,0:T(8,128)S(1)} custom-call(bf16[128,768]{1,0:T(8,128)(2,1)S(1)} %copy-done.1, bf16[128,768]{1,0:T(8,128)(2,1)S(1)} %collective-permute-done.qd_c, bf16[256,768]{1,0:T(8,128)(2,1)S(1)} %collective-permute-done.1.qd_y, bf16[64,256]{1,0:T(8,128)(2,1)S(1)} %collective-permute-done.2.kvx, ...), custom_call_target="tpu_custom_call" | custom-call | flops 10569646080 | bytes 1048576 | tf_op jit(solution)/shard_map/softmax_stats/pallas_call | solution.py:324
  43.4 4.5 %collective-permute-start.5 = (f32[32,128]{1,0:T(8,128)S(1)}, f32[32,128]{1,0:T(8,128)S(1)}, u32[]{:S(2)}, u32[]{:S(2)}) collective-permute-start(f32[32,128]{1,0:T(8,128)S(1)} %softmax_stats.1.mine), channel_id=1, source_target_pairs={{0,16},{16,0},{1,17},{17,1},{2,18},{18,2},{3,19},{19,3},{4,20},{20... | collective-permute-start | bytes 49160 | tf_op jit(solution)/shard_map/ppermute | solution.py:332
  47.9 0.8 collective-permute-done.5.arrived
  48.7 3.6 %collective-permute-start.6 = (f32[32,128]{1,0:T(8,128)S(1)}, f32[32,128]{1,0:T(8,128)S(1)}, u32[]{:S(2)}, u32[]{:S(2)}) collective-permute-start(f32[32,128]{1,0:T(8,128)S(1)} %merge_stats.1.stats), channel_id=1, source_target_pairs={{0,1},{1,0},{2,3},{3,2},{4,5},{5,4},{6,7},{7,6},{8,9},{9,8},{10,11... | collective-permute-start | bytes 49160 | tf_op jit(solution)/shard_map/ppermute | solution.py:334
  52.4 0.9 all-to-all-done.1.rows
  53.3 10.0 %collective-permute-start.10 = (bf16[8,32,384]{2,1,0:T(8,128)(2,1)S(1)}, bf16[8,32,384]{2,1,0:T(8,128)(2,1)S(1)}, u32[]{:S(2)}, u32[]{:S(2)}) collective-permute-start(bf16[8,32,384]{2,1,0:T(8,128)(2,1)S(1)} %dynamic-slice_bitcast_fusion), channel_id=1, source_target_pairs={{0,8},{8,0},{1,9},{9,1},{2,10},{10,2},{3,11},{11,3},{4,12},{12,4},... | collective-permute-start | bytes 589832 | tf_op jit(solution)/shard_map/ppermute | solution.py:309
  63.3 4.2 %score_grads.1 = (bf16[384,256]{1,0:T(8,128)(2,1)S(1)}, bf16[384,256]{1,0:T(8,128)(2,1)S(1)}, f32[384,256]{1,0:T(8,128)S(1)}, bf16[64,256]{1,0:T(8,128)(2,1)S(1)...) custom-call(bf16[128,768]{1,0:T(8,128)(2,1)S(1)} %copy-done.1, ...), custom_call_target="tpu_custom_call" | custom-call | flops 1761607680 | bytes 1048576 | tf_op jit(solution)/shard_map/score_grads/pallas_call | solution.py:335
  67.5 1.3 %collective-permute-start.7 = (bf16[384,256]{1,0:T(8,128)(2,1)S(1)}, bf16[384,256]{1,0:T(8,128)(2,1)S(1)}, u32[]{:S(2)}, u32[]{:S(2)}) collective-permute-start(bf16[384,256]{1,0:T(8,128)(2,1)S(1)} %get-tuple-element.29), channel_id=1, source_target_pairs={{192,0},{384,192},{576,384},{193,1},{385,193},{577,385},{194,2},{3... | collective-permute-start | bytes 589832 | tf_op jit(solution)/shard_map/ppermute | solution.py:350
  68.8 1.3 %collective-permute-start.8 = (bf16[384,256]{1,0:T(8,128)(2,1)S(1)}, bf16[384,256]{1,0:T(8,128)(2,1)S(1)}, u32[]{:S(2)}, u32[]{:S(2)}) collective-permute-start(bf16[384,256]{1,0:T(8,128)(2,1)S(1)} %get-tuple-element.30), channel_id=1, source_target_pairs={{384,0},{576,192},{385,1},{577,193},{386,2},{578,194},{387,3},{579... | collective-permute-start | bytes 589832 | tf_op jit(solution)/shard_map/ppermute | solution.py:349
  70.1 6.0 %collective-permute-start.9 = (bf16[2,384,128]{2,1,0:T(8,128)(2,1)S(1)}, bf16[2,384,128]{2,1,0:T(8,128)(2,1)S(1)}, u32[]{:S(2)}, u32[]{:S(2)}) collective-permute-start(bf16[2,384,128]{2,1,0:T(8,128)(2,1)S(1)} %get-tuple-element.31), channel_id=1, source_target_pairs={{0,16},{16,0},{1,17},{17,1},{2,18},{18,2},{3,19},{19,3},{4,20},{20... | collective-permute-start | bytes 589832 | tf_op jit(solution)/shard_map/ppermute | solution.py:352
  76.1 0.7 collective-permute-start.11
  76.8 0.7 copy-done.3
  77.4 1.0 %combine_grads.1 = (f32[1,32]{1,0:T(1,128)}, bf16[32,6144]{1,0:T(8,128)(2,1)}) custom-call(bf16[8,2,32,384]{3,2,1,0:T(8,128)(2,1)S(1)} %all-to-all-done.1.rows, bf16[8,32,384]{2,1,0:T(8,128)(2,1)S(1)} %collective-permute-done.10.rows_other, s32[2,128]{1,0:T(2,128)S(1)} %bitcast.16, f32[2,128]{1,0:T(2,128)S(1)} %bitcast.17, bf16[32,6144]{1,0:T(8,128)(2,1)S(1)} %bitcast.10), custom_call_target="tpu_custom_call" | custom-call | bytes 1048576 | tf_op jit(solution)/shard_map/combine_grads/pallas_call | solution.py:354
  78.5 0.7 plane_sum.1
  79.2 13.1 %all-to-all-start.2 = ((bf16[12,64,128]{2,1,0:T(8,128)(2,1)}), bf16[12,64,128]{2,1,0:T(8,128)(2,1)S(1)}, u32[]{:S(2)}, u32[]{:S(2)}) async-start(bf16[12,64,128]{2,1,0:T(8,128)(2,1)} %plane_sum.1), calls=%async_computation.2 | async-start | bytes 393216 | tf_op jit(solution)/shard_map/all_to_all | solution.py:374
  92.4 0.1 query_pool.1
  92.4 3.3 %collective-permute-start.12 = (bf16[384,128]{1,0:T(8,128)(2,1)S(1)}, bf16[384,128]{1,0:T(8,128)(2,1)S(1)}, u32[]{:S(2)}, u32[]{:S(2)}) collective-permute-start(bf16[384,128]{1,0:T(8,128)(2,1)S(1)} %get-tuple-element.40), channel_id=1, source_target_pairs={{0,1},{1,0},{2,3},{3,2},{4,5},{5,4},{6,7},{7,6},{8,9},{9,8},{10,11... | collective-permute-start | bytes 294920 | tf_op jit(solution)/shard_map/ppermute | solution.py:370
  95.7 2.2 %collective-permute-done.12.arrived = bf16[384,128]{1,0:T(8,128)(2,1)S(1)} collective-permute-done((bf16[384,128]{1,0:T(8,128)(2,1)S(1)}, bf16[384,128]{1,0:T(8,128)(2,1)S(1)}, u32[]{:S(2)}, u32[]{:S(2)}) %collective-permute-start.12) | collective-permute-done | bytes 98336 | tf_op jit(solution)/shard_map/ppermute | solution.py:370
  97.9 3.6 %all-to-all-done.2.parts = bf16[12,64,128]{2,1,0:T(8,128)(2,1)S(1)} async-done(((bf16[12,64,128]{2,1,0:T(8,128)(2,1)}), bf16[12,64,128]{2,1,0:T(8,128)(2,1)S(1)}, u32[]{:S(2)}, u32[]{:S(2)}) %all-to-all-start.2) | async-done | bytes 196640 | tf_op jit(solution)/shard_map/all_to_all | solution.py:374
  101.5 0.8 final_sums.1
  (27 shorter events, 0.1 us)
Async XLA Ops:
  2.4 12.8 %copy-start.1 = (bf16[128,768]{1,0:T(8,128)(2,1)S(1)}, bf16[128,768]{1,0:T(8,128)(2,1)}, u32[]{:S(2)}) copy-start(bf16[128,768]{1,0:T(8,128)(2,1)} %get-tuple-element.25.qd) | copy-start | bytes 589828
  2.4 23.9 %all-to-all-start = ((bf16[6,64,256]{2,1,0:T(8,128)(2,1)}), bf16[6,64,256]{2,1,0:T(8,128)(2,1)S(1)}, u32[]{:S(2)}, u32[]{:S(2)}) async-start(bf16[6,64,256]{2,1,0:T(8,128)(2,1)} %get-tuple-element.27), calls=%async_computation | async-start | bytes 393216 | tf_op jit(solution)/shard_map/all_to_all | solution.py:296
  15.2 7.3 %copy-start.7 = (bf16[64,256]{1,0:T(8,128)(2,1)S(1)}, bf16[64,256]{1,0:T(8,128)(2,1)}, u32[]{:S(2)}) copy-start(bf16[64,256]{1,0:T(8,128)(2,1)} %get-tuple-element.26) | copy-start | bytes 98308
  15.2 18.1 %copy-start.4 = (bf16[128,384]{1,0:T(8,128)(2,1)S(1)}, bf16[128,384]{1,0:T(8,128)(2,1)}, u32[]{:S(2)}) copy-start(bf16[128,384]{1,0:T(8,128)(2,1)} %mine.1) | copy-start | bytes 294916
  15.2 4.4 %collective-permute-start = (bf16[128,768]{1,0:T(8,128)(2,1)S(1)}, bf16[128,768]{1,0:T(8,128)(2,1)S(1)}, u32[]{:S(2)}, u32[]{:S(2)}) collective-permute-start(bf16[128,768]{1,0:T(8,128)(2,1)S(1)} %copy-done.1), channel_id=1, source_target_pairs={{0,16},{16,0},{1,17},{17,1},{2,18},{18,2},{3,19},{19,3},{4,20},{20... | collective-permute-start | bytes 589832 | tf_op jit(solution)/shard_map/ppermute | solution.py:297
  19.6 21.8 %collective-permute-start.1 = (bf16[256,768]{1,0:T(8,128)(2,1)S(1)}, bf16[256,768]{1,0:T(8,128)(2,1)S(1)}, u32[]{:S(2)}, u32[]{:S(2)}) collective-permute-start(bf16[256,768]{1,0:T(8,128)(2,1)S(1)} %pad_maximum_fusion), channel_id=1, source_target_pairs={{0,1},{1,0},{2,3},{3,2},{4,5},{5,4},{6,7},{7,6},{8,9},{9,8},{10,11... | collective-permute-start | bytes 1179656 | tf_op jit(solution)/shard_map/ppermute | solution.py:298
  22.5 18.9 %collective-permute-start.2 = (bf16[64,256]{1,0:T(8,128)(2,1)S(1)}, bf16[64,256]{1,0:T(8,128)(2,1)S(1)}, u32[]{:S(2)}, u32[]{:S(2)}) collective-permute-start(bf16[64,256]{1,0:T(8,128)(2,1)S(1)} %copy-done.7), channel_id=1, source_target_pairs={{176,592},{177,593},{178,594},{179,595},{180,596},{181,597},{182,5... | collective-permute-start | bytes 98312 | tf_op jit(solution)/shard_map/ppermute | solution.py:314
  26.3 7.0 %copy-start.2 = (s32[128,2]{0,1:T(2,128)S(1)}, s32[128,2]{0,1:T(2,128)}, u32[]{:S(2)}) copy-start(s32[128,2]{0,1:T(2,128)} %param.18) | copy-start | bytes 3076
  26.3 15.2 %collective-permute-start.3 = (bf16[384,256]{1,0:T(8,128)(2,1)S(1)}, bf16[384,256]{1,0:T(8,128)(2,1)S(1)}, u32[]{:S(2)}, u32[]{:S(2)}) collective-permute-start(bf16[384,256]{1,0:T(8,128)(2,1)S(1)} %bitcast.11), channel_id=1, source_target_pairs={{0,384},{192,576},{1,385},{193,577},{2,386},{194,578},{3,387},{195... | collective-permute-start | bytes 589832 | tf_op jit(solution)/shard_map/ppermute | solution.py:312
  31.1 10.4 %collective-permute-start.4 = (bf16[384,256]{1,0:T(8,128)(2,1)S(1)}, bf16[384,256]{1,0:T(8,128)(2,1)S(1)}, u32[]{:S(2)}, u32[]{:S(2)}) collective-permute-start(bf16[384,256]{1,0:T(8,128)(2,1)S(1)} %bitcast.12), channel_id=1, source_target_pairs={{0,192},{192,384},{384,576},{1,193},{193,385},{385,577},{2,194},{1... | collective-permute-start | bytes 589832 | tf_op jit(solution)/shard_map/ppermute | solution.py:313
  34.5 7.0 %copy-start.5 = (bf16[128,384]{1,0:T(8,128)(2,1)S(1)}, bf16[128,384]{1,0:T(8,128)(2,1)}, u32[]{:S(2)}) copy-start(bf16[128,384]{1,0:T(8,128)(2,1)} %o_own.1) | copy-start | bytes 294916
  34.5 7.0 %copy-start.6 = (s32[6144]{0:T(1024)S(1)}, s32[6144]{0:T(1024)}, u32[]{:S(2)}) copy-start(s32[6144]{0:T(1024)} %param.15) | copy-start | bytes 73732
  34.5 18.8 %all-to-all-start.1 = ((bf16[8,2,32,384]{3,2,1,0:T(8,128)(2,1)}), bf16[8,2,32,384]{3,2,1,0:T(8,128)(2,1)S(1)}, u32[]{:S(2)}, u32[]{:S(2)}) async-start(bf16[8,2,32,384]{3,2,1,0:T(8,128)(2,1)} %select_rows.1), calls=%async_computation.1 | async-start | bytes 786432 | tf_op jit(solution)/shard_map/all_to_all | solution.py:307
  43.4 5.3 %collective-permute-start.5 = (f32[32,128]{1,0:T(8,128)S(1)}, f32[32,128]{1,0:T(8,128)S(1)}, u32[]{:S(2)}, u32[]{:S(2)}) collective-permute-start(f32[32,128]{1,0:T(8,128)S(1)} %softmax_stats.1.mine), channel_id=1, source_target_pairs={{0,16},{16,0},{1,17},{17,1},{2,18},{18,2},{3,19},{19,3},{4,20},{20... | collective-permute-start | bytes 49160 | tf_op jit(solution)/shard_map/ppermute | solution.py:332
  48.7 14.5 %collective-permute-start.6 = (f32[32,128]{1,0:T(8,128)S(1)}, f32[32,128]{1,0:T(8,128)S(1)}, u32[]{:S(2)}, u32[]{:S(2)}) collective-permute-start(f32[32,128]{1,0:T(8,128)S(1)} %merge_stats.1.stats), channel_id=1, source_target_pairs={{0,1},{1,0},{2,3},{3,2},{4,5},{5,4},{6,7},{7,6},{8,9},{9,8},{10,11... | collective-permute-start | bytes 49160 | tf_op jit(solution)/shard_map/ppermute | solution.py:334
  53.3 23.5 %copy-start = (bf16[1,32,6144]{2,1,0:T(8,128)(2,1)S(1)}, bf16[1,32,6144]{2,1,0:T(8,128)(2,1)}, u32[]{:S(2)}) copy-start(bf16[1,32,6144]{2,1,0:T(8,128)(2,1)} %param.19) | copy-start | bytes 1179652
  53.3 23.4 %collective-permute-start.10 = (bf16[8,32,384]{2,1,0:T(8,128)(2,1)S(1)}, bf16[8,32,384]{2,1,0:T(8,128)(2,1)S(1)}, u32[]{:S(2)}, u32[]{:S(2)}) collective-permute-start(bf16[8,32,384]{2,1,0:T(8,128)(2,1)S(1)} %dynamic-slice_bitcast_fusion), channel_id=1, source_target_pairs={{0,8},{8,0},{1,9},{9,1},{2,10},{10,2},{3,11},{11,3},{4,12},{12,4},... | collective-permute-start | bytes 589832 | tf_op jit(solution)/shard_map/ppermute | solution.py:309
  67.5 11.0 %collective-permute-start.7 = (bf16[384,256]{1,0:T(8,128)(2,1)S(1)}, bf16[384,256]{1,0:T(8,128)(2,1)S(1)}, u32[]{:S(2)}, u32[]{:S(2)}) collective-permute-start(bf16[384,256]{1,0:T(8,128)(2,1)S(1)} %get-tuple-element.29), channel_id=1, source_target_pairs={{192,0},{384,192},{576,384},{193,1},{385,193},{577,385},{194,2},{3... | collective-permute-start | bytes 589832 | tf_op jit(solution)/shard_map/ppermute | solution.py:350
  68.8 9.7 %collective-permute-start.8 = (bf16[384,256]{1,0:T(8,128)(2,1)S(1)}, bf16[384,256]{1,0:T(8,128)(2,1)S(1)}, u32[]{:S(2)}, u32[]{:S(2)}) collective-permute-start(bf16[384,256]{1,0:T(8,128)(2,1)S(1)} %get-tuple-element.30), channel_id=1, source_target_pairs={{384,0},{576,192},{385,1},{577,193},{386,2},{578,194},{387,3},{579... | collective-permute-start | bytes 589832 | tf_op jit(solution)/shard_map/ppermute | solution.py:349
  70.1 8.4 %collective-permute-start.9 = (bf16[2,384,128]{2,1,0:T(8,128)(2,1)S(1)}, bf16[2,384,128]{2,1,0:T(8,128)(2,1)S(1)}, u32[]{:S(2)}, u32[]{:S(2)}) collective-permute-start(bf16[2,384,128]{2,1,0:T(8,128)(2,1)S(1)} %get-tuple-element.31), channel_id=1, source_target_pairs={{0,16},{16,0},{1,17},{17,1},{2,18},{18,2},{3,19},{19,3},{4,20},{20... | collective-permute-start | bytes 589832 | tf_op jit(solution)/shard_map/ppermute | solution.py:352
  76.1 2.4 %collective-permute-start.11 = (bf16[64,256]{1,0:T(8,128)(2,1)S(1)}, bf16[64,256]{1,0:T(8,128)(2,1)S(1)}, u32[]{:S(2)}, u32[]{:S(2)}) collective-permute-start(bf16[64,256]{1,0:T(8,128)(2,1)S(1)} %get-tuple-element.36), channel_id=1, source_target_pairs={{592,176},{593,177},{594,178},{595,179},{596,180},{597,181},{598,1... | collective-permute-start | bytes 98312 | tf_op jit(solution)/shard_map/ppermute | solution.py:351
  76.7 0.7 copy-start.3
  79.2 22.3 %all-to-all-start.2 = ((bf16[12,64,128]{2,1,0:T(8,128)(2,1)}), bf16[12,64,128]{2,1,0:T(8,128)(2,1)S(1)}, u32[]{:S(2)}, u32[]{:S(2)}) async-start(bf16[12,64,128]{2,1,0:T(8,128)(2,1)} %plane_sum.1), calls=%async_computation.2 | async-start | bytes 393216 | tf_op jit(solution)/shard_map/all_to_all | solution.py:374
  92.4 5.5 %collective-permute-start.12 = (bf16[384,128]{1,0:T(8,128)(2,1)S(1)}, bf16[384,128]{1,0:T(8,128)(2,1)S(1)}, u32[]{:S(2)}, u32[]{:S(2)}) collective-permute-start(bf16[384,128]{1,0:T(8,128)(2,1)S(1)} %get-tuple-element.40), channel_id=1, source_target_pairs={{0,1},{1,0},{2,3},{3,2},{4,5},{5,4},{6,7},{7,6},{8,9},{9,8},{10,11... | collective-permute-start | bytes 294920 | tf_op jit(solution)/shard_map/ppermute | solution.py:370

commit v9 on v8

--- a/solution.py
+++ b/solution.py
@@ -148,7 +148,7 @@
 
 
 def grads_kernel(
-    qd, qd_c, qd_y, kvx, kv2, kv1, kv0, doc, stats, stats_y, d2, d1, d0, dx, dq_keep, dq_send, q_s, do_s, kv_s, acc_s
+    qd, qd_c, qd_y, kvx, kv2, kv1, kv0, doc, stats, stats_y, d2, d1, d0, dx, dq_keep, dq_send, q_s, do_s, kv_s, acc_s, dq_s
 ):
     x, z, c, p = (lax.axis_index(a) for a in ("x", "z", "c", "yl"))
     chip = x * Z + z
@@ -176,11 +176,11 @@
         score = (probs * (dot_nt(values, do) - delta)).astype(BF16)
         dv = dv + dot_nn(probs.astype(BF16), do)
         dk = dk + dot_nn(score, q)
-        part = dot_nn(keys_t, score) * SCALE
-        lower, upper = part[:, 0:ROWS], part[:, ROWS : 2 * ROWS]
-        rows = slice((h % OWN) * HD, (h % OWN + 1) * HD)
-        dq_keep[owner, rows, :] = jnp.where(c == 0, lower, upper)
-        dq_send[owner, rows, :] = jnp.where(c == 0, upper, lower).astype(BF16)
+        dq_s[h] = dot_nn(keys_t, score) * SCALE
+    for h in range(OWN):
+        rows = slice(h * HD, (h + 1) * HD)
+        dq_keep[rows, :] = dq_s[p * OWN + h]
+        dq_send[rows, :] = dq_s[(1 - p) * OWN + h].astype(BF16)
     acc_s[pl.ds(at, SPAN), 0:HD] = dk * SCALE
     acc_s[pl.ds(at, SPAN), HD : 2 * HD] = dv
     for ref, start, size in (
@@ -206,9 +206,10 @@
 
 
 def pool_kernel(keep, arrived, mine, other):
-    p = lax.axis_index("yl")
-    mine[...] = keep[p] + arrived[p].astype(F32)
-    other[...] = (keep[1 - p] + arrived[1 - p].astype(F32)).astype(BF16)
+    lower = lax.axis_index("c") == 0
+    total = keep[...] + arrived[...].astype(F32)
+    mine[...] = jnp.where(lower, total[:, 0:ROWS], total[:, ROWS : 2 * ROWS])
+    other[...] = jnp.where(lower, total[:, ROWS : 2 * ROWS], total[:, 0:ROWS]).astype(BF16)
 
 
 def final_kernel(parts, mine, arrived, query_grad, key_grad, value_grad):
@@ -237,7 +238,9 @@
     return (slot == rank) & (hit > 0.0), first_hit, other_hit
 
 
-def select_kernel(mine, ids, out):
+def select_kernel(mine, ids, gates, out, ids_on, gates_on):
+    ids_on[...] = ids[...]
+    gates_on[...] = gates[...]
     expert = lax.broadcasted_iota(jnp.int32, (16, ROWS), 0)
     hit = jnp.where((ids[0:1, :] == expert) | (ids[1:2, :] == expert), 1.0, 0.0)
     earlier = lax.broadcasted_iota(jnp.int32, (ROWS, ROWS), 0) < lax.broadcasted_iota(jnp.int32, (ROWS, ROWS), 1)
@@ -297,13 +300,17 @@
     pool_c = lax.ppermute(pool, "c", [(0, 1), (1, 0)])
     pool_y = lax.ppermute(jnp.concatenate([pool, pool_c], axis=0), "yl", [(0, 1), (1, 0)])
     ids = expert_ids.T
-    chosen_rows = call(
+    chosen_rows, ids, gates = call(
         select_kernel,
-        jax.ShapeDtypeStruct((8, 2, SLOTS, OWN * HD), BF16),
+        (
+            jax.ShapeDtypeStruct((8, 2, SLOTS, OWN * HD), BF16),
+            jax.ShapeDtypeStruct((2, ROWS), jnp.int32),
+            jax.ShapeDtypeStruct((2, ROWS), F32),
+        ),
         [],
         flops=100 * 256 * ROWS * 2 * OWN * HD,
         name="select_rows",
-    )(row_grad, ids)
+    )(row_grad, ids, gate_weights.T)
     rows = lax.all_to_all(chosen_rows, ("yh", "yl"), split_axis=0, concat_axis=0, tiled=True)
     away = lax.dynamic_index_in_dim(rows, 1 - lax.axis_index("zh"), 1, keepdims=False)
     rows_other = lax.ppermute(away, "zh", [(0, 1), (1, 0)])
@@ -339,17 +346,17 @@
             jax.ShapeDtypeStruct((PLANE, 2 * HD), BF16),
             jax.ShapeDtypeStruct((PLANE, 2 * HD), F32),
             jax.ShapeDtypeStruct((KB, 2 * HD), BF16),
-            jax.ShapeDtypeStruct((2, OWN * HD, ROWS), F32),
-            jax.ShapeDtypeStruct((2, OWN * HD, ROWS), BF16),
+            jax.ShapeDtypeStruct((OWN * HD, 2 * ROWS), F32),
+            jax.ShapeDtypeStruct((OWN * HD, 2 * ROWS), BF16),
         ),
-        pool_scratch + [pltpu.VMEM((PLACES, 2 * HD), F32)],
+        pool_scratch + [pltpu.VMEM((PLACES, 2 * HD), F32), pltpu.VMEM((HEADS, HD, 2 * ROWS), F32)],
         flops=10 * HD * pairs,
         name="score_grads",
     )(*shared, doc, stats, stats_y)
     back2 = lax.ppermute(d2, "x", [(i + 2, i) for i in range(X - 2)])
     back1 = lax.ppermute(d1, "x", [(i + 1, i) for i in range(X - 1)])
     backx = lax.ppermute(dx, ("x", "z", "c"), [(b, a) for a, b in lone])
-    dq_arrived = lax.ppermute(dq_send, "c", [(0, 1), (1, 0)])
+    dq_arrived = lax.ppermute(dq_send, "yl", [(0, 1), (1, 0)])
     back1, back2, dq_arrived = lax.optimization_barrier((back1, back2, dq_arrived))
     gate_grad, expert_grad = call(
         combine_kernel,
@@ -359,7 +366,7 @@
         ),
         [],
         name="combine_grads",
-    )(rows, rows_other, ids, gate_weights.T, expert_out[0])
+    )(rows, rows_other, ids, gates, expert_out[0])
     back1, _ = lax.optimization_barrier((back1, expert_grad))
     dq_mine, dq_other = call(
         pool_kernel,
@@ -367,7 +374,7 @@
         [],
         name="query_pool",
     )(dq_keep, dq_arrived)
-    dq_other = lax.ppermute(dq_other, "yl", [(0, 1), (1, 0)])
+    dq_other = lax.ppermute(dq_other, "c", [(0, 1), (1, 0)])
     plane_sums = call(plane_kernel, jax.ShapeDtypeStruct((2 * Z, KB, HD), BF16), [], name="plane_sum")(
         d0, back1, back2, backx
     )

time: 103 us -> 101 us (0.981)
  starting transfers between devices: 77.3 us -> 70.6 us
  waiting for transfers between devices: 11.6 us -> 16.3 us
    ppermute x2, starting transfers between devices: 9.29 us -> 3.84 us  [the longest x1 1.92 us: local(): dq_arrived = lax.ppermute(dq_send, 'yl', [(0, 1), (1, 0)])]
    ppermute x1, waiting for transfers between devices: 0.01 us -> 2.8 us  [local(): back2 = lax.ppermute(d2, 'x', [(i + 2, i) for i in range(X - 2)])]
    all_to_all x1, waiting for transfers between devices: 3.57 us -> 5.91 us  [local(): lax.all_to_all(plane_sums, ('z', 'yl'), split_axis=0, concat_axis=0, tile...]
    all_to_all x1, starting transfers between devices: 13.1 us -> 11.9 us  [local(): lax.all_to_all(plane_sums, ('z', 'yl'), split_axis=0, concat_axis=0, tile...]
  transfers between devices with their start and end apart: 16 -> 16, of which waited for: 6 -> 8; matrix products, arithmetic and copies ran while one was open for 0% -> 0% of each run, Pallas kernels for 8% -> 8%
where the time goes in v9:
time: 101 us; the launch traced here: 100 us
  starting transfers between devices  70.6 us (70%)
  waiting for transfers between devices  16.3 us (16%)
  Pallas kernels  11.7 us (12%)
    all_to_all x1, starting transfers between devices, local(): lax.all_to_all(spread, 'z', split_axis=0, concat_axis=0, tiled=True)  12.8 us
    all_to_all x1, starting transfers between devices, local(): lax.all_to_all(plane_sums, ('z', 'yl'), split_axis=0, concat_axis=0, tile...  11.9 us
    ppermute x1, starting transfers between devices, local(): rows_other = lax.ppermute(away, 'zh', [(0, 1), (1, 0)])  9.95 us
    all_to_all x1, starting transfers between devices, local(): lax.all_to_all(chosen_rows, ('yh', 'yl'), split_axis=0, concat_axis=0, ti...  6.95 us
    all_to_all x1, waiting for transfers between devices, local(): lax.all_to_all(plane_sums, ('z', 'yl'), split_axis=0, concat_axis=0, tile...  5.91 us
    ppermute x1, starting transfers between devices, local(): ahead2 = lax.ppermute(plane, 'x', [(i, i + 2) for i in range(X - 2)])  4.66 us
    ppermute x1, starting transfers between devices, local(): lax.ppermute(stats, 'c', [(0, 1), (1, 0)])  4.48 us
    pallas_call x1, Pallas kernels, local(): call(grads_kernel, (jax.ShapeDtypeStruct((PLANE, 2 * HD), BF16), jax.Shap...  4.28 us
  transfers between devices with their start and end apart: 16, of which 8 were waited for; matrix products, arithmetic and copies ran while one was open for 0% of the time, Pallas kernels for 8%

profile of v9, /device:TPU:1, one launch (start us, length us, event | category | flops | bytes accessed | tf_op | source)
XLA Modules:
  0.0 100.2 jit_solution(12993725917292430259)
XLA Ops:
  0.6 1.8 %prep.1 = (bf16[128,768]{1,0:T(8,128)(2,1)}, bf16[6,64,256]{2,1,0:T(8,128)(2,1)}, bf16[64,256]{1,0:T(8,128)(2,1)}) custom-call(bf16[128,384]{1,0:T(8,128)(2,1)} %queries.1, bf16[128,384]{1,0:T(8,128)(2,1)} %out_grad.1, bf16[128,1024]{1,0:T(8,128)(2,1)} %key_rows.1, bf16[128,1024]{1,0:T(8,128)(2,1)} %value_rows.1), custom_call_target="tpu_custom_call" | custom-call | bytes 1048576 | tf_op jit(solution)/shard_map/prep/pallas_call | solution.py:287
  2.4 12.8 %all-to-all-start = ((bf16[6,64,256]{2,1,0:T(8,128)(2,1)}), bf16[6,64,256]{2,1,0:T(8,128)(2,1)S(1)}, u32[]{:S(2)}, u32[]{:S(2)}) async-start(bf16[6,64,256]{2,1,0:T(8,128)(2,1)} %get-tuple-element.30), calls=%async_computation | async-start | bytes 393216 | tf_op jit(solution)/shard_map/all_to_all | solution.py:299
  15.2 3.3 %collective-permute-start = (bf16[128,768]{1,0:T(8,128)(2,1)S(1)}, bf16[128,768]{1,0:T(8,128)(2,1)S(1)}, u32[]{:S(2)}, u32[]{:S(2)}) collective-permute-start(bf16[128,768]{1,0:T(8,128)(2,1)S(1)} %copy-done.1), channel_id=1, source_target_pairs={{0,16},{16,0},{1,17},{17,1},{2,18},{18,2},{3,19},{19,3},{4,20},{20... | collective-permute-start | bytes 589832 | tf_op jit(solution)/shard_map/ppermute | solution.py:300
  18.6 1.0 %collective-permute-done.qd_c = bf16[128,768]{1,0:T(8,128)(2,1)S(1)} collective-permute-done((bf16[128,768]{1,0:T(8,128)(2,1)S(1)}, bf16[128,768]{1,0:T(8,128)(2,1)S(1)}, u32[]{:S(2)}, u32[]{:S(2)}) %collective-permute-start) | collective-permute-done | bytes 196640 | tf_op jit(solution)/shard_map/ppermute | solution.py:300
  19.6 2.9 %collective-permute-start.1 = (bf16[256,768]{1,0:T(8,128)(2,1)S(1)}, bf16[256,768]{1,0:T(8,128)(2,1)S(1)}, u32[]{:S(2)}, u32[]{:S(2)}) collective-permute-start(bf16[256,768]{1,0:T(8,128)(2,1)S(1)} %pad_maximum_fusion), channel_id=1, source_target_pairs={{0,1},{1,0},{2,3},{3,2},{4,5},{5,4},{6,7},{7,6},{8,9},{9,8},{10,11... | collective-permute-start | bytes 1179656 | tf_op jit(solution)/shard_map/ppermute | solution.py:301
  22.5 0.7 collective-permute-start.2
  23.2 3.1 %all-to-all-done = bf16[6,64,256]{2,1,0:T(8,128)(2,1)S(1)} async-done(((bf16[6,64,256]{2,1,0:T(8,128)(2,1)}), bf16[6,64,256]{2,1,0:T(8,128)(2,1)S(1)}, u32[]{:S(2)}, u32[]{:S(2)}) %all-to-all-start) | async-done | bytes 196640 | tf_op jit(solution)/shard_map/all_to_all | solution.py:299
  26.3 4.7 %collective-permute-start.3 = (bf16[384,256]{1,0:T(8,128)(2,1)S(1)}, bf16[384,256]{1,0:T(8,128)(2,1)S(1)}, u32[]{:S(2)}, u32[]{:S(2)}) collective-permute-start(bf16[384,256]{1,0:T(8,128)(2,1)S(1)} %bitcast.11), channel_id=1, source_target_pairs={{0,384},{192,576},{1,385},{193,577},{2,386},{194,578},{3,387},{195... | collective-permute-start | bytes 589832 | tf_op jit(solution)/shard_map/ppermute | solution.py:319
  30.9 2.2 %collective-permute-start.4 = (bf16[384,256]{1,0:T(8,128)(2,1)S(1)}, bf16[384,256]{1,0:T(8,128)(2,1)S(1)}, u32[]{:S(2)}, u32[]{:S(2)}) collective-permute-start(bf16[384,256]{1,0:T(8,128)(2,1)S(1)} %bitcast.12), channel_id=1, source_target_pairs={{0,192},{192,384},{384,576},{1,193},{193,385},{385,577},{2,194},{1... | collective-permute-start | bytes 589832 | tf_op jit(solution)/shard_map/ppermute | solution.py:320
  33.2 0.7 copy-done.5
  33.9 1.1 %select_rows.1 = (bf16[8,2,32,384]{3,2,1,0:T(8,128)(2,1)}, s32[2,128]{1,0:T(2,128)S(1)}, f32[2,128]{1,0:T(2,128)S(1)}) custom-call(bf16[128,384]{1,0:T(8,128)(2,1)S(1)} %copy-done.2, s32[2,128]{1,0:T(2,128)S(1)} %bitcast.17, f32[2,128]{1,0:T(2,128)S(1)} %bitcast.18), custom_call_target="tpu_custom_call" | custom-call | flops 2516582400 | bytes 1048576 | tf_op jit(solution)/shard_map/select_rows/pallas_call | solution.py:303
  35.0 7.0 %all-to-all-start.1 = ((bf16[8,2,32,384]{3,2,1,0:T(8,128)(2,1)}), bf16[8,2,32,384]{3,2,1,0:T(8,128)(2,1)S(1)}, u32[]{:S(2)}, u32[]{:S(2)}) async-start(bf16[8,2,32,384]{3,2,1,0:T(8,128)(2,1)} %get-tuple-element.36), calls=%async_computation.1 | async-start | bytes 786432 | tf_op jit(solution)/shard_map/all_to_all | solution.py:314
  42.0 1.9 %softmax_stats.1.mine = f32[32,128]{1,0:T(8,128)S(1)} custom-call(bf16[128,768]{1,0:T(8,128)(2,1)S(1)} %copy-done.1, bf16[128,768]{1,0:T(8,128)(2,1)S(1)} %collective-permute-done.qd_c, bf16[256,768]{1,0:T(8,128)(2,1)S(1)} %collective-permute-done.1.qd_y, bf16[64,256]{1,0:T(8,128)(2,1)S(1)} %collective-permute-done.2.kvx, ...), custom_call_target="tpu_custom_call" | custom-call | flops 10569646080 | bytes 1048576 | tf_op jit(solution)/shard_map/softmax_stats/pallas_call | solution.py:331
  43.9 4.5 %collective-permute-start.5 = (f32[32,128]{1,0:T(8,128)S(1)}, f32[32,128]{1,0:T(8,128)S(1)}, u32[]{:S(2)}, u32[]{:S(2)}) collective-permute-start(f32[32,128]{1,0:T(8,128)S(1)} %softmax_stats.1.mine), channel_id=1, source_target_pairs={{0,16},{16,0},{1,17},{17,1},{2,18},{18,2},{3,19},{19,3},{4,20},{20... | collective-permute-start | bytes 49160 | tf_op jit(solution)/shard_map/ppermute | solution.py:339
  48.4 0.8 collective-permute-done.5.arrived
  49.2 3.6 %collective-permute-start.6 = (f32[32,128]{1,0:T(8,128)S(1)}, f32[32,128]{1,0:T(8,128)S(1)}, u32[]{:S(2)}, u32[]{:S(2)}) collective-permute-start(f32[32,128]{1,0:T(8,128)S(1)} %merge_stats.1.stats), channel_id=1, source_target_pairs={{0,1},{1,0},{2,3},{3,2},{4,5},{5,4},{6,7},{7,6},{8,9},{9,8},{10,11... | collective-permute-start | bytes 49160 | tf_op jit(solution)/shard_map/ppermute | solution.py:341
  52.9 0.9 all-to-all-done.1.rows
  53.8 9.9 %collective-permute-start.10 = (bf16[8,32,384]{2,1,0:T(8,128)(2,1)S(1)}, bf16[8,32,384]{2,1,0:T(8,128)(2,1)S(1)}, u32[]{:S(2)}, u32[]{:S(2)}) collective-permute-start(bf16[8,32,384]{2,1,0:T(8,128)(2,1)S(1)} %dynamic-slice_bitcast_fusion), channel_id=1, source_target_pairs={{0,8},{8,0},{1,9},{9,1},{2,10},{10,2},{3,11},{11,3},{4,12},{12,4},... | collective-permute-start | bytes 589832 | tf_op jit(solution)/shard_map/ppermute | solution.py:316
  63.8 4.3 %score_grads.1 = (bf16[384,256]{1,0:T(8,128)(2,1)S(1)}, bf16[384,256]{1,0:T(8,128)(2,1)S(1)}, f32[384,256]{1,0:T(8,128)S(1)}, bf16[64,256]{1,0:T(8,128)(2,1)S(1)...) custom-call(bf16[128,768]{1,0:T(8,128)(2,1)S(1)} %copy-done.1, bf16[128,768]{1,0:T(8,128)(2,1)S(1)} %collective-permute-done.qd_c, ...), custom_call_target="tpu_custom_call" | custom-call | flops 1761607680 | bytes 1048576 | tf_op jit(solution)/shard_map/score_grads/pallas_call | solution.py:342
  68.1 1.3 %collective-permute-start.7 = (bf16[384,256]{1,0:T(8,128)(2,1)S(1)}, bf16[384,256]{1,0:T(8,128)(2,1)S(1)}, u32[]{:S(2)}, u32[]{:S(2)}) collective-permute-start(bf16[384,256]{1,0:T(8,128)(2,1)S(1)} %get-tuple-element.32), channel_id=1, source_target_pairs={{192,0},{384,192},{576,384},{193,1},{385,193},{577,385},{194,2},{3... | collective-permute-start | bytes 589832 | tf_op jit(solution)/shard_map/ppermute | solution.py:357
  69.4 1.3 %collective-permute-start.8 = (bf16[384,256]{1,0:T(8,128)(2,1)S(1)}, bf16[384,256]{1,0:T(8,128)(2,1)S(1)}, u32[]{:S(2)}, u32[]{:S(2)}) collective-permute-start(bf16[384,256]{1,0:T(8,128)(2,1)S(1)} %get-tuple-element.33), channel_id=1, source_target_pairs={{384,0},{576,192},{385,1},{577,193},{386,2},{578,194},{387,3},{579... | collective-permute-start | bytes 589832 | tf_op jit(solution)/shard_map/ppermute | solution.py:356
  70.7 1.9 %collective-permute-start.9 = (bf16[384,256]{1,0:T(8,128)(2,1)S(1)}, bf16[384,256]{1,0:T(8,128)(2,1)S(1)}, u32[]{:S(2)}, u32[]{:S(2)}) collective-permute-start(bf16[384,256]{1,0:T(8,128)(2,1)S(1)} %get-tuple-element.34), channel_id=1, source_target_pairs={{0,1},{1,0},{2,3},{3,2},{4,5},{5,4},{6,7},{7,6},{8,9},{9,8},{10,11... | collective-permute-start | bytes 589832 | tf_op jit(solution)/shard_map/ppermute | solution.py:359
  72.6 0.7 collective-permute-start.11
  73.3 1.1 %combine_grads.1 = (f32[1,32]{1,0:T(1,128)}, bf16[32,6144]{1,0:T(8,128)(2,1)}) custom-call(bf16[8,2,32,384]{3,2,1,0:T(8,128)(2,1)S(1)} %all-to-all-done.1.rows, bf16[8,32,384]{2,1,0:T(8,128)(2,1)S(1)} %collective-permute-done.10.rows_other, s32[2,128]{1,0:T(2,128)S(1)} %get-tuple-element.37.ids, f32[2,128]{1,0:T(2,128)S(1)} %get-tuple-element.38.gates, ...), custom_call_target="tpu_custom_call" | custom-call | bytes 1048576 | tf_op jit(solution)/shard_map/combine_grads/pallas_call | solution.py:361
  74.4 0.4 collective-permute-done.7.r1
  74.8 2.8 %collective-permute-done.8.r2 = bf16[384,256]{1,0:T(8,128)(2,1)S(1)} collective-permute-done((bf16[384,256]{1,0:T(8,128)(2,1)S(1)}, bf16[384,256]{1,0:T(8,128)(2,1)S(1)}, u32[]{:S(2)}, u32[]{:S(2)}) %collective-permute-start.8) | collective-permute-done | bytes 196640 | tf_op jit(solution)/shard_map/ppermute | solution.py:356
  77.6 0.8 plane_sum.1
  78.4 11.9 %all-to-all-start.2 = ((bf16[12,64,128]{2,1,0:T(8,128)(2,1)}), bf16[12,64,128]{2,1,0:T(8,128)(2,1)S(1)}, u32[]{:S(2)}, u32[]{:S(2)}) async-start(bf16[12,64,128]{2,1,0:T(8,128)(2,1)} %plane_sum.1), calls=%async_computation.2 | async-start | bytes 393216 | tf_op jit(solution)/shard_map/all_to_all | solution.py:381
  90.4 1.9 %collective-permute-start.12 = (bf16[384,128]{1,0:T(8,128)(2,1)S(1)}, bf16[384,128]{1,0:T(8,128)(2,1)S(1)}, u32[]{:S(2)}, u32[]{:S(2)}) collective-permute-start(bf16[384,128]{1,0:T(8,128)(2,1)S(1)} %get-tuple-element.46), channel_id=1, source_target_pairs={{0,16},{16,0},{1,17},{17,1},{2,18},{18,2},{3,19},{19,3},{4,20},{20... | collective-permute-start | bytes 294920 | tf_op jit(solution)/shard_map/ppermute | solution.py:377
  92.3 1.3 %collective-permute-done.12.arrived = bf16[384,128]{1,0:T(8,128)(2,1)S(1)} collective-permute-done((bf16[384,128]{1,0:T(8,128)(2,1)S(1)}, bf16[384,128]{1,0:T(8,128)(2,1)S(1)}, u32[]{:S(2)}, u32[]{:S(2)}) %collective-permute-start.12) | collective-permute-done | bytes 98336 | tf_op jit(solution)/shard_map/ppermute | solution.py:377
  93.6 5.9 %all-to-all-done.2.parts = bf16[12,64,128]{2,1,0:T(8,128)(2,1)S(1)} async-done(((bf16[12,64,128]{2,1,0:T(8,128)(2,1)}), bf16[12,64,128]{2,1,0:T(8,128)(2,1)S(1)}, u32[]{:S(2)}, u32[]{:S(2)}) %all-to-all-start.2) | async-done | bytes 196640 | tf_op jit(solution)/shard_map/all_to_all | solution.py:381
  99.5 0.8 final_sums.1
  (27 shorter events, 0.2 us)
Async XLA Ops:
  2.4 12.8 %copy-start.1 = (bf16[128,768]{1,0:T(8,128)(2,1)S(1)}, bf16[128,768]{1,0:T(8,128)(2,1)}, u32[]{:S(2)}) copy-start(bf16[128,768]{1,0:T(8,128)(2,1)} %get-tuple-element.28.qd) | copy-start | bytes 589828
  2.4 23.9 %all-to-all-start = ((bf16[6,64,256]{2,1,0:T(8,128)(2,1)}), bf16[6,64,256]{2,1,0:T(8,128)(2,1)S(1)}, u32[]{:S(2)}, u32[]{:S(2)}) async-start(bf16[6,64,256]{2,1,0:T(8,128)(2,1)} %get-tuple-element.30), calls=%async_computation | async-start | bytes 393216 | tf_op jit(solution)/shard_map/all_to_all | solution.py:299
  15.2 7.3 %copy-start.7 = (bf16[64,256]{1,0:T(8,128)(2,1)S(1)}, bf16[64,256]{1,0:T(8,128)(2,1)}, u32[]{:S(2)}) copy-start(bf16[64,256]{1,0:T(8,128)(2,1)} %get-tuple-element.29) | copy-start | bytes 98308
  15.2 18.0 %copy-start.2 = (bf16[128,384]{1,0:T(8,128)(2,1)S(1)}, bf16[128,384]{1,0:T(8,128)(2,1)}, u32[]{:S(2)}) copy-start(bf16[128,384]{1,0:T(8,128)(2,1)} %mine.1) | copy-start | bytes 294916
  15.2 4.4 %collective-permute-start = (bf16[128,768]{1,0:T(8,128)(2,1)S(1)}, bf16[128,768]{1,0:T(8,128)(2,1)S(1)}, u32[]{:S(2)}, u32[]{:S(2)}) collective-permute-start(bf16[128,768]{1,0:T(8,128)(2,1)S(1)} %copy-done.1), channel_id=1, source_target_pairs={{0,16},{16,0},{1,17},{17,1},{2,18},{18,2},{3,19},{19,3},{4,20},{20... | collective-permute-start | bytes 589832 | tf_op jit(solution)/shard_map/ppermute | solution.py:300
  19.6 13.6 %copy-start.6 = (f32[128,2]{0,1:T(2,128)S(1)}, f32[128,2]{0,1:T(2,128)}, u32[]{:S(2)}) copy-start(f32[128,2]{0,1:T(2,128)} %param.17) | copy-start | bytes 3076
  19.6 22.3 %collective-permute-start.1 = (bf16[256,768]{1,0:T(8,128)(2,1)S(1)}, bf16[256,768]{1,0:T(8,128)(2,1)S(1)}, u32[]{:S(2)}, u32[]{:S(2)}) collective-permute-start(bf16[256,768]{1,0:T(8,128)(2,1)S(1)} %pad_maximum_fusion), channel_id=1, source_target_pairs={{0,1},{1,0},{2,3},{3,2},{4,5},{5,4},{6,7},{7,6},{8,9},{9,8},{10,11... | collective-permute-start | bytes 1179656 | tf_op jit(solution)/shard_map/ppermute | solution.py:301
  22.5 19.4 %collective-permute-start.2 = (bf16[64,256]{1,0:T(8,128)(2,1)S(1)}, bf16[64,256]{1,0:T(8,128)(2,1)S(1)}, u32[]{:S(2)}, u32[]{:S(2)}) collective-permute-start(bf16[64,256]{1,0:T(8,128)(2,1)S(1)} %copy-done.7), channel_id=1, source_target_pairs={{176,592},{177,593},{178,594},{179,595},{180,596},{181,597},{182,5... | collective-permute-start | bytes 98312 | tf_op jit(solution)/shard_map/ppermute | solution.py:321
  26.3 15.7 %collective-permute-start.3 = (bf16[384,256]{1,0:T(8,128)(2,1)S(1)}, bf16[384,256]{1,0:T(8,128)(2,1)S(1)}, u32[]{:S(2)}, u32[]{:S(2)}) collective-permute-start(bf16[384,256]{1,0:T(8,128)(2,1)S(1)} %bitcast.11), channel_id=1, source_target_pairs={{0,384},{192,576},{1,385},{193,577},{2,386},{194,578},{3,387},{195... | collective-permute-start | bytes 589832 | tf_op jit(solution)/shard_map/ppermute | solution.py:319
  30.9 11.0 %collective-permute-start.4 = (bf16[384,256]{1,0:T(8,128)(2,1)S(1)}, bf16[384,256]{1,0:T(8,128)(2,1)S(1)}, u32[]{:S(2)}, u32[]{:S(2)}) collective-permute-start(bf16[384,256]{1,0:T(8,128)(2,1)S(1)} %bitcast.12), channel_id=1, source_target_pairs={{0,192},{192,384},{384,576},{1,193},{193,385},{385,577},{2,194},{1... | collective-permute-start | bytes 589832 | tf_op jit(solution)/shard_map/ppermute | solution.py:320
  33.2 0.7 copy-start.5
  35.0 7.0 %copy-start.3 = (bf16[128,384]{1,0:T(8,128)(2,1)S(1)}, bf16[128,384]{1,0:T(8,128)(2,1)}, u32[]{:S(2)}) copy-start(bf16[128,384]{1,0:T(8,128)(2,1)} %o_own.1) | copy-start | bytes 294916
  35.0 7.0 %copy-start.4 = (s32[6144]{0:T(1024)S(1)}, s32[6144]{0:T(1024)}, u32[]{:S(2)}) copy-start(s32[6144]{0:T(1024)} %param.15) | copy-start | bytes 73732
  35.0 18.8 %all-to-all-start.1 = ((bf16[8,2,32,384]{3,2,1,0:T(8,128)(2,1)}), bf16[8,2,32,384]{3,2,1,0:T(8,128)(2,1)S(1)}, u32[]{:S(2)}, u32[]{:S(2)}) async-start(bf16[8,2,32,384]{3,2,1,0:T(8,128)(2,1)} %get-tuple-element.36), calls=%async_computation.1 | async-start | bytes 786432 | tf_op jit(solution)/shard_map/all_to_all | solution.py:314
  43.9 5.3 %collective-permute-start.5 = (f32[32,128]{1,0:T(8,128)S(1)}, f32[32,128]{1,0:T(8,128)S(1)}, u32[]{:S(2)}, u32[]{:S(2)}) collective-permute-start(f32[32,128]{1,0:T(8,128)S(1)} %softmax_stats.1.mine), channel_id=1, source_target_pairs={{0,16},{16,0},{1,17},{17,1},{2,18},{18,2},{3,19},{19,3},{4,20},{20... | collective-permute-start | bytes 49160 | tf_op jit(solution)/shard_map/ppermute | solution.py:339
  49.2 14.6 %collective-permute-start.6 = (f32[32,128]{1,0:T(8,128)S(1)}, f32[32,128]{1,0:T(8,128)S(1)}, u32[]{:S(2)}, u32[]{:S(2)}) collective-permute-start(f32[32,128]{1,0:T(8,128)S(1)} %merge_stats.1.stats), channel_id=1, source_target_pairs={{0,1},{1,0},{2,3},{3,2},{4,5},{5,4},{6,7},{7,6},{8,9},{9,8},{10,11... | collective-permute-start | bytes 49160 | tf_op jit(solution)/shard_map/ppermute | solution.py:341
  53.8 19.5 %copy-start = (bf16[1,32,6144]{2,1,0:T(8,128)(2,1)S(1)}, bf16[1,32,6144]{2,1,0:T(8,128)(2,1)}, u32[]{:S(2)}) copy-start(bf16[1,32,6144]{2,1,0:T(8,128)(2,1)} %param.19) | copy-start | bytes 1179652
  53.8 19.5 %collective-permute-start.10 = (bf16[8,32,384]{2,1,0:T(8,128)(2,1)S(1)}, bf16[8,32,384]{2,1,0:T(8,128)(2,1)S(1)}, u32[]{:S(2)}, u32[]{:S(2)}) collective-permute-start(bf16[8,32,384]{2,1,0:T(8,128)(2,1)S(1)} %dynamic-slice_bitcast_fusion), channel_id=1, source_target_pairs={{0,8},{8,0},{1,9},{9,1},{2,10},{10,2},{3,11},{11,3},{4,12},{12,4},... | collective-permute-start | bytes 589832 | tf_op jit(solution)/shard_map/ppermute | solution.py:316
  68.1 6.7 %collective-permute-start.7 = (bf16[384,256]{1,0:T(8,128)(2,1)S(1)}, bf16[384,256]{1,0:T(8,128)(2,1)S(1)}, u32[]{:S(2)}, u32[]{:S(2)}) collective-permute-start(bf16[384,256]{1,0:T(8,128)(2,1)S(1)} %get-tuple-element.32), channel_id=1, source_target_pairs={{192,0},{384,192},{576,384},{193,1},{385,193},{577,385},{194,2},{3... | collective-permute-start | bytes 589832 | tf_op jit(solution)/shard_map/ppermute | solution.py:357
  69.4 8.2 %collective-permute-start.8 = (bf16[384,256]{1,0:T(8,128)(2,1)S(1)}, bf16[384,256]{1,0:T(8,128)(2,1)S(1)}, u32[]{:S(2)}, u32[]{:S(2)}) collective-permute-start(bf16[384,256]{1,0:T(8,128)(2,1)S(1)} %get-tuple-element.33), channel_id=1, source_target_pairs={{384,0},{576,192},{385,1},{577,193},{386,2},{578,194},{387,3},{579... | collective-permute-start | bytes 589832 | tf_op jit(solution)/shard_map/ppermute | solution.py:356
  70.7 6.9 %collective-permute-start.9 = (bf16[384,256]{1,0:T(8,128)(2,1)S(1)}, bf16[384,256]{1,0:T(8,128)(2,1)S(1)}, u32[]{:S(2)}, u32[]{:S(2)}) collective-permute-start(bf16[384,256]{1,0:T(8,128)(2,1)S(1)} %get-tuple-element.34), channel_id=1, source_target_pairs={{0,1},{1,0},{2,3},{3,2},{4,5},{5,4},{6,7},{7,6},{8,9},{9,8},{10,11... | collective-permute-start | bytes 589832 | tf_op jit(solution)/shard_map/ppermute | solution.py:359
  72.6 5.0 %collective-permute-start.11 = (bf16[64,256]{1,0:T(8,128)(2,1)S(1)}, bf16[64,256]{1,0:T(8,128)(2,1)S(1)}, u32[]{:S(2)}, u32[]{:S(2)}) collective-permute-start(bf16[64,256]{1,0:T(8,128)(2,1)S(1)} %get-tuple-element.42), channel_id=1, source_target_pairs={{592,176},{593,177},{594,178},{595,179},{596,180},{597,181},{598,1... | collective-permute-start | bytes 98312 | tf_op jit(solution)/shard_map/ppermute | solution.py:358
  78.4 21.1 %all-to-all-start.2 = ((bf16[12,64,128]{2,1,0:T(8,128)(2,1)}), bf16[12,64,128]{2,1,0:T(8,128)(2,1)S(1)}, u32[]{:S(2)}, u32[]{:S(2)}) async-start(bf16[12,64,128]{2,1,0:T(8,128)(2,1)} %plane_sum.1), calls=%async_computation.2 | async-start | bytes 393216 | tf_op jit(solution)/shard_map/all_to_all | solution.py:381
  90.4 3.2 %collective-permute-start.12 = (bf16[384,128]{1,0:T(8,128)(2,1)S(1)}, bf16[384,128]{1,0:T(8,128)(2,1)S(1)}, u32[]{:S(2)}, u32[]{:S(2)}) collective-permute-start(bf16[384,128]{1,0:T(8,128)(2,1)S(1)} %get-tuple-element.46), channel_id=1, source_target_pairs={{0,16},{16,0},{1,17},{17,1},{2,18},{18,2},{3,19},{19,3},{4,20},{20... | collective-permute-start | bytes 294920 | tf_op jit(solution)/shard_map/ppermute | solution.py:377

commit v10 on v9

--- a/solution.py
+++ b/solution.py
@@ -195,7 +195,7 @@
         ref[:, HD : 2 * HD] = jnp.where(low, pltpu.roll(dk, HD // 2, 1), dv).astype(ref.dtype)
 
 
-def plane_kernel(d0, r1, r2, rx, out):
+def plane_kernel(d0, r2, r1, rx, out):
     for block in range(Z):
         rows = slice(block * KB, (block + 1) * KB)
         total = d0[rows, :] + r1[rows, :].astype(F32) + r2[rows, :].astype(F32)
@@ -353,11 +353,11 @@
         flops=10 * HD * pairs,
         name="score_grads",
     )(*shared, doc, stats, stats_y)
+    back1 = lax.ppermute(d1, "x", [(i + 1, i) for i in range(X - 1)])
     back2 = lax.ppermute(d2, "x", [(i + 2, i) for i in range(X - 2)])
-    back1 = lax.ppermute(d1, "x", [(i + 1, i) for i in range(X - 1)])
     backx = lax.ppermute(dx, ("x", "z", "c"), [(b, a) for a, b in lone])
     dq_arrived = lax.ppermute(dq_send, "yl", [(0, 1), (1, 0)])
-    back1, back2, dq_arrived = lax.optimization_barrier((back1, back2, dq_arrived))
+    back2, back1, dq_arrived = lax.optimization_barrier((back2, back1, dq_arrived))
     gate_grad, expert_grad = call(
         combine_kernel,
         (
@@ -367,7 +367,7 @@
         [],
         name="combine_grads",
     )(rows, rows_other, ids, gates, expert_out[0])
-    back1, _ = lax.optimization_barrier((back1, expert_grad))
+    back2, _ = lax.optimization_barrier((back2, expert_grad))
     dq_mine, dq_other = call(
         pool_kernel,
         (jax.ShapeDtypeStruct((OWN * HD, ROWS), F32), jax.ShapeDtypeStruct((OWN * HD, ROWS), BF16)),
@@ -376,7 +376,7 @@
     )(dq_keep, dq_arrived)
     dq_other = lax.ppermute(dq_other, "c", [(0, 1), (1, 0)])
     plane_sums = call(plane_kernel, jax.ShapeDtypeStruct((2 * Z, KB, HD), BF16), [], name="plane_sum")(
-        d0, back1, back2, backx
+        d0, back2, back1, backx
     )
     parts = lax.all_to_all(plane_sums, ("z", "yl"), split_axis=0, concat_axis=0, tiled=True)
 

time: 101 us -> 101 us (level)
    ppermute x1, waiting for transfers between devices: 0.01 us -> 1.09 us  [local(): dq_arrived = lax.ppermute(dq_send, 'yl', [(0, 1), (1, 0)])]
where the time goes in v10:
time: 101 us; the launch traced here: 100 us
  starting transfers between devices  70.8 us (70%)
  waiting for transfers between devices  16.1 us (16%)
  Pallas kernels  11.7 us (12%)
    all_to_all x1, starting transfers between devices, local(): lax.all_to_all(spread, 'z', split_axis=0, concat_axis=0, tiled=True)  12.8 us
    all_to_all x1, starting transfers between devices, local(): lax.all_to_all(plane_sums, ('z', 'yl'), split_axis=0, concat_axis=0, tile...  12.1 us
    ppermute x1, starting transfers between devices, local(): rows_other = lax.ppermute(away, 'zh', [(0, 1), (1, 0)])  9.95 us
    all_to_all x1, starting transfers between devices, local(): lax.all_to_all(chosen_rows, ('yh', 'yl'), split_axis=0, concat_axis=0, ti...  6.95 us
    all_to_all x1, waiting for transfers between devices, local(): lax.all_to_all(plane_sums, ('z', 'yl'), split_axis=0, concat_axis=0, tile...  5.91 us
    ppermute x1, starting transfers between devices, local(): ahead2 = lax.ppermute(plane, 'x', [(i, i + 2) for i in range(X - 2)])  4.66 us
    ppermute x1, starting transfers between devices, local(): lax.ppermute(stats, 'c', [(0, 1), (1, 0)])  4.48 us
    pallas_call x1, Pallas kernels, local(): call(grads_kernel, (jax.ShapeDtypeStruct((PLANE, 2 * HD), BF16), jax.Shap...  4.28 us
  transfers between devices with their start and end apart: 16, of which 8 were waited for; matrix products, arithmetic and copies ran while one was open for 0% of the time, Pallas kernels for 8%

profile of v10, /device:TPU:1, one launch (start us, length us, event | category | flops | bytes accessed | tf_op | source)
XLA Modules:
  0.0 100.2 jit_solution(856196857537371187)
XLA Ops:
  0.6 1.8 %prep.1 = (bf16[128,768]{1,0:T(8,128)(2,1)}, bf16[6,64,256]{2,1,0:T(8,128)(2,1)}, bf16[64,256]{1,0:T(8,128)(2,1)}) custom-call(bf16[128,384]{1,0:T(8,128)(2,1)} %queries.1, bf16[128,384]{1,0:T(8,128)(2,1)} %out_grad.1, bf16[128,1024]{1,0:T(8,128)(2,1)} %key_rows.1, bf16[128,1024]{1,0:T(8,128)(2,1)} %value_rows.1), custom_call_target="tpu_custom_call" | custom-call | bytes 1048576 | tf_op jit(solution)/shard_map/prep/pallas_call | solution.py:287
  2.4 12.8 %all-to-all-start = ((bf16[6,64,256]{2,1,0:T(8,128)(2,1)}), bf16[6,64,256]{2,1,0:T(8,128)(2,1)S(1)}, u32[]{:S(2)}, u32[]{:S(2)}) async-start(bf16[6,64,256]{2,1,0:T(8,128)(2,1)} %get-tuple-element.30), calls=%async_computation | async-start | bytes 393216 | tf_op jit(solution)/shard_map/all_to_all | solution.py:299
  15.2 3.3 %collective-permute-start = (bf16[128,768]{1,0:T(8,128)(2,1)S(1)}, bf16[128,768]{1,0:T(8,128)(2,1)S(1)}, u32[]{:S(2)}, u32[]{:S(2)}) collective-permute-start(bf16[128,768]{1,0:T(8,128)(2,1)S(1)} %copy-done.1), channel_id=1, source_target_pairs={{0,16},{16,0},{1,17},{17,1},{2,18},{18,2},{3,19},{19,3},{4,20},{20... | collective-permute-start | bytes 589832 | tf_op jit(solution)/shard_map/ppermute | solution.py:300
  18.6 1.0 %collective-permute-done.qd_c = bf16[128,768]{1,0:T(8,128)(2,1)S(1)} collective-permute-done((bf16[128,768]{1,0:T(8,128)(2,1)S(1)}, bf16[128,768]{1,0:T(8,128)(2,1)S(1)}, u32[]{:S(2)}, u32[]{:S(2)}) %collective-permute-start) | collective-permute-done | bytes 196640 | tf_op jit(solution)/shard_map/ppermute | solution.py:300
  19.6 2.9 %collective-permute-start.1 = (bf16[256,768]{1,0:T(8,128)(2,1)S(1)}, bf16[256,768]{1,0:T(8,128)(2,1)S(1)}, u32[]{:S(2)}, u32[]{:S(2)}) collective-permute-start(bf16[256,768]{1,0:T(8,128)(2,1)S(1)} %pad_maximum_fusion), channel_id=1, source_target_pairs={{0,1},{1,0},{2,3},{3,2},{4,5},{5,4},{6,7},{7,6},{8,9},{9,8},{10,11... | collective-permute-start | bytes 1179656 | tf_op jit(solution)/shard_map/ppermute | solution.py:301
  22.5 0.7 collective-permute-start.2
  23.2 3.1 %all-to-all-done = bf16[6,64,256]{2,1,0:T(8,128)(2,1)S(1)} async-done(((bf16[6,64,256]{2,1,0:T(8,128)(2,1)}), bf16[6,64,256]{2,1,0:T(8,128)(2,1)S(1)}, u32[]{:S(2)}, u32[]{:S(2)}) %all-to-all-start) | async-done | bytes 196640 | tf_op jit(solution)/shard_map/all_to_all | solution.py:299
  26.3 4.7 %collective-permute-start.3 = (bf16[384,256]{1,0:T(8,128)(2,1)S(1)}, bf16[384,256]{1,0:T(8,128)(2,1)S(1)}, u32[]{:S(2)}, u32[]{:S(2)}) collective-permute-start(bf16[384,256]{1,0:T(8,128)(2,1)S(1)} %bitcast.11), channel_id=1, source_target_pairs={{0,384},{192,576},{1,385},{193,577},{2,386},{194,578},{3,387},{195... | collective-permute-start | bytes 589832 | tf_op jit(solution)/shard_map/ppermute | solution.py:319
  30.9 2.2 %collective-permute-start.4 = (bf16[384,256]{1,0:T(8,128)(2,1)S(1)}, bf16[384,256]{1,0:T(8,128)(2,1)S(1)}, u32[]{:S(2)}, u32[]{:S(2)}) collective-permute-start(bf16[384,256]{1,0:T(8,128)(2,1)S(1)} %bitcast.12), channel_id=1, source_target_pairs={{0,192},{192,384},{384,576},{1,193},{193,385},{385,577},{2,194},{1... | collective-permute-start | bytes 589832 | tf_op jit(solution)/shard_map/ppermute | solution.py:320
  33.2 0.7 copy-done.5
  33.9 1.1 %select_rows.1 = (bf16[8,2,32,384]{3,2,1,0:T(8,128)(2,1)}, s32[2,128]{1,0:T(2,128)S(1)}, f32[2,128]{1,0:T(2,128)S(1)}) custom-call(bf16[128,384]{1,0:T(8,128)(2,1)S(1)} %copy-done.2, s32[2,128]{1,0:T(2,128)S(1)} %bitcast.17, f32[2,128]{1,0:T(2,128)S(1)} %bitcast.18), custom_call_target="tpu_custom_call" | custom-call | flops 2516582400 | bytes 1048576 | tf_op jit(solution)/shard_map/select_rows/pallas_call | solution.py:303
  35.0 7.0 %all-to-all-start.1 = ((bf16[8,2,32,384]{3,2,1,0:T(8,128)(2,1)}), bf16[8,2,32,384]{3,2,1,0:T(8,128)(2,1)S(1)}, u32[]{:S(2)}, u32[]{:S(2)}) async-start(bf16[8,2,32,384]{3,2,1,0:T(8,128)(2,1)} %get-tuple-element.36), calls=%async_computation.1 | async-start | bytes 786432 | tf_op jit(solution)/shard_map/all_to_all | solution.py:314
  42.0 1.9 %softmax_stats.1.mine = f32[32,128]{1,0:T(8,128)S(1)} custom-call(bf16[128,768]{1,0:T(8,128)(2,1)S(1)} %copy-done.1, bf16[128,768]{1,0:T(8,128)(2,1)S(1)} %collective-permute-done.qd_c, bf16[256,768]{1,0:T(8,128)(2,1)S(1)} %collective-permute-done.1.qd_y, bf16[64,256]{1,0:T(8,128)(2,1)S(1)} %collective-permute-done.2.kvx, ...), custom_call_target="tpu_custom_call" | custom-call | flops 10569646080 | bytes 1048576 | tf_op jit(solution)/shard_map/softmax_stats/pallas_call | solution.py:331
  43.9 4.5 %collective-permute-start.5 = (f32[32,128]{1,0:T(8,128)S(1)}, f32[32,128]{1,0:T(8,128)S(1)}, u32[]{:S(2)}, u32[]{:S(2)}) collective-permute-start(f32[32,128]{1,0:T(8,128)S(1)} %softmax_stats.1.mine), channel_id=1, source_target_pairs={{0,16},{16,0},{1,17},{17,1},{2,18},{18,2},{3,19},{19,3},{4,20},{20... | collective-permute-start | bytes 49160 | tf_op jit(solution)/shard_map/ppermute | solution.py:339
  48.4 0.8 collective-permute-done.5.arrived
  49.2 3.6 %collective-permute-start.6 = (f32[32,128]{1,0:T(8,128)S(1)}, f32[32,128]{1,0:T(8,128)S(1)}, u32[]{:S(2)}, u32[]{:S(2)}) collective-permute-start(f32[32,128]{1,0:T(8,128)S(1)} %merge_stats.1.stats), channel_id=1, source_target_pairs={{0,1},{1,0},{2,3},{3,2},{4,5},{5,4},{6,7},{7,6},{8,9},{9,8},{10,11... | collective-permute-start | bytes 49160 | tf_op jit(solution)/shard_map/ppermute | solution.py:341
  52.9 0.9 all-to-all-done.1.rows
  53.8 9.9 %collective-permute-start.10 = (bf16[8,32,384]{2,1,0:T(8,128)(2,1)S(1)}, bf16[8,32,384]{2,1,0:T(8,128)(2,1)S(1)}, u32[]{:S(2)}, u32[]{:S(2)}) collective-permute-start(bf16[8,32,384]{2,1,0:T(8,128)(2,1)S(1)} %dynamic-slice_bitcast_fusion), channel_id=1, source_target_pairs={{0,8},{8,0},{1,9},{9,1},{2,10},{10,2},{3,11},{11,3},{4,12},{12,4},... | collective-permute-start | bytes 589832 | tf_op jit(solution)/shard_map/ppermute | solution.py:316
  63.8 4.3 %score_grads.1 = (bf16[384,256]{1,0:T(8,128)(2,1)S(1)}, bf16[384,256]{1,0:T(8,128)(2,1)S(1)}, f32[384,256]{1,0:T(8,128)S(1)}, bf16[64,256]{1,0:T(8,128)(2,1)S(1)...) custom-call(bf16[128,768]{1,0:T(8,128)(2,1)S(1)} %copy-done.1, bf16[128,768]{1,0:T(8,128)(2,1)S(1)} %collective-permute-done.qd_c, ...), custom_call_target="tpu_custom_call" | custom-call | flops 1761607680 | bytes 1048576 | tf_op jit(solution)/shard_map/score_grads/pallas_call | solution.py:342
  68.1 1.3 %collective-permute-start.7 = (bf16[384,256]{1,0:T(8,128)(2,1)S(1)}, bf16[384,256]{1,0:T(8,128)(2,1)S(1)}, u32[]{:S(2)}, u32[]{:S(2)}) collective-permute-start(bf16[384,256]{1,0:T(8,128)(2,1)S(1)} %get-tuple-element.32), channel_id=1, source_target_pairs={{384,0},{576,192},{385,1},{577,193},{386,2},{578,194},{387,3},{579... | collective-permute-start | bytes 589832 | tf_op jit(solution)/shard_map/ppermute | solution.py:357
  69.4 1.3 %collective-permute-start.8 = (bf16[384,256]{1,0:T(8,128)(2,1)S(1)}, bf16[384,256]{1,0:T(8,128)(2,1)S(1)}, u32[]{:S(2)}, u32[]{:S(2)}) collective-permute-start(bf16[384,256]{1,0:T(8,128)(2,1)S(1)} %get-tuple-element.33), channel_id=1, source_target_pairs={{192,0},{384,192},{576,384},{193,1},{385,193},{577,385},{194,2},{3... | collective-permute-start | bytes 589832 | tf_op jit(solution)/shard_map/ppermute | solution.py:356
  70.7 1.9 %collective-permute-start.9 = (bf16[384,256]{1,0:T(8,128)(2,1)S(1)}, bf16[384,256]{1,0:T(8,128)(2,1)S(1)}, u32[]{:S(2)}, u32[]{:S(2)}) collective-permute-start(bf16[384,256]{1,0:T(8,128)(2,1)S(1)} %get-tuple-element.34), channel_id=1, source_target_pairs={{0,1},{1,0},{2,3},{3,2},{4,5},{5,4},{6,7},{7,6},{8,9},{9,8},{10,11... | collective-permute-start | bytes 589832 | tf_op jit(solution)/shard_map/ppermute | solution.py:359
  72.6 0.7 collective-permute-start.11
  73.3 1.1 %combine_grads.1 = (f32[1,32]{1,0:T(1,128)}, bf16[32,6144]{1,0:T(8,128)(2,1)}) custom-call(bf16[8,2,32,384]{3,2,1,0:T(8,128)(2,1)S(1)} %all-to-all-done.1.rows, bf16[8,32,384]{2,1,0:T(8,128)(2,1)S(1)} %collective-permute-done.10.rows_other, s32[2,128]{1,0:T(2,128)S(1)} %get-tuple-element.37.ids, f32[2,128]{1,0:T(2,128)S(1)} %get-tuple-element.38.gates, ...), custom_call_target="tpu_custom_call" | custom-call | bytes 1048576 | tf_op jit(solution)/shard_map/combine_grads/pallas_call | solution.py:361
  74.4 1.9 %collective-permute-done.7.r2 = bf16[384,256]{1,0:T(8,128)(2,1)S(1)} collective-permute-done((bf16[384,256]{1,0:T(8,128)(2,1)S(1)}, bf16[384,256]{1,0:T(8,128)(2,1)S(1)}, u32[]{:S(2)}, u32[]{:S(2)}) %collective-permute-start.7) | collective-permute-done | bytes 196640 | tf_op jit(solution)/shard_map/ppermute | solution.py:357
  76.3 1.1 %collective-permute-done.9.arrived = bf16[384,256]{1,0:T(8,128)(2,1)S(1)} collective-permute-done((bf16[384,256]{1,0:T(8,128)(2,1)S(1)}, bf16[384,256]{1,0:T(8,128)(2,1)S(1)}, u32[]{:S(2)}, u32[]{:S(2)}) %collective-permute-start.9) | collective-permute-done | bytes 196640 | tf_op jit(solution)/shard_map/ppermute | solution.py:359
  77.4 0.8 plane_sum.1
  78.2 12.1 %all-to-all-start.2 = ((bf16[12,64,128]{2,1,0:T(8,128)(2,1)}), bf16[12,64,128]{2,1,0:T(8,128)(2,1)S(1)}, u32[]{:S(2)}, u32[]{:S(2)}) async-start(bf16[12,64,128]{2,1,0:T(8,128)(2,1)} %plane_sum.1), calls=%async_computation.2 | async-start | bytes 393216 | tf_op jit(solution)/shard_map/all_to_all | solution.py:381
  90.4 1.9 %collective-permute-start.12 = (bf16[384,128]{1,0:T(8,128)(2,1)S(1)}, bf16[384,128]{1,0:T(8,128)(2,1)S(1)}, u32[]{:S(2)}, u32[]{:S(2)}) collective-permute-start(bf16[384,128]{1,0:T(8,128)(2,1)S(1)} %get-tuple-element.46), channel_id=1, source_target_pairs={{0,16},{16,0},{1,17},{17,1},{2,18},{18,2},{3,19},{19,3},{4,20},{20... | collective-permute-start | bytes 294920 | tf_op jit(solution)/shard_map/ppermute | solution.py:377
  92.3 1.3 %collective-permute-done.12.arrived = bf16[384,128]{1,0:T(8,128)(2,1)S(1)} collective-permute-done((bf16[384,128]{1,0:T(8,128)(2,1)S(1)}, bf16[384,128]{1,0:T(8,128)(2,1)S(1)}, u32[]{:S(2)}, u32[]{:S(2)}) %collective-permute-start.12) | collective-permute-done | bytes 98336 | tf_op jit(solution)/shard_map/ppermute | solution.py:377
  93.6 5.9 %all-to-all-done.2.parts = bf16[12,64,128]{2,1,0:T(8,128)(2,1)S(1)} async-done(((bf16[12,64,128]{2,1,0:T(8,128)(2,1)}), bf16[12,64,128]{2,1,0:T(8,128)(2,1)S(1)}, u32[]{:S(2)}, u32[]{:S(2)}) %all-to-all-start.2) | async-done | bytes 196640 | tf_op jit(solution)/shard_map/all_to_all | solution.py:381
  99.5 0.8 final_sums.1
  (27 shorter events, 0.2 us)
Async XLA Ops:
  2.4 12.8 %copy-start.1 = (bf16[128,768]{1,0:T(8,128)(2,1)S(1)}, bf16[128,768]{1,0:T(8,128)(2,1)}, u32[]{:S(2)}) copy-start(bf16[128,768]{1,0:T(8,128)(2,1)} %get-tuple-element.28.qd) | copy-start | bytes 589828
  2.4 23.9 %all-to-all-start = ((bf16[6,64,256]{2,1,0:T(8,128)(2,1)}), bf16[6,64,256]{2,1,0:T(8,128)(2,1)S(1)}, u32[]{:S(2)}, u32[]{:S(2)}) async-start(bf16[6,64,256]{2,1,0:T(8,128)(2,1)} %get-tuple-element.30), calls=%async_computation | async-start | bytes 393216 | tf_op jit(solution)/shard_map/all_to_all | solution.py:299
  15.2 7.3 %copy-start.7 = (bf16[64,256]{1,0:T(8,128)(2,1)S(1)}, bf16[64,256]{1,0:T(8,128)(2,1)}, u32[]{:S(2)}) copy-start(bf16[64,256]{1,0:T(8,128)(2,1)} %get-tuple-element.29) | copy-start | bytes 98308
  15.2 18.0 %copy-start.2 = (bf16[128,384]{1,0:T(8,128)(2,1)S(1)}, bf16[128,384]{1,0:T(8,128)(2,1)}, u32[]{:S(2)}) copy-start(bf16[128,384]{1,0:T(8,128)(2,1)} %mine.1) | copy-start | bytes 294916
  15.2 4.4 %collective-permute-start = (bf16[128,768]{1,0:T(8,128)(2,1)S(1)}, bf16[128,768]{1,0:T(8,128)(2,1)S(1)}, u32[]{:S(2)}, u32[]{:S(2)}) collective-permute-start(bf16[128,768]{1,0:T(8,128)(2,1)S(1)} %copy-done.1), channel_id=1, source_target_pairs={{0,16},{16,0},{1,17},{17,1},{2,18},{18,2},{3,19},{19,3},{4,20},{20... | collective-permute-start | bytes 589832 | tf_op jit(solution)/shard_map/ppermute | solution.py:300
  19.6 13.6 %copy-start.6 = (f32[128,2]{0,1:T(2,128)S(1)}, f32[128,2]{0,1:T(2,128)}, u32[]{:S(2)}) copy-start(f32[128,2]{0,1:T(2,128)} %param.17) | copy-start | bytes 3076
  19.6 22.3 %collective-permute-start.1 = (bf16[256,768]{1,0:T(8,128)(2,1)S(1)}, bf16[256,768]{1,0:T(8,128)(2,1)S(1)}, u32[]{:S(2)}, u32[]{:S(2)}) collective-permute-start(bf16[256,768]{1,0:T(8,128)(2,1)S(1)} %pad_maximum_fusion), channel_id=1, source_target_pairs={{0,1},{1,0},{2,3},{3,2},{4,5},{5,4},{6,7},{7,6},{8,9},{9,8},{10,11... | collective-permute-start | bytes 1179656 | tf_op jit(solution)/shard_map/ppermute | solution.py:301
  22.5 19.4 %collective-permute-start.2 = (bf16[64,256]{1,0:T(8,128)(2,1)S(1)}, bf16[64,256]{1,0:T(8,128)(2,1)S(1)}, u32[]{:S(2)}, u32[]{:S(2)}) collective-permute-start(bf16[64,256]{1,0:T(8,128)(2,1)S(1)} %copy-done.7), channel_id=1, source_target_pairs={{176,592},{177,593},{178,594},{179,595},{180,596},{181,597},{182,5... | collective-permute-start | bytes 98312 | tf_op jit(solution)/shard_map/ppermute | solution.py:321
  26.3 15.7 %collective-permute-start.3 = (bf16[384,256]{1,0:T(8,128)(2,1)S(1)}, bf16[384,256]{1,0:T(8,128)(2,1)S(1)}, u32[]{:S(2)}, u32[]{:S(2)}) collective-permute-start(bf16[384,256]{1,0:T(8,128)(2,1)S(1)} %bitcast.11), channel_id=1, source_target_pairs={{0,384},{192,576},{1,385},{193,577},{2,386},{194,578},{3,387},{195... | collective-permute-start | bytes 589832 | tf_op jit(solution)/shard_map/ppermute | solution.py:319
  30.9 11.0 %collective-permute-start.4 = (bf16[384,256]{1,0:T(8,128)(2,1)S(1)}, bf16[384,256]{1,0:T(8,128)(2,1)S(1)}, u32[]{:S(2)}, u32[]{:S(2)}) collective-permute-start(bf16[384,256]{1,0:T(8,128)(2,1)S(1)} %bitcast.12), channel_id=1, source_target_pairs={{0,192},{192,384},{384,576},{1,193},{193,385},{385,577},{2,194},{1... | collective-permute-start | bytes 589832 | tf_op jit(solution)/shard_map/ppermute | solution.py:320
  33.2 0.7 copy-start.5
  35.0 7.0 %copy-start.3 = (bf16[128,384]{1,0:T(8,128)(2,1)S(1)}, bf16[128,384]{1,0:T(8,128)(2,1)}, u32[]{:S(2)}) copy-start(bf16[128,384]{1,0:T(8,128)(2,1)} %o_own.1) | copy-start | bytes 294916
  35.0 7.0 %copy-start.4 = (s32[6144]{0:T(1024)S(1)}, s32[6144]{0:T(1024)}, u32[]{:S(2)}) copy-start(s32[6144]{0:T(1024)} %param.15) | copy-start | bytes 73732
  35.0 18.8 %all-to-all-start.1 = ((bf16[8,2,32,384]{3,2,1,0:T(8,128)(2,1)}), bf16[8,2,32,384]{3,2,1,0:T(8,128)(2,1)S(1)}, u32[]{:S(2)}, u32[]{:S(2)}) async-start(bf16[8,2,32,384]{3,2,1,0:T(8,128)(2,1)} %get-tuple-element.36), calls=%async_computation.1 | async-start | bytes 786432 | tf_op jit(solution)/shard_map/all_to_all | solution.py:314
  43.9 5.3 %collective-permute-start.5 = (f32[32,128]{1,0:T(8,128)S(1)}, f32[32,128]{1,0:T(8,128)S(1)}, u32[]{:S(2)}, u32[]{:S(2)}) collective-permute-start(f32[32,128]{1,0:T(8,128)S(1)} %softmax_stats.1.mine), channel_id=1, source_target_pairs={{0,16},{16,0},{1,17},{17,1},{2,18},{18,2},{3,19},{19,3},{4,20},{20... | collective-permute-start | bytes 49160 | tf_op jit(solution)/shard_map/ppermute | solution.py:339
  49.2 14.6 %collective-permute-start.6 = (f32[32,128]{1,0:T(8,128)S(1)}, f32[32,128]{1,0:T(8,128)S(1)}, u32[]{:S(2)}, u32[]{:S(2)}) collective-permute-start(f32[32,128]{1,0:T(8,128)S(1)} %merge_stats.1.stats), channel_id=1, source_target_pairs={{0,1},{1,0},{2,3},{3,2},{4,5},{5,4},{6,7},{7,6},{8,9},{9,8},{10,11... | collective-permute-start | bytes 49160 | tf_op jit(solution)/shard_map/ppermute | solution.py:341
  53.8 19.5 %copy-start = (bf16[1,32,6144]{2,1,0:T(8,128)(2,1)S(1)}, bf16[1,32,6144]{2,1,0:T(8,128)(2,1)}, u32[]{:S(2)}) copy-start(bf16[1,32,6144]{2,1,0:T(8,128)(2,1)} %param.19) | copy-start | bytes 1179652
  53.8 19.5 %collective-permute-start.10 = (bf16[8,32,384]{2,1,0:T(8,128)(2,1)S(1)}, bf16[8,32,384]{2,1,0:T(8,128)(2,1)S(1)}, u32[]{:S(2)}, u32[]{:S(2)}) collective-permute-start(bf16[8,32,384]{2,1,0:T(8,128)(2,1)S(1)} %dynamic-slice_bitcast_fusion), channel_id=1, source_target_pairs={{0,8},{8,0},{1,9},{9,1},{2,10},{10,2},{3,11},{11,3},{4,12},{12,4},... | collective-permute-start | bytes 589832 | tf_op jit(solution)/shard_map/ppermute | solution.py:316
  68.1 8.2 %collective-permute-start.7 = (bf16[384,256]{1,0:T(8,128)(2,1)S(1)}, bf16[384,256]{1,0:T(8,128)(2,1)S(1)}, u32[]{:S(2)}, u32[]{:S(2)}) collective-permute-start(bf16[384,256]{1,0:T(8,128)(2,1)S(1)} %get-tuple-element.32), channel_id=1, source_target_pairs={{384,0},{576,192},{385,1},{577,193},{386,2},{578,194},{387,3},{579... | collective-permute-start | bytes 589832 | tf_op jit(solution)/shard_map/ppermute | solution.py:357
  69.4 6.9 %collective-permute-start.8 = (bf16[384,256]{1,0:T(8,128)(2,1)S(1)}, bf16[384,256]{1,0:T(8,128)(2,1)S(1)}, u32[]{:S(2)}, u32[]{:S(2)}) collective-permute-start(bf16[384,256]{1,0:T(8,128)(2,1)S(1)} %get-tuple-element.33), channel_id=1, source_target_pairs={{192,0},{384,192},{576,384},{193,1},{385,193},{577,385},{194,2},{3... | collective-permute-start | bytes 589832 | tf_op jit(solution)/shard_map/ppermute | solution.py:356
  70.7 6.7 %collective-permute-start.9 = (bf16[384,256]{1,0:T(8,128)(2,1)S(1)}, bf16[384,256]{1,0:T(8,128)(2,1)S(1)}, u32[]{:S(2)}, u32[]{:S(2)}) collective-permute-start(bf16[384,256]{1,0:T(8,128)(2,1)S(1)} %get-tuple-element.34), channel_id=1, source_target_pairs={{0,1},{1,0},{2,3},{3,2},{4,5},{5,4},{6,7},{7,6},{8,9},{9,8},{10,11... | collective-permute-start | bytes 589832 | tf_op jit(solution)/shard_map/ppermute | solution.py:359
  72.6 4.8 %collective-permute-start.11 = (bf16[64,256]{1,0:T(8,128)(2,1)S(1)}, bf16[64,256]{1,0:T(8,128)(2,1)S(1)}, u32[]{:S(2)}, u32[]{:S(2)}) collective-permute-start(bf16[64,256]{1,0:T(8,128)(2,1)S(1)} %get-tuple-element.42), channel_id=1, source_target_pairs={{592,176},{593,177},{594,178},{595,179},{596,180},{597,181},{598,1... | collective-permute-start | bytes 98312 | tf_op jit(solution)/shard_map/ppermute | solution.py:358
  78.2 21.3 %all-to-all-start.2 = ((bf16[12,64,128]{2,1,0:T(8,128)(2,1)}), bf16[12,64,128]{2,1,0:T(8,128)(2,1)S(1)}, u32[]{:S(2)}, u32[]{:S(2)}) async-start(bf16[12,64,128]{2,1,0:T(8,128)(2,1)} %plane_sum.1), calls=%async_computation.2 | async-start | bytes 393216 | tf_op jit(solution)/shard_map/all_to_all | solution.py:381
  90.4 3.2 %collective-permute-start.12 = (bf16[384,128]{1,0:T(8,128)(2,1)S(1)}, bf16[384,128]{1,0:T(8,128)(2,1)S(1)}, u32[]{:S(2)}, u32[]{:S(2)}) collective-permute-start(bf16[384,128]{1,0:T(8,128)(2,1)S(1)} %get-tuple-element.46), channel_id=1, source_target_pairs={{0,16},{16,0},{1,17},{17,1},{2,18},{18,2},{3,19},{19,3},{4,20},{20... | collective-permute-start | bytes 294920 | tf_op jit(solution)/shard_map/ppermute | solution.py:377
